TPU v7x, 32 devices: a whole 2x2x4 slice. The times are simulated.
32 devices in a mesh: dp: 8 (over y, x, core), fsdp: 4 (over z).
Axes of the slice: x: 2, y: 2, z: 4, core: 2. Of those that a mesh axis runs over, the one named last changes fastest.
Arguments:
- tokens: bfloat16 [32, 512, 1024], P(('dp', 'fsdp')), may hold values from -6 to 6
- crop_ids: int32 [32, 512], P(('dp', 'fsdp')), may hold values from 0 to 2, never falling along the last dimension, each value on 1 to 384 neighbouring positions
- kv_mask: int32 [32, 512], P(('dp', 'fsdp')), may hold values 0 or 1
- norm1_gain: bfloat16 [1024], P(('dp', 'fsdp')), may hold values from 0.099609375 to 1.8984375
- norm1_bias: bfloat16 [1024], P(('dp', 'fsdp')), may hold values from -4 to 4
- w_query: bfloat16 [1024, 1024], P(('dp', 'fsdp')), may hold values from -0.1875 to 0.1875
- w_key: bfloat16 [1024, 1024], P(('dp', 'fsdp')), may hold values from -0.1875 to 0.1875
- w_value: bfloat16 [1024, 1024], P(('dp', 'fsdp')), may hold values from -0.1875 to 0.1875
- w_out: bfloat16 [1024, 1024], P(('dp', 'fsdp')), may hold values from -2 to 2
- norm2_gain: bfloat16 [1024], P(('dp', 'fsdp')), may hold values from 0.099609375 to 1.8984375
- norm2_bias: bfloat16 [1024], P(('dp', 'fsdp')), may hold values from -4 to 4
- w_up: bfloat16 [1024, 4096], P(('dp', 'fsdp')), may hold values from -0.1875 to 0.1875
- up_bias: bfloat16 [4096], P(('dp', 'fsdp')), may hold values from -6 to 6
- w_down: bfloat16 [4096, 1024], P(('dp', 'fsdp')), may hold values from -0.09375 to 0.09375
- down_bias: bfloat16 [1024], P(('dp', 'fsdp')), may hold values from -4 to 4
- cotangent: bfloat16 [32, 512, 1024], P(('dp', 'fsdp')), may hold values from -6 to 6
Outputs:
- output: bfloat16 [32, 512, 1024], P(('dp', 'fsdp'))
- input_grad: bfloat16 [32, 512, 1024], P(('dp', 'fsdp'))
- grad_norm1_gain: float32 [1024], P(('dp', 'fsdp'))
- grad_norm1_bias: float32 [1024], P(('dp', 'fsdp'))
- grad_w_query: float32 [1024, 1024], P(('dp', 'fsdp'))
- grad_w_key: float32 [1024, 1024], P(('dp', 'fsdp'))
- grad_w_value: float32 [1024, 1024], P(('dp', 'fsdp'))
- grad_w_out: float32 [1024, 1024], P(('dp', 'fsdp'))
- grad_norm2_gain: float32 [1024], P(('dp', 'fsdp'))
- grad_norm2_bias: float32 [1024], P(('dp', 'fsdp'))
- grad_w_up: float32 [1024, 4096], P(('dp', 'fsdp'))
- grad_up_bias: float32 [4096], P(('dp', 'fsdp'))
- grad_w_down: float32 [4096, 1024], P(('dp', 'fsdp'))
- grad_down_bias: float32 [1024], P(('dp', 'fsdp'))
Inputs may be any that keep to these rules, and one draw needn't show every extreme that they name: `crop_ids`: in every slot the crop ids never fall, each of the 3 crops has 1 to 384 pixels, and one crop has exactly 384.
All inputs are finite; a program needn't handle non-finite values. No bound on the sum of `kv_mask` on one device may be relied on, other than what follows from the above.
Results may differ from a plain program's by a relative error of at most 0.0093.
Values may be sent and summed in bfloat16 or wider, within the bound.
A program may use at most 192 MiB of HBM per device.

v0:
```python
import jax
import jax.numpy as jnp
from jax import lax
from jax.sharding import PartitionSpec as P

HEADS = 16
BLOCK = 512


HIGH = lax.Precision.HIGHEST
norm_eps = 1e-05


def norm_affine(values, gain, shift):
    mean = jnp.mean(values, axis=-1, keepdims=True)
    centred = values - mean
    spread = jnp.mean(centred * centred, axis=-1, keepdims=True)
    return centred * lax.rsqrt(spread + norm_eps) * gain + shift


def feature(values):
    return jax.nn.elu(values) + 1.0


def gelu_exact(values):
    return jax.nn.gelu(values, approximate=False)


def allowed_weight(crop, keymask):
    places = jnp.arange(crop.shape[0])
    earlier = places[None, :] <= places[:, None]
    same = crop[:, None] == crop[None, :]
    visible = (keymask[None, :] > 0) | (places[None, :] == places[:, None])
    return (earlier & same & visible).astype(jnp.float32)


def attend_forward(carry, pieces):
    state, norm_state, prev_crop = carry
    query_feat, key_feat, values, crop, keymask = pieces
    weight = allowed_weight(crop, keymask)
    scores = (
        jnp.einsum("ihe,jhe->hij", query_feat, key_feat, preferred_element_type=jnp.float32)
        * weight[None]
    )
    value_wide = values.astype(jnp.float32)
    query_wide = query_feat.astype(jnp.float32)
    key_wide = key_feat.astype(jnp.float32)
    numer = jnp.einsum("hij,jhe->ihe", scores, value_wide, precision=HIGH)
    denom = jnp.sum(scores, axis=2).T
    follows = (crop == prev_crop).astype(jnp.float32)
    numer = numer + follows[:, None, None] * jnp.einsum(
        "ihe,hef->ihf", query_wide, state, precision=HIGH
    )
    denom = denom + follows[:, None] * jnp.einsum(
        "ihe,he->ih", query_wide, norm_state, precision=HIGH
    )
    last_crop = crop[crop.shape[0] - 1]
    carried = (prev_crop == last_crop).astype(jnp.float32)
    select = ((crop == last_crop) & (keymask > 0)).astype(jnp.float32)
    chosen = key_wide * select[:, None, None]
    new_state = carried * state + jnp.einsum("jhe,jhf->hef", chosen, value_wide, precision=HIGH)
    new_norm = carried * norm_state + jnp.sum(chosen, axis=0)
    return ((new_state, new_norm, last_crop), (numer / denom[:, :, None], denom, state, norm_state))


def attend_backward(carry, pieces):
    grad_state, grad_norm = carry
    (
        query_feat,
        key_feat,
        values,
        crop,
        keymask,
        prev_crop,
        state,
        norm_state,
        grad_numer,
        grad_denom,
    ) = pieces
    weight = allowed_weight(crop, keymask)
    scores = (
        jnp.einsum("ihe,jhe->hij", query_feat, key_feat, preferred_element_type=jnp.float32)
        * weight[None]
    )
    value_wide = values.astype(jnp.float32)
    query_wide = query_feat.astype(jnp.float32)
    key_wide = key_feat.astype(jnp.float32)
    grad_scores = (
        jnp.einsum("ihe,jhe->hij", grad_numer, value_wide, precision=HIGH)
        + grad_denom.T[:, :, None]
    ) * weight[None]
    follows = (crop == prev_crop).astype(jnp.float32)
    last_crop = crop[crop.shape[0] - 1]
    carried = (prev_crop == last_crop).astype(jnp.float32)
    select = ((crop == last_crop) & (keymask > 0)).astype(jnp.float32)
    grad_query = jnp.einsum("hij,jhe->ihe", grad_scores, key_wide, precision=HIGH)
    grad_query = grad_query + follows[:, None, None] * (
        jnp.einsum("ihf,hef->ihe", grad_numer, state, precision=HIGH)
        + grad_denom[:, :, None] * norm_state[None]
    )
    grad_key = jnp.einsum("hij,ihe->jhe", grad_scores, query_wide, precision=HIGH)
    grad_key = grad_key + select[:, None, None] * (
        jnp.einsum("jhf,hef->jhe", value_wide, grad_state, precision=HIGH) + grad_norm[None]
    )
    grad_value = jnp.einsum("hij,ihe->jhe", scores, grad_numer, precision=HIGH)
    grad_value = grad_value + select[:, None, None] * jnp.einsum(
        "jhe,hef->jhf", key_wide, grad_state, precision=HIGH
    )
    query_kept = query_wide * follows[:, None, None]
    earlier_state = carried * grad_state + jnp.einsum(
        "ihe,ihf->hef", query_kept, grad_numer, precision=HIGH
    )
    earlier_norm = carried * grad_norm + jnp.einsum(
        "ihe,ih->he", query_kept, grad_denom, precision=HIGH
    )
    return ((earlier_state, earlier_norm), (grad_query, grad_key, grad_value))


def split_blocks(array):
    blocks = array.shape[0] // BLOCK
    return array.reshape((blocks, BLOCK) + array.shape[1:])


def attend_slot(pieces):
    query_feat, key_feat, values, crop, keymask = pieces
    length, heads, head_width = query_feat.shape
    start = (
        jnp.zeros((heads, head_width, head_width), jnp.float32),
        jnp.zeros((heads, head_width), jnp.float32),
        jnp.int32(-1),
    )
    finish, (mixed, denom, states, norms) = lax.scan(
        attend_forward,
        start,
        (
            split_blocks(query_feat),
            split_blocks(key_feat),
            split_blocks(values),
            split_blocks(crop),
            split_blocks(keymask),
        ),
    )
    return (mixed.reshape(length, heads, head_width), denom.reshape(length, heads), states, norms)


def attend_slot_back(pieces):
    query_feat, key_feat, values, crop, keymask, states, norms, grad_numer, grad_denom = pieces
    length, heads, head_width = query_feat.shape
    crop_blocks = split_blocks(crop)
    prev_crops = jnp.concatenate([jnp.full((1,), -1, jnp.int32), crop_blocks[:-1, -1]])
    start = (
        jnp.zeros((heads, head_width, head_width), jnp.float32),
        jnp.zeros((heads, head_width), jnp.float32),
    )
    finish, (grad_query, grad_key, grad_value) = lax.scan(
        attend_backward,
        start,
        (
            split_blocks(query_feat),
            split_blocks(key_feat),
            split_blocks(values),
            crop_blocks,
            split_blocks(keymask),
            prev_crops,
            states,
            norms,
            split_blocks(grad_numer),
            split_blocks(grad_denom),
        ),
        reverse=True,
    )
    shape = (length, heads, head_width)
    return (grad_query.reshape(shape), grad_key.reshape(shape), grad_value.reshape(shape))


def body(
    tokens,
    crop_ids,
    kv_mask,
    norm1_gain,
    norm1_bias,
    w_query,
    w_key,
    w_value,
    w_out,
    norm2_gain,
    norm2_bias,
    w_up,
    up_bias,
    w_down,
    down_bias,
    cotangent,
):
    slots, length, width = tokens.shape
    heads = HEADS
    head_width = width // heads
    count = slots * length
    attention_set = (
        lax.all_gather(norm1_gain, ("dp", "fsdp"), axis=0, tiled=True),
        lax.all_gather(norm1_bias, ("dp", "fsdp"), axis=0, tiled=True),
        lax.all_gather(w_query, ("dp", "fsdp"), axis=0, tiled=True),
        lax.all_gather(w_key, ("dp", "fsdp"), axis=0, tiled=True),
        lax.all_gather(w_value, ("dp", "fsdp"), axis=0, tiled=True),
        lax.all_gather(w_out, ("dp", "fsdp"), axis=0, tiled=True),
    )
    gain_one, bias_one, full_query, full_key, full_value, full_out = attention_set
    inputs = tokens.reshape(count, width).astype(jnp.float32)
    normed_wide, pull_one = jax.vjp(
        norm_affine, inputs, gain_one.astype(jnp.float32), bias_one.astype(jnp.float32)
    )
    normed = normed_wide.astype(jnp.bfloat16)
    query = jnp.dot(normed, full_query, preferred_element_type=jnp.float32)
    keys = jnp.dot(normed, full_key, preferred_element_type=jnp.float32)
    values = jnp.dot(normed, full_value, preferred_element_type=jnp.float32).astype(jnp.bfloat16)
    query_wide, pull_query = jax.vjp(feature, query)
    key_wide, pull_key = jax.vjp(feature, keys)
    query_feat = query_wide.astype(jnp.bfloat16).reshape(slots, length, heads, head_width)
    key_feat = key_wide.astype(jnp.bfloat16).reshape(slots, length, heads, head_width)
    value_heads = values.reshape(slots, length, heads, head_width)
    mixed_wide, denom, states, norms = lax.map(
        attend_slot, (query_feat, key_feat, value_heads, crop_ids, kv_mask)
    )
    mixed = mixed_wide.reshape(count, width).astype(jnp.bfloat16)
    feedforward_set = (
        lax.all_gather(norm2_gain, ("dp", "fsdp"), axis=0, tiled=True),
        lax.all_gather(norm2_bias, ("dp", "fsdp"), axis=0, tiled=True),
        lax.all_gather(w_up, ("dp", "fsdp"), axis=0, tiled=True),
        lax.all_gather(up_bias, ("dp", "fsdp"), axis=0, tiled=True),
        lax.all_gather(w_down, ("dp", "fsdp"), axis=0, tiled=True),
        lax.all_gather(down_bias, ("dp", "fsdp"), axis=0, tiled=True),
    )
    gain_two, bias_two, full_up, full_up_bias, full_down, full_down_bias = feedforward_set
    middle = inputs + jnp.dot(mixed, full_out, preferred_element_type=jnp.float32)
    normed_two_wide, pull_two = jax.vjp(
        norm_affine, middle, gain_two.astype(jnp.float32), bias_two.astype(jnp.float32)
    )
    normed_two = normed_two_wide.astype(jnp.bfloat16)
    upper = jnp.dot(normed_two, full_up, preferred_element_type=jnp.float32) + full_up_bias.astype(
        jnp.float32
    )
    hidden_wide, pull_gelu = jax.vjp(gelu_exact, upper)
    hidden = hidden_wide.astype(jnp.bfloat16)
    result = (
        middle
        + jnp.dot(hidden, full_down, preferred_element_type=jnp.float32)
        + full_down_bias.astype(jnp.float32)
    )
    output = result.astype(jnp.bfloat16).reshape(slots, length, width)
    feedforward_set = (
        lax.all_gather(norm2_gain, ("dp", "fsdp"), axis=0, tiled=True),
        lax.all_gather(norm2_bias, ("dp", "fsdp"), axis=0, tiled=True),
        lax.all_gather(w_up, ("dp", "fsdp"), axis=0, tiled=True),
        lax.all_gather(up_bias, ("dp", "fsdp"), axis=0, tiled=True),
        lax.all_gather(w_down, ("dp", "fsdp"), axis=0, tiled=True),
        lax.all_gather(down_bias, ("dp", "fsdp"), axis=0, tiled=True),
    )
    attention_set = (
        lax.all_gather(norm1_gain, ("dp", "fsdp"), axis=0, tiled=True),
        lax.all_gather(norm1_bias, ("dp", "fsdp"), axis=0, tiled=True),
        lax.all_gather(w_query, ("dp", "fsdp"), axis=0, tiled=True),
        lax.all_gather(w_key, ("dp", "fsdp"), axis=0, tiled=True),
        lax.all_gather(w_value, ("dp", "fsdp"), axis=0, tiled=True),
        lax.all_gather(w_out, ("dp", "fsdp"), axis=0, tiled=True),
    )
    back_up = feedforward_set[2]
    back_down = feedforward_set[4]
    back_query = attention_set[2]
    back_key = attention_set[3]
    back_value = attention_set[4]
    back_out = attention_set[5]
    grad_out = cotangent.reshape(count, width)
    grad_down_bias = jnp.sum(grad_out.astype(jnp.float32), axis=0)
    grad_w_down = jnp.dot(hidden.T, grad_out, preferred_element_type=jnp.float32)
    grad_hidden = jnp.dot(grad_out, back_down.T, preferred_element_type=jnp.float32)
    grad_upper = pull_gelu(grad_hidden)[0].astype(jnp.bfloat16)
    grad_up_bias = jnp.sum(grad_upper.astype(jnp.float32), axis=0)
    grad_w_up = jnp.dot(normed_two.T, grad_upper, preferred_element_type=jnp.float32)
    grad_normed_two = jnp.dot(grad_upper, back_up.T, preferred_element_type=jnp.float32)
    grad_middle_part, grad_gain_two, grad_bias_two = pull_two(grad_normed_two)
    feedforward_owned = (
        lax.psum_scatter(grad_gain_two, ("dp", "fsdp"), scatter_dimension=0, tiled=True),
        lax.psum_scatter(grad_bias_two, ("dp", "fsdp"), scatter_dimension=0, tiled=True),
        lax.psum_scatter(grad_w_up, ("dp", "fsdp"), scatter_dimension=0, tiled=True),
        lax.psum_scatter(grad_up_bias, ("dp", "fsdp"), scatter_dimension=0, tiled=True),
        lax.psum_scatter(grad_w_down, ("dp", "fsdp"), scatter_dimension=0, tiled=True),
        lax.psum_scatter(grad_down_bias, ("dp", "fsdp"), scatter_dimension=0, tiled=True),
    )
    grad_middle = grad_out.astype(jnp.float32) + grad_middle_part
    grad_attended = grad_middle.astype(jnp.bfloat16)
    grad_w_out = jnp.dot(mixed.T, grad_attended, preferred_element_type=jnp.float32)
    grad_mixed = jnp.dot(grad_attended, back_out.T, preferred_element_type=jnp.float32).reshape(
        slots, length, heads, head_width
    )
    grad_numer = grad_mixed / denom[..., None]
    grad_denom = -jnp.sum(grad_mixed * mixed_wide, axis=-1) / denom
    grad_query_feat, grad_key_feat, grad_values = lax.map(
        attend_slot_back,
        (
            query_feat,
            key_feat,
            value_heads,
            crop_ids,
            kv_mask,
            states,
            norms,
            grad_numer,
            grad_denom,
        ),
    )
    grad_query = pull_query(grad_query_feat.reshape(count, width))[0].astype(jnp.bfloat16)
    grad_keys = pull_key(grad_key_feat.reshape(count, width))[0].astype(jnp.bfloat16)
    grad_values = grad_values.reshape(count, width).astype(jnp.bfloat16)
    grad_w_query = jnp.dot(normed.T, grad_query, preferred_element_type=jnp.float32)
    grad_w_key = jnp.dot(normed.T, grad_keys, preferred_element_type=jnp.float32)
    grad_w_value = jnp.dot(normed.T, grad_values, preferred_element_type=jnp.float32)
    grad_normed = jnp.dot(grad_query, back_query.T, preferred_element_type=jnp.float32)
    grad_normed = grad_normed + jnp.dot(grad_keys, back_key.T, preferred_element_type=jnp.float32)
    grad_normed = grad_normed + jnp.dot(
        grad_values, back_value.T, preferred_element_type=jnp.float32
    )
    grad_input_part, grad_gain_one, grad_bias_one = pull_one(grad_normed)
    attention_owned = (
        lax.psum_scatter(grad_gain_one, ("dp", "fsdp"), scatter_dimension=0, tiled=True),
        lax.psum_scatter(grad_bias_one, ("dp", "fsdp"), scatter_dimension=0, tiled=True),
        lax.psum_scatter(grad_w_query, ("dp", "fsdp"), scatter_dimension=0, tiled=True),
        lax.psum_scatter(grad_w_key, ("dp", "fsdp"), scatter_dimension=0, tiled=True),
        lax.psum_scatter(grad_w_value, ("dp", "fsdp"), scatter_dimension=0, tiled=True),
        lax.psum_scatter(grad_w_out, ("dp", "fsdp"), scatter_dimension=0, tiled=True),
    )
    input_grad = (grad_middle + grad_input_part).astype(jnp.bfloat16).reshape(slots, length, width)
    return (
        output,
        input_grad,
        attention_owned[0],
        attention_owned[1],
        attention_owned[2],
        attention_owned[3],
        attention_owned[4],
        attention_owned[5],
        feedforward_owned[0],
        feedforward_owned[1],
        feedforward_owned[2],
        feedforward_owned[3],
        feedforward_owned[4],
        feedforward_owned[5],
    )


def solution(mesh):
    return jax.shard_map(
        body,
        mesh=mesh,
        in_specs=(
            P(("dp", "fsdp"), None, None),
            P(("dp", "fsdp"), None),
            P(("dp", "fsdp"), None),
            P(("dp", "fsdp")),
            P(("dp", "fsdp")),
            P(("dp", "fsdp"), None),
            P(("dp", "fsdp"), None),
            P(("dp", "fsdp"), None),
            P(("dp", "fsdp"), None),
            P(("dp", "fsdp")),
            P(("dp", "fsdp")),
            P(("dp", "fsdp"), None),
            P(("dp", "fsdp")),
            P(("dp", "fsdp"), None),
            P(("dp", "fsdp")),
            P(("dp", "fsdp"), None, None),
        ),
        out_specs=(
            P(("dp", "fsdp"), None, None),
            P(("dp", "fsdp"), None, None),
            P(("dp", "fsdp")),
            P(("dp", "fsdp")),
            P(("dp", "fsdp"), None),
            P(("dp", "fsdp"), None),
            P(("dp", "fsdp"), None),
            P(("dp", "fsdp"), None),
            P(("dp", "fsdp")),
            P(("dp", "fsdp")),
            P(("dp", "fsdp"), None),
            P(("dp", "fsdp")),
            P(("dp", "fsdp"), None),
            P(("dp", "fsdp")),
        ),
        check_vma=False,
    )
```

profile of v0, /device:TPU:0, one launch (start us, length us, event | category | flops | bytes accessed | tf_op | source)
XLA Modules:
  0.0 1764.9 jit_solution(4994519197335623371)
XLA Ops:
  16.6 42.2 %all-reduce.12 = (bf16[1024]{0:T(1024)(128)(2,1)S(1)}, bf16[1024]{0:T(1024)(128)(2,1)S(1)}, bf16[1024]{0:T(1024)(128)(2,1)S(1)}, bf16[1024]{0:T(1024)(128)(2,1)S(1)}, bf16[1024]{0:T(1024)(128)(2,1)}) all-reduce(bf16[1024]{0:T(1024)(128)(2,1)S(1)} %dynamic-update-slice.1, ...), channel_id=1, replica_groups=mesh['dp'=8,'fsdp'=4] {'dp','fsdp'}, use_global_device_ids=true, to_apply=%add.1 | all-reduce | flops 5120 | bytes 20480
  58.8 66.1 %all-gather = bf16[32,1,128]{2,1,0:T(2,128)(2,1)S(1)} all-gather(bf16[1,1,128]{2,1,0:T(2,128)(2,1)} %bitcast.163), channel_id=1, replica_groups=mesh['dp'=8,'fsdp'=4] {'dp','fsdp'}, dimensions={0}, use_global_device_ids=true | all-gather | bytes 8448 | tf_op jit(solution)/shard_map/all_gather | solution.py:228
  128.5 3.9 convolution_convert_fusion
  134.2 5.1 fusion.42
  141.6 45.4 %all-gather.12.cloned.1.call-done = bf16[1024,1024]{1,0:T(8,128)(2,1)} async-done(((bf16[32,1024]{1,0:T(8,128)(2,1)}), bf16[1024,1024]{1,0:T(8,128)(2,1)}) %all-gather.12.cloned.1.call-update) | async-done | bytes 2097168 | tf_op jit(solution)/shard_map/all_gather | solution.py:202
  186.9 5.1 fusion.39
  196.0 9.7 multiply_reduce_fusion
  205.7 11.2 fusion.4
  219.8 25.3 %all-gather.14.cloned.1.call-done = bf16[1024,1024]{1,0:T(8,128)(2,1)} async-done(((bf16[32,1024]{1,0:T(8,128)(2,1)}), bf16[1024,1024]{1,0:T(8,128)(2,1)}) %all-gather.14.cloned.1.call-update) | async-done | bytes 2097168 | tf_op jit(solution)/shard_map/all_gather | solution.py:204
  250.1 74.1 %all-gather.16.cloned.1.call-done = bf16[1024,4096]{1,0:T(8,128)(2,1)} async-done(((bf16[32,4096]{1,0:T(8,128)(2,1)}), bf16[1024,4096]{1,0:T(8,128)(2,1)}) %all-gather.16.cloned.1.call-update) | async-done | bytes 8388624 | tf_op jit(solution)/shard_map/all_gather | solution.py:227
  324.1 28.0 %multiply_convert_fusion = (bf16[512,4096]{1,0:T(8,128)(2,1)}, f32[512,4096]{1,0:T(8,128)}, f32[512,4096]{1,0:T(8,128)}) fusion(f32[4096]{0:T(1024)S(1)} %bitcast.161, bf16[1024,4096]{1,0:T(8,128)(2,1)} %all-gather.16.cloned.1.call-done, f32[512,1024]{1,0:T(8,128)} %copy-done.1, f32[1024]{0:T(1024)S(1)} %convert_element_type.169, ...), kind=kOutput, calls=%fused_computation.14 | convolution fusion | flops 4436000768 | bytes 31485952 | tf_op jit(solution)/shard_map/dot_general | solution.py:238
  352.2 50.8 %all-gather.18.cloned.1.call-done = bf16[4096,1024]{1,0:T(8,128)(2,1)} async-done(((bf16[128,1024]{1,0:T(8,128)(2,1)}), bf16[4096,1024]{1,0:T(8,128)(2,1)}) %all-gather.18.cloned.1.call-update) | async-done | bytes 8388624 | tf_op jit(solution)/shard_map/all_gather | solution.py:229
  403.0 13.6 convert_reduce_fusion
  416.6 8.9 multiply_reduce_fusion.1
  431.9 3.8 multiply_reduce_fusion.2
  435.8 19.9 %fusion.2 = f32[16,64,512]{2,1,0:T(8,128)S(1)} fusion(f32[16,512,512]{1,2,0:T(8,128)} %get-tuple-element.226, f32[512,512]{0,1:T(8,128)S(1)} %fusion.61, f32[512,16,64]{0,2,1:T(8,128)S(1)} %bitcast.139, f32[512,16]{0,1:T(8,128)S(1)} %fusion.69), kind=kOutput, calls=%fused_computation.3 | convolution fusion | flops 3225944064 | bytes 22052864 | tf_op jit(solution)/shard_map/while/body/eval_jaxpr/while/body/eval_jaxpr/hij,ihe->jhe/dot_general | solution.py:105
  457.8 3.5 fusion.47
  461.4 3.6 fusion.65
  465.0 10.4 fusion.76
  475.4 14.4 fusion.36
  497.1 3.4 fusion.82
  500.6 14.1 fusion
  522.1 3.4 fusion.80
  527.1 10.7 fusion.78
  537.9 12.8 fusion.49
  562.5 40.5 %all-reduce.11 = (f32[1024]{0:T(1024)S(1)}, f32[1024]{0:T(1024)S(1)}, f32[1024]{0:T(1024)S(1)}, f32[1024]{0:T(1024)S(1)}, f32[4096]{0:T(1024)S(1)}, /*index=5*/f32[1024]{0:T(1024)S(1)}) all-reduce(f32[1024]{0:T(1024)S(1)} %get-tuple-element.184, ...), channel_id=2, replica_groups=mesh['dp'=8,'fsdp'=4] {'dp','fsdp'}, use_global_device_ids=true, to_apply=%region_11.12.clone | all-reduce | flops 9216 | bytes 73728
  606.5 10.1 fusion.43
  616.6 111.7 %reduce-scatter.11.cloned.1.call-done = f32[32,1024]{1,0:T(8,128)} async-done(((f32[1024,1024]{1,0:T(8,128)}), f32[32,1024]{1,0:T(8,128)}) %reduce-scatter.11.cloned.1.call-update) | async-done | bytes 131088 | tf_op jit(solution)/shard_map/reduce_scatter | solution.py:327
  728.3 149.5 %reduce-scatter.7.cloned.1.call-done = f32[32,1024]{1,0:T(8,128)} async-done(((f32[1024,1024]{1,0:T(8,128)}), f32[32,1024]{1,0:T(8,128)}) %reduce-scatter.7.cloned.1.call-update) | async-done | bytes 131088 | tf_op jit(solution)/shard_map/reduce_scatter | solution.py:325
  877.8 149.3 %reduce-scatter.9.cloned.1.call-done = f32[32,1024]{1,0:T(8,128)} async-done(((f32[1024,1024]{1,0:T(8,128)}), f32[32,1024]{1,0:T(8,128)}) %reduce-scatter.9.cloned.1.call-update) | async-done | bytes 131088 | tf_op jit(solution)/shard_map/reduce_scatter | solution.py:326
  1027.1 365.8 %reduce-scatter.15.cloned.1.call-done = f32[32,4096]{1,0:T(8,128)} async-done(((f32[1024,4096]{1,0:T(8,128)}), f32[32,4096]{1,0:T(8,128)}) %reduce-scatter.15.cloned.1.call-update) | async-done | bytes 524304 | tf_op jit(solution)/shard_map/reduce_scatter | solution.py:283
  1392.9 364.9 %reduce-scatter.17.cloned.1.call-done = f32[128,1024]{1,0:T(8,128)} async-done(((f32[4096,1024]{1,0:T(8,128)}), f32[128,1024]{1,0:T(8,128)}) %reduce-scatter.17.cloned.1.call-update) | async-done | bytes 524304 | tf_op jit(solution)/shard_map/reduce_scatter | solution.py:285
  (142 shorter events, 68.7 us)
Async XLA Ops:
  7.2 120.4 %copy-start.21 = (s32[1,512]{1,0:T(1,128)S(1)}, s32[1,512]{1,0:T(1,128)}, u32[]{:S(2)}) copy-start(s32[1,512]{1,0:T(1,128)} %param.17) | copy-start | bytes 6148
  7.2 120.0 %copy-start = (bf16[1,512,1024]{2,1,0:T(8,128)(2,1)S(1)}, bf16[1,512,1024]{2,1,0:T(8,128)(2,1)}, u32[]{:S(2)}) copy-start(bf16[1,512,1024]{2,1,0:T(8,128)(2,1)} %param.16) | copy-start | bytes 3145732
  7.2 121.3 %all-gather.8.cloned.1.call-start = ((), (), s32[]{:S(2)}) async-start(), calls=%async_computation.6 | async-start | bytes 2162688 | tf_op jit(solution)/shard_map/all_gather | solution.py:203
  7.9 126.3 %all-gather.10.cloned.1.call-start = ((), (), s32[]{:S(2)}) async-start(), calls=%async_computation.7 | async-start | bytes 2162688 | tf_op jit(solution)/shard_map/all_gather | solution.py:201
  8.7 178.3 %all-gather.12.cloned.1.call-start = ((), (), s32[]{:S(2)}) async-start(), calls=%async_computation.8 | async-start | bytes 2162688 | tf_op jit(solution)/shard_map/all_gather | solution.py:202
  9.4 235.7 %all-gather.14.cloned.1.call-start = ((), (), s32[]{:S(2)}) async-start(), calls=%async_computation.9 | async-start | bytes 2162688 | tf_op jit(solution)/shard_map/all_gather | solution.py:204
  10.0 314.2 %all-gather.16.cloned.1.call-start = ((), (), s32[]{:S(2)}) async-start(), calls=%async_computation.10 | async-start | bytes 8650752 | tf_op jit(solution)/shard_map/all_gather | solution.py:227
  10.6 392.4 %all-gather.18.cloned.1.call-start = ((), (), s32[]{:S(2)}) async-start(), calls=%async_computation.11 | async-start | bytes 8650752 | tf_op jit(solution)/shard_map/all_gather | solution.py:229
  11.2 605.5 %reduce-scatter.13.cloned.1.call-start = ((), (), s32[]{:S(2)}) async-start(), calls=%async_computation.15 | async-start | bytes 4325376 | tf_op jit(solution)/shard_map/reduce_scatter | solution.py:328
  205.7 11.2 copy-start.8
  248.4 1.3 copy-start.1
  403.0 13.7 copy-start.2
  416.6 9.0 copy-start.26
  426.3 1.4 copy-start.4
  426.8 1.8 copy-start.20
  431.9 296.4 %reduce-scatter.11.cloned.1.call-start = ((), (), s32[]{:S(2)}) async-start(), calls=%async_computation.14 | async-start | bytes 4325376 | tf_op jit(solution)/shard_map/reduce_scatter | solution.py:327
  435.8 19.9 %copy-start.6 = (f32[512,1024]{0,1:T(8,128)}, f32[512,1024]{0,1:T(8,128)S(1)}, u32[]{:S(2)}) copy-start(f32[512,1024]{0,1:T(8,128)S(1)} %get-tuple-element.234) | copy-start | bytes 6291460
  435.8 19.9 %copy-start.9 = (bf16[512,1024]{0,1:T(8,128)(2,1)S(1)}, bf16[512,1024]{0,1:T(8,128)(2,1)}, u32[]{:S(2)}) copy-start(bf16[512,1024]{0,1:T(8,128)(2,1)} %copy.66) | copy-start | bytes 3145732
  461.3 416.5 %reduce-scatter.7.cloned.1.call-start = ((), (), s32[]{:S(2)}) async-start(), calls=%async_computation.12 | async-start | bytes 4325376 | tf_op jit(solution)/shard_map/reduce_scatter | solution.py:325
  461.4 3.6 copy-start.7
  465.0 10.5 copy-start.10
  500.5 526.6 %reduce-scatter.9.cloned.1.call-start = ((), (), s32[]{:S(2)}) async-start(), calls=%async_computation.13 | async-start | bytes 4325376 | tf_op jit(solution)/shard_map/reduce_scatter | solution.py:326
  525.5 1.6 copy-start.3
  525.6 867.4 %reduce-scatter.15.cloned.1.call-start = ((), (), s32[]{:S(2)}) async-start(), calls=%async_computation.16 | async-start | bytes 17301504 | tf_op jit(solution)/shard_map/reduce_scatter | solution.py:283
  537.8 1220.0 %reduce-scatter.17.cloned.1.call-start = ((), (), s32[]{:S(2)}) async-start(), calls=%async_computation.17 | async-start | bytes 17301504 | tf_op jit(solution)/shard_map/reduce_scatter | solution.py:285
  551.3 3.4 copy-start.18
  551.3 3.4 copy-start.25
  554.7 1.3 copy-start.15
  554.7 1.9 copy-start.16
  556.7 1.8 copy-start.23
  558.4 1.6 copy-start.5
  558.4 1.9 copy-start.13
  (7 other events, 6.8 us)
Sparse Core Ops, SparseCore 0:
  11.0 59.2 all-gather.7
  73.1 55.4 all-gather.9
  131.6 55.3 all-gather.11
  189.7 55.3 all-gather.13
  247.9 76.2 all-gather.15
  326.9 75.9 all-gather.17
  432.0 146.7 reduce-scatter.12
  581.6 146.6 reduce-scatter.10
  731.2 146.5 reduce-scatter.6
  880.5 146.5 reduce-scatter.8
  1030.0 362.8 reduce-scatter.14
  1395.6 362.1 reduce-scatter.16
where the time goes:
time: 1770 us; the launch traced here: 1760 us
  waiting for transfers between devices  1340 us (76%)
  matrix products  216 us (12%)
  blocking collectives  149 us (8%)
  local copies, waits for them, and re-layouts  30.4 us (2%)
    reduce_scatter x1, waiting for transfers between devices, body(): lax.psum_scatter(grad_w_up, ('dp', 'fsdp'), scatter_dimension=0, tiled=True)  366 us
    reduce_scatter x1, waiting for transfers between devices, body(): lax.psum_scatter(grad_w_down, ('dp', 'fsdp'), scatter_dimension=0, tiled=...  365 us
    reduce_scatter x1, waiting for transfers between devices, body(): lax.psum_scatter(grad_w_query, ('dp', 'fsdp'), scatter_dimension=0, tiled...  149 us
    reduce_scatter x1, waiting for transfers between devices, body(): lax.psum_scatter(grad_w_key, ('dp', 'fsdp'), scatter_dimension=0, tiled=T...  149 us
    reduce_scatter x1, waiting for transfers between devices, body(): lax.psum_scatter(grad_w_value, ('dp', 'fsdp'), scatter_dimension=0, tiled...  112 us
    unnamed x2, blocking collectives  82.7 us
    all_gather x1, waiting for transfers between devices, body(): lax.all_gather(w_up, ('dp', 'fsdp'), axis=0, tiled=True)  74.1 us
    all_gather x1, blocking collectives, body(): lax.all_gather(up_bias, ('dp', 'fsdp'), axis=0, tiled=True)  66.1 us
  transfers between devices with their start and end apart: 12, of which 9 were waited for; matrix products, arithmetic and copies ran while one was open for 13% of the time, Pallas kernels for 0%

commit v1 on v0

--- a/solution.py
+++ b/solution.py
@@ -1,10 +1,346 @@
+import functools
+
 import jax
 import jax.numpy as jnp
 from jax import lax
+from jax.experimental import pallas as pl
+from jax.experimental.pallas import tpu as pltpu
 from jax.sharding import PartitionSpec as P
 
 HEADS = 16
 BLOCK = 512
+MESH = pl.DeviceIdType.MESH
+WIDE = 512
+OUTER = 2
+
+
+class Place:
+    def __init__(self, dims):
+        self.size = {"a": dims[0], "b": dims[1], "c": 2, "z": dims[2]}
+        dp = lax.axis_index("dp")
+        self.at = {
+            "a": dp // (2 * dims[1]),
+            "b": (dp // 2) % dims[1],
+            "c": dp % 2,
+            "z": lax.axis_index("fsdp"),
+        }
+
+    def moved(self, axis, step):
+        spot = dict(self.at)
+        spot[axis] = (spot[axis] + step) % self.size[axis]
+        return spot
+
+    def device(self, axis, step):
+        spot = self.moved(axis, step)
+        return ((spot["a"] * self.size["b"] + spot["b"]) * 2 + spot["c"], spot["z"])
+
+    def partners(self, axis):
+        return range(1, self.size[axis])
+
+    def greet(self):
+        barrier = pltpu.get_barrier_semaphore()
+        count = 0
+        for axis in "abcz":
+            for step in self.partners(axis):
+                pl.semaphore_signal(
+                    barrier, 1, device_id=self.device(axis, step), device_id_type=MESH
+                )
+                count += 1
+        pl.semaphore_wait(barrier, count)
+
+
+def pieces_of(rows, columns, unit):
+    wide = min(WIDE, columns)
+    return [
+        (row, unit, column, wide)
+        for row in range(0, rows, unit)
+        for column in range(0, columns, wide)
+    ]
+
+
+def gather_kernel(dims, orders, lag, ahead, pieces, *refs):
+    count = len(pieces)
+    shards, wholes = refs[:count], refs[count : 2 * count]
+    local_sem, send_sem, recv_sem = refs[2 * count :]
+    place = Place(dims)
+    place.greet()
+    chunks = [
+        (shard.at[pl.ds(ro, rn), pl.ds(co, cn)], whole, pl.ds(ro, rn), pl.ds(co, cn))
+        for shard, whole, items in zip(shards, wholes, pieces)
+        for ro, rn, co, cn in items
+    ]
+    total = len(chunks)
+    sent, kept = [], []
+
+    def region(index, done, spot):
+        _, whole, rows, columns = chunks[index]
+        lead = tuple(slice(None) if axis in done else spot[axis] for axis in "abcz")
+        return whole.at[lead + (rows, columns)]
+
+    def copy(index, stage, step, axis, source, target):
+        return pltpu.make_async_remote_copy(
+            source,
+            target,
+            send_sem.at[index, stage, step - 1],
+            recv_sem.at[index, stage, step - 1],
+            device_id=place.device(axis, step),
+            device_id_type=MESH,
+        )
+
+    def send(index, stage):
+        order = orders[index % len(orders)]
+        axis, done = order[stage], order[:stage]
+        target = region(index, done, place.at)
+        for step in place.partners(axis):
+            item = copy(index, stage, step, axis, target if done else chunks[index][0], target)
+            item.start()
+            sent.append(item)
+
+    def receive(index, stage):
+        order = orders[index % len(orders)]
+        axis, done = order[stage], order[:stage]
+        for step in place.partners(axis):
+            target = region(index, done, place.moved(axis, place.size[axis] - step))
+            copy(index, stage, step, axis, target, target).wait_recv()
+
+    def begin(index):
+        if index < total:
+            item = pltpu.make_async_copy(
+                chunks[index][0], region(index, "", place.at), local_sem.at[index]
+            )
+            item.start()
+            kept.append(item)
+            send(index, 0)
+
+    for index in range(ahead):
+        begin(index)
+    for tick in range(total + 3 * lag):
+        begin(tick + ahead)
+        for stage in range(4):
+            index = tick - stage * lag
+            if 0 <= index < total:
+                receive(index, stage)
+                if stage == 0:
+                    kept[index].wait()
+                if stage < 3:
+                    send(index, stage + 1)
+    for item in sent:
+        item.wait_send()
+
+
+def gather(dims, shards, unit, lag=3, ahead=6):
+    pieces = [pieces_of(*shard.shape, min(unit, shard.shape[0])) for shard in shards]
+    total = sum(len(items) for items in pieces)
+    most = max(dims) - 1
+    anywhere = pl.BlockSpec(memory_space=pl.ANY)
+    orders = ("zbac", "zabc", "zbac", "zabc", "bzac", "azbc")
+    wholes = pl.pallas_call(
+        functools.partial(gather_kernel, dims, orders, lag, ahead, pieces),
+        out_shape=[
+            jax.ShapeDtypeStruct(dims[:2] + (2, dims[2]) + shard.shape, shard.dtype)
+            for shard in shards
+        ],
+        in_specs=[anywhere] * len(shards),
+        out_specs=[anywhere] * len(shards),
+        scratch_shapes=[
+            pltpu.SemaphoreType.DMA((total,)),
+            pltpu.SemaphoreType.DMA((total, 4, most)),
+            pltpu.SemaphoreType.DMA((total, 4, most)),
+        ],
+        compiler_params=pltpu.CompilerParams(collective_id=0, has_side_effects=True),
+        name="gather",
+    )(*shards)
+    return [whole.reshape((-1, whole.shape[-1])) for whole in wholes]
+
+
+def scatter_kernel(dims, lag, ahead, pieces, *refs):
+    count = len(pieces)
+    terms, owned = refs[:count], refs[count : 2 * count]
+    main = refs[2 * count : 2 * count + 7]
+    side = refs[2 * count + 7 : 2 * count + 12]
+    local_sem, send_sem, recv_sem = refs[2 * count + 12 :]
+    place = Place(dims)
+    place.greet()
+    spot = place.at
+    chunks = []
+    for array, items in enumerate(pieces):
+        for ro, rn, co, cn in items:
+            index = len(chunks)
+            if array == 0:
+                rooms = side
+                order = "ab"
+            else:
+                half = (index - 1) // 2
+                order = "ab" if index % 2 else "ba"
+                first, second = (main[2], main[4]) if index % 2 else (main[3], main[5])
+                rooms = (
+                    main[0].at[index - 1],
+                    main[1].at[index - 1],
+                    first.at[half],
+                    second.at[half],
+                    main[6].at[index - 1],
+                )
+            chunks.append((terms[array], owned[array], pl.ds(ro, rn), pl.ds(co, cn), order, rooms))
+    total = len(chunks)
+    sent, kept = [], []
+
+    def copy(index, stage, step, axis, source, target):
+        return pltpu.make_async_remote_copy(
+            source,
+            target,
+            send_sem.at[index, stage, step - 1],
+            recv_sem.at[index, stage, step - 1],
+            device_id=place.device(axis, step),
+            device_id_type=MESH,
+        )
+
+    def send(index, stage, step, axis, source, target):
+        item = copy(index, stage, step, axis, source, target)
+        item.start()
+        sent.append(item)
+
+    def begin(index):
+        if index < total:
+            term, _, rows, columns, _, rooms = chunks[index]
+            send(index, 0, 1, "c", term.at[:, :, 1 - spot["c"], :, rows, columns], rooms[1])
+            item = pltpu.make_async_copy(
+                term.at[:, :, spot["c"], :, rows, columns], rooms[0], local_sem.at[index]
+            )
+            item.start()
+            kept.append(item)
+
+    def await_all(index, stage, axis, room):
+        for step in place.partners(axis):
+            copy(index, stage, step, axis, room.at[step - 1], room.at[step - 1]).wait_recv()
+
+    def pick(order, first, second):
+        return (first, second) if order == "ab" else (second, first)
+
+    def after_core(index):
+        order, (own, other, came, _, _) = chunks[index][4:]
+        kept[index].wait()
+        copy(index, 0, 1, "c", other, other).wait_recv()
+        axis, rest = order
+
+        def add(where):
+            for item in range(place.size[rest]):
+                at = pick(order, where, item)
+                own[at] = own[at] + other[at]
+
+        for step in place.partners(axis):
+            where = place.moved(axis, step)[axis]
+            add(where)
+            source = own.at[where] if order == "ab" else own.at[:, where]
+            send(index, 1, step, axis, source, came.at[step - 1])
+        add(spot[axis])
+
+    def after_first(index):
+        order, (own, _, came, later, _) = chunks[index][4:]
+        axis, rest = order
+        await_all(index, 1, axis, came)
+
+        def add(where):
+            at = pick(order, spot[axis], where)
+            value = own[at].astype(jnp.float32)
+            for step in place.partners(axis):
+                value = value + came[step - 1, where].astype(jnp.float32)
+            own[at] = value.astype(own.dtype)
+
+        for step in place.partners(rest):
+            where = place.moved(rest, step)[rest]
+            add(where)
+            at = pick(order, spot[axis], where)
+            send(index, 2, step, rest, own.at[at], later.at[step - 1])
+        add(spot[rest])
+
+    def after_second(index):
+        _, result, rows, columns, order, (own, _, _, later, last) = chunks[index]
+        rest = order[1]
+        await_all(index, 2, rest, later)
+
+        def add(where):
+            value = own[spot["a"], spot["b"], where].astype(jnp.float32)
+            for step in place.partners(rest):
+                value = value + later[step - 1, where].astype(jnp.float32)
+            return value
+
+        for step in place.partners("z"):
+            where = place.moved("z", step)["z"]
+            own[spot["a"], spot["b"], where] = add(where).astype(own.dtype)
+            send(index, 3, step, "z", own.at[spot["a"], spot["b"], where], last.at[step - 1])
+        result[rows, columns] = add(spot["z"])
+
+    def after_last(index):
+        _, result, rows, columns, _, (_, _, _, _, last) = chunks[index]
+        await_all(index, 3, "z", last)
+        value = result[rows, columns]
+        for step in place.partners("z"):
+            value = value + last[step - 1].astype(jnp.float32)
+        result[rows, columns] = value
+
+    for index in range(ahead):
+        begin(index)
+    for tick in range(total + 3 * lag):
+        begin(tick + ahead)
+        for stage, work in enumerate((after_core, after_first, after_second, after_last)):
+            index = tick - stage * lag
+            if 0 <= index < total:
+                work(index)
+    for item in sent:
+        item.wait_send()
+
+
+def rooms_of(dims, many, unit, wide, dtype):
+    outer, inner, depth = dims
+    ones, twos = (many + 1) // 2, many // 2
+    tail = (unit, wide)
+    return [
+        pltpu.VMEM((many, outer, inner, depth) + tail, dtype),
+        pltpu.VMEM((many, outer, inner, depth) + tail, dtype),
+        pltpu.VMEM((ones, outer - 1, inner, depth) + tail, dtype),
+        pltpu.VMEM((twos, inner - 1, outer, depth) + tail, dtype),
+        pltpu.VMEM((ones, inner - 1, depth) + tail, dtype),
+        pltpu.VMEM((twos, outer - 1, depth) + tail, dtype),
+        pltpu.VMEM((many, depth - 1) + tail, dtype),
+    ]
+
+
+def scatter(dims, small, terms, unit, lag=2, ahead=4):
+    outer, inner, depth = dims
+    devices = 2 * outer * inner * depth
+    lead = (outer, inner, 2, depth)
+    arrays = [small.reshape(lead + small.shape[1:])] + [
+        term.reshape(lead + (term.shape[0] // devices, term.shape[1])) for term in terms
+    ]
+    pieces = [pieces_of(*arrays[0].shape[4:], arrays[0].shape[4])]
+    pieces += [pieces_of(*array.shape[4:], unit) for array in arrays[1:]]
+    total = sum(len(items) for items in pieces)
+    most = max(dims) - 1
+    tail = small.shape[1:]
+    side = [
+        pltpu.VMEM((outer, inner, depth) + tail, jnp.float32),
+        pltpu.VMEM((outer, inner, depth) + tail, jnp.float32),
+        pltpu.VMEM((outer - 1, inner, depth) + tail, jnp.float32),
+        pltpu.VMEM((inner - 1, depth) + tail, jnp.float32),
+        pltpu.VMEM((depth - 1,) + tail, jnp.float32),
+    ]
+    return pl.pallas_call(
+        functools.partial(scatter_kernel, dims, lag, ahead, pieces),
+        out_shape=[jax.ShapeDtypeStruct(array.shape[4:], jnp.float32) for array in arrays],
+        in_specs=[pl.BlockSpec(memory_space=pl.ANY)] * len(arrays),
+        out_specs=[pl.BlockSpec(memory_space=pltpu.VMEM)] * len(arrays),
+        scratch_shapes=rooms_of(dims, total - 1, unit, WIDE, jnp.bfloat16)
+        + side
+        + [
+            pltpu.SemaphoreType.DMA((total,)),
+            pltpu.SemaphoreType.DMA((total, 4, most)),
+            pltpu.SemaphoreType.DMA((total, 4, most)),
+        ],
+        compiler_params=pltpu.CompilerParams(
+            collective_id=1, has_side_effects=True, vmem_limit_bytes=60 << 20
+        ),
+        name="scatter",
+    )(*arrays)
 
 
 HIGH = lax.Precision.HIGHEST
@@ -195,15 +531,19 @@
     heads = HEADS
     head_width = width // heads
     count = slots * length
-    attention_set = (
-        lax.all_gather(norm1_gain, ("dp", "fsdp"), axis=0, tiled=True),
-        lax.all_gather(norm1_bias, ("dp", "fsdp"), axis=0, tiled=True),
-        lax.all_gather(w_query, ("dp", "fsdp"), axis=0, tiled=True),
-        lax.all_gather(w_key, ("dp", "fsdp"), axis=0, tiled=True),
-        lax.all_gather(w_value, ("dp", "fsdp"), axis=0, tiled=True),
-        lax.all_gather(w_out, ("dp", "fsdp"), axis=0, tiled=True),
-    )
-    gain_one, bias_one, full_query, full_key, full_value, full_out = attention_set
+    devices = lax.axis_size("dp") * lax.axis_size("fsdp")
+    dims = (OUTER, lax.axis_size("dp") // (2 * OUTER), lax.axis_size("fsdp"))
+    unit = width // devices
+    packed = jnp.concatenate([norm1_gain, norm1_bias, norm2_gain, norm2_bias, down_bias, up_bias])
+    packed = jnp.pad(packed, (0, 16 * 128 - packed.shape[0])).reshape(16, 128)
+    vectors, full_query, full_key, full_value, full_out, full_up, full_down = gather(
+        dims, [packed, w_query, w_key, w_value, w_out, w_up, w_down], unit
+    )
+    vectors = vectors.reshape(devices, 16 * 128)
+    gain_one, bias_one, gain_two, bias_two, full_down_bias = (
+        vectors[:, index * unit : (index + 1) * unit].reshape(-1) for index in range(5)
+    )
+    full_up_bias = vectors[:, 5 * unit : 5 * unit + up_bias.shape[0]].reshape(-1)
     inputs = tokens.reshape(count, width).astype(jnp.float32)
     normed_wide, pull_one = jax.vjp(
         norm_affine, inputs, gain_one.astype(jnp.float32), bias_one.astype(jnp.float32)
@@ -221,15 +561,6 @@
         attend_slot, (query_feat, key_feat, value_heads, crop_ids, kv_mask)
     )
     mixed = mixed_wide.reshape(count, width).astype(jnp.bfloat16)
-    feedforward_set = (
-        lax.all_gather(norm2_gain, ("dp", "fsdp"), axis=0, tiled=True),
-        lax.all_gather(norm2_bias, ("dp", "fsdp"), axis=0, tiled=True),
-        lax.all_gather(w_up, ("dp", "fsdp"), axis=0, tiled=True),
-        lax.all_gather(up_bias, ("dp", "fsdp"), axis=0, tiled=True),
-        lax.all_gather(w_down, ("dp", "fsdp"), axis=0, tiled=True),
-        lax.all_gather(down_bias, ("dp", "fsdp"), axis=0, tiled=True),
-    )
-    gain_two, bias_two, full_up, full_up_bias, full_down, full_down_bias = feedforward_set
     middle = inputs + jnp.dot(mixed, full_out, preferred_element_type=jnp.float32)
     normed_two_wide, pull_two = jax.vjp(
         norm_affine, middle, gain_two.astype(jnp.float32), bias_two.astype(jnp.float32)
@@ -246,48 +577,20 @@
         + full_down_bias.astype(jnp.float32)
     )
     output = result.astype(jnp.bfloat16).reshape(slots, length, width)
-    feedforward_set = (
-        lax.all_gather(norm2_gain, ("dp", "fsdp"), axis=0, tiled=True),
-        lax.all_gather(norm2_bias, ("dp", "fsdp"), axis=0, tiled=True),
-        lax.all_gather(w_up, ("dp", "fsdp"), axis=0, tiled=True),
-        lax.all_gather(up_bias, ("dp", "fsdp"), axis=0, tiled=True),
-        lax.all_gather(w_down, ("dp", "fsdp"), axis=0, tiled=True),
-        lax.all_gather(down_bias, ("dp", "fsdp"), axis=0, tiled=True),
-    )
-    attention_set = (
-        lax.all_gather(norm1_gain, ("dp", "fsdp"), axis=0, tiled=True),
-        lax.all_gather(norm1_bias, ("dp", "fsdp"), axis=0, tiled=True),
-        lax.all_gather(w_query, ("dp", "fsdp"), axis=0, tiled=True),
-        lax.all_gather(w_key, ("dp", "fsdp"), axis=0, tiled=True),
-        lax.all_gather(w_value, ("dp", "fsdp"), axis=0, tiled=True),
-        lax.all_gather(w_out, ("dp", "fsdp"), axis=0, tiled=True),
-    )
-    back_up = feedforward_set[2]
-    back_down = feedforward_set[4]
-    back_query = attention_set[2]
-    back_key = attention_set[3]
-    back_value = attention_set[4]
-    back_out = attention_set[5]
+    back_up, back_down = full_up, full_down
+    back_query, back_key, back_value, back_out = full_query, full_key, full_value, full_out
     grad_out = cotangent.reshape(count, width)
     grad_down_bias = jnp.sum(grad_out.astype(jnp.float32), axis=0)
-    grad_w_down = jnp.dot(hidden.T, grad_out, preferred_element_type=jnp.float32)
+    grad_w_down = jnp.dot(hidden.T, grad_out, preferred_element_type=jnp.float32).astype(jnp.bfloat16)
     grad_hidden = jnp.dot(grad_out, back_down.T, preferred_element_type=jnp.float32)
     grad_upper = pull_gelu(grad_hidden)[0].astype(jnp.bfloat16)
     grad_up_bias = jnp.sum(grad_upper.astype(jnp.float32), axis=0)
-    grad_w_up = jnp.dot(normed_two.T, grad_upper, preferred_element_type=jnp.float32)
+    grad_w_up = jnp.dot(normed_two.T, grad_upper, preferred_element_type=jnp.float32).astype(jnp.bfloat16)
     grad_normed_two = jnp.dot(grad_upper, back_up.T, preferred_element_type=jnp.float32)
     grad_middle_part, grad_gain_two, grad_bias_two = pull_two(grad_normed_two)
-    feedforward_owned = (
-        lax.psum_scatter(grad_gain_two, ("dp", "fsdp"), scatter_dimension=0, tiled=True),
-        lax.psum_scatter(grad_bias_two, ("dp", "fsdp"), scatter_dimension=0, tiled=True),
-        lax.psum_scatter(grad_w_up, ("dp", "fsdp"), scatter_dimension=0, tiled=True),
-        lax.psum_scatter(grad_up_bias, ("dp", "fsdp"), scatter_dimension=0, tiled=True),
-        lax.psum_scatter(grad_w_down, ("dp", "fsdp"), scatter_dimension=0, tiled=True),
-        lax.psum_scatter(grad_down_bias, ("dp", "fsdp"), scatter_dimension=0, tiled=True),
-    )
     grad_middle = grad_out.astype(jnp.float32) + grad_middle_part
     grad_attended = grad_middle.astype(jnp.bfloat16)
-    grad_w_out = jnp.dot(mixed.T, grad_attended, preferred_element_type=jnp.float32)
+    grad_w_out = jnp.dot(mixed.T, grad_attended, preferred_element_type=jnp.float32).astype(jnp.bfloat16)
     grad_mixed = jnp.dot(grad_attended, back_out.T, preferred_element_type=jnp.float32).reshape(
         slots, length, heads, head_width
     )
@@ -310,39 +613,57 @@
     grad_query = pull_query(grad_query_feat.reshape(count, width))[0].astype(jnp.bfloat16)
     grad_keys = pull_key(grad_key_feat.reshape(count, width))[0].astype(jnp.bfloat16)
     grad_values = grad_values.reshape(count, width).astype(jnp.bfloat16)
-    grad_w_query = jnp.dot(normed.T, grad_query, preferred_element_type=jnp.float32)
-    grad_w_key = jnp.dot(normed.T, grad_keys, preferred_element_type=jnp.float32)
-    grad_w_value = jnp.dot(normed.T, grad_values, preferred_element_type=jnp.float32)
+    grad_w_query = jnp.dot(normed.T, grad_query, preferred_element_type=jnp.float32).astype(jnp.bfloat16)
+    grad_w_key = jnp.dot(normed.T, grad_keys, preferred_element_type=jnp.float32).astype(jnp.bfloat16)
+    grad_w_value = jnp.dot(normed.T, grad_values, preferred_element_type=jnp.float32).astype(jnp.bfloat16)
     grad_normed = jnp.dot(grad_query, back_query.T, preferred_element_type=jnp.float32)
     grad_normed = grad_normed + jnp.dot(grad_keys, back_key.T, preferred_element_type=jnp.float32)
     grad_normed = grad_normed + jnp.dot(
         grad_values, back_value.T, preferred_element_type=jnp.float32
     )
     grad_input_part, grad_gain_one, grad_bias_one = pull_one(grad_normed)
-    attention_owned = (
-        lax.psum_scatter(grad_gain_one, ("dp", "fsdp"), scatter_dimension=0, tiled=True),
-        lax.psum_scatter(grad_bias_one, ("dp", "fsdp"), scatter_dimension=0, tiled=True),
-        lax.psum_scatter(grad_w_query, ("dp", "fsdp"), scatter_dimension=0, tiled=True),
-        lax.psum_scatter(grad_w_key, ("dp", "fsdp"), scatter_dimension=0, tiled=True),
-        lax.psum_scatter(grad_w_value, ("dp", "fsdp"), scatter_dimension=0, tiled=True),
-        lax.psum_scatter(grad_w_out, ("dp", "fsdp"), scatter_dimension=0, tiled=True),
-    )
+    small = jnp.concatenate(
+        [
+            vector.reshape(devices, -1)
+            for vector in (
+                grad_gain_one,
+                grad_bias_one,
+                grad_gain_two,
+                grad_bias_two,
+                grad_down_bias,
+                grad_up_bias,
+            )
+        ],
+        axis=1,
+    )
+    small = jnp.pad(small, ((0, 0), (0, 8 * 128 - small.shape[1]))).reshape(devices, 8, 128)
+    small, own_up, own_down, own_query, own_key, own_value, own_out = scatter(
+        dims,
+        small,
+        [grad_w_up, grad_w_down, grad_w_query, grad_w_key, grad_w_value, grad_w_out],
+        unit,
+    )
+    small = small.reshape(8 * 128)
+    own_gain_one, own_bias_one, own_gain_two, own_bias_two, own_down_bias = (
+        small[index * unit : (index + 1) * unit] for index in range(5)
+    )
+    own_up_bias = small[5 * unit : 5 * unit + up_bias.shape[0]]
     input_grad = (grad_middle + grad_input_part).astype(jnp.bfloat16).reshape(slots, length, width)
     return (
         output,
         input_grad,
-        attention_owned[0],
-        attention_owned[1],
-        attention_owned[2],
-        attention_owned[3],
-        attention_owned[4],
-        attention_owned[5],
-        feedforward_owned[0],
-        feedforward_owned[1],
-        feedforward_owned[2],
-        feedforward_owned[3],
-        feedforward_owned[4],
-        feedforward_owned[5],
+        own_gain_one,
+        own_bias_one,
+        own_query,
+        own_key,
+        own_value,
+        own_out,
+        own_gain_two,
+        own_bias_two,
+        own_up,
+        own_up_bias,
+        own_down,
+        own_down_bias,
     )
 
 

time: 1770 us -> 506 us (0.29)
  waiting for transfers between devices: 1340 us -> 0 us
  Pallas kernels: 0 us -> 248 us
  blocking collectives: 149 us -> 0 us
  matrix products: 216 us -> 197 us
    reduce_scatter x6 -> x0, waiting for transfers between devices: 1140 us -> none  [the longest x1 366 us: body(): lax.psum_scatter(grad_w_up, ('dp', 'fsdp'), scatter_dimension=0, tiled=True)]
    pallas_call x0 -> x2, Pallas kernels: none -> 248 us  [the longest x1 125 us: scatter(): pl.pallas_call(functools.partial(scatter_kernel, dims, lag, ahead, pieces...]
    all_gather x6 -> x0, waiting for transfers between devices: 196 us -> none  [the longest x1 74.1 us: body(): lax.all_gather(w_up, ('dp', 'fsdp'), axis=0, tiled=True)]
    unnamed x2 -> x0, blocking collectives: 82.7 us -> none
    all_gather x1 -> x0, blocking collectives: 66.1 us -> none  [body(): lax.all_gather(up_bias, ('dp', 'fsdp'), axis=0, tiled=True)]
  transfers between devices with their start and end apart: 12 -> 0, of which waited for: 9 -> 0; matrix products, arithmetic and copies ran while one was open for 13% -> 0% of each run, Pallas kernels for 0% -> 0%
where the time goes in v1:
time: 506 us; the launch traced here: 501 us
  Pallas kernels  248 us (49%)
  matrix products  197 us (39%)
  local copies, waits for them, and re-layouts  36.4 us (7%)
  other arithmetic  18.1 us (4%)
    pallas_call x1, Pallas kernels, scatter(): pl.pallas_call(functools.partial(scatter_kernel, dims, lag, ahead, pieces...  125 us
    pallas_call x1, Pallas kernels, gather(): pl.pallas_call(functools.partial(gather_kernel, dims, orders, lag, ahead,...  123 us
    dot_general x1, matrix products, body(): jnp.dot(normed_two, full_up, preferred_element_type=jnp.float32)  28 us
    dot_general x1, matrix products, attend_backward(): grad_value = jnp.einsum('hij,ihe->jhe', scores, grad_numer, precision=HIGH)  19.5 us
    unnamed x77, local copies, waits for them, and re-layouts  16.6 us
    dot_general x1, matrix products, body(): jnp.dot(grad_out, back_down.T, preferred_element_type=jnp.float32)  16.3 us
    dot_general x1, matrix products, attend_backward(): jnp.einsum('hij,jhe->ihe', grad_scores, key_wide, precision=HIGH)  14.5 us
    dot_general x1, matrix products, attend_backward(): jnp.einsum('hij,ihe->jhe', grad_scores, query_wide, precision=HIGH)  13.5 us

profile of v1, /device:TPU:0, one launch (start us, length us, event | category | flops | bytes accessed | tf_op | source)
XLA Modules:
  0.0 500.8 jit_solution(954130159671652468)
XLA Ops:
  2.7 4.1 concatenate.6
  11.5 122.7 %gather.1 = (bf16[2,2,2,4,16,128]{5,4,3,2,1,0:T(8,128)(2,1)}, bf16[2,2,2,4,32,1024]{5,4,3,2,1,0:T(8,128)(2,1)}, bf16[2,2,2,4,32,1024]{5,4,3,2,1,0:T(8,128)(2,1)}...) custom-call(bf16[16,128]{1,0:T(8,128)(2,1)} %pad_bitcast_fusion.1.re, ...), custom_call_target="tpu_custom_call" | custom-call | tf_op jit(solution)/shard_map/gather/pallas_call | solution.py:137
  135.7 3.9 convolution_convert_fusion.6
  141.5 5.1 %fusion.49 = (bf16[512,1024]{1,0:T(8,128)(2,1)}, f32[512,1024]{1,0:T(8,128)}) fusion(bf16[1024,1024]{1,0:T(8,128)(2,1)} %bitcast.231, bf16[1,512,1024]{2,1,0:T(8,128)(2,1)S(1)} %copy-done, f32[1024]{0:T(1024)S(1)} %reshape.549, f32[1024]{0:T(1024)S(1)} %reshape.548, f32[512]{0:T(512)S(1)} %fusion.73, f32[512]{0:T(512)S(1)} %broadcast_multiply_fusion.1), kind=kOutput, calls=%fused_computation.86 | convolution fusion | flops 1079508992 | bytes 6303744 | tf_op jit(solution)/shard_map/dot_general | solution.py:552
  146.6 2.3 copy.49
  150.6 5.1 %fusion.46 = (bf16[512,1024]{1,0:T(8,128)(2,1)}, f32[512,1024]{1,0:T(8,128)}) fusion(bf16[1024,1024]{1,0:T(8,128)(2,1)} %bitcast.233, bf16[1,512,1024]{2,1,0:T(8,128)(2,1)S(1)} %copy-done, f32[1024]{0:T(1024)S(1)} %reshape.549, f32[1024]{0:T(1024)S(1)} %reshape.548, f32[512]{0:T(512)S(1)} %fusion.73, f32[512]{0:T(512)S(1)} %broadcast_multiply_fusion.1), kind=kOutput, calls=%fused_computation.79 | convolution fusion | flops 1079508992 | bytes 6303744 | tf_op jit(solution)/shard_map/dot_general | solution.py:553
  155.7 2.3 copy.50
  157.9 9.7 %multiply_reduce_fusion = (f32[16,512]{1,0:T(8,128)S(1)}, f32[16,512,512]{1,2,0:T(8,128)}) fusion(f32[512,512]{0,1:T(8,128)S(1)} %fusion.63, bf16[512,16,64]{0,2,1:T(8,128)(2,1)} %bitcast.193, bf16[512,16,64]{0,2,1:T(8,128)(2,1)} %bitcast.196), kind=kOutput, calls=%fused_computation.5 | convolution fusion | flops 545251328 | bytes 19955712 | tf_op jit(solution)/shard_map/while/body/eval_jaxpr/while/body/eval_jaxpr/ihe,jhe->hij/dot_general | solution.py:378
  167.6 10.8 %fusion.4 = f32[16,64,512]{2,1,0:T(8,128)S(1)} fusion(bf16[512,16,64]{0,2,1:T(8,128)(2,1)S(1)} %bitcast.189, f32[16,512,512]{1,2,0:T(8,128)} %get-tuple-element.253, f32[512,512]{0,1:T(8,128)S(1)} %fusion.63), kind=kOutput, calls=%fused_computation.6 | convolution fusion | flops 3225419776 | bytes 20971520 | tf_op jit(solution)/shard_map/while/body/eval_jaxpr/while/body/eval_jaxpr/hij,jhe->ihe/dot_general | solution.py:384
  178.5 2.5 fusion.94
  182.7 28.0 %multiply_convert_fusion = (bf16[512,4096]{1,0:T(8,128)(2,1)S(1)}, f32[512,4096]{1,0:T(8,128)}, f32[512,4096]{1,0:T(8,128)}) fusion(f32[4096]{0:T(1024)S(1)} %fusion.72, bf16[1024,4096]{1,0:T(8,128)(2,1)} %bitcast.225, f32[512,1024]{1,0:T(8,128)S(1)} %get-tuple-element.257, f32[1024]{0:T(1024)S(1)} %reshape.551, f32[1024]{0:T(1024)S(1)} %reshape.550, ...), kind=kOutput, calls=%fused_computation.22 | convolution fusion | flops 4436000768 | bytes 31485952 | tf_op jit(solution)/shard_map/dot_general | solution.py:569
  210.6 16.3 %convert_reduce_fusion = (f32[4096]{0:T(1024)S(1)}, bf16[512,4096]{1,0:T(8,128)(2,1)}) fusion(f32[512,4096]{1,0:T(8,128)} %get-tuple-element.233, bf16[4096,1024]{1,0:T(8,128)(2,1)} %bitcast.229, bf16[1,512,1024]{2,1,0:T(8,128)(2,1)S(1)} %copy-done.10, f32[512,4096]{1,0:T(8,128)} %get-tuple-element.258, f32[4096]{0:T(1024)S(1)} %fusion.72), kind=kOutput, calls=%fused_computation.19 | convolution fusion | flops 4330614784 | bytes 30441472 | tf_op jit(solution)/shard_map/dot_general | solution.py:585
  227.0 8.9 %fusion.50 = bf16[1,512,1024]{2,1,0:T(8,128)(2,1)} fusion(f32[512,1024]{1,0:T(8,128)S(1)} %get-tuple-element.257, bf16[512,4096]{1,0:T(8,128)(2,1)S(1)} %get-tuple-element.232, bf16[4096,1024]{1,0:T(8,128)(2,1)} %bitcast.230, f32[1024]{0:T(1024)S(1)} %reshape.553), kind=kOutput, calls=%fused_computation.97 | convolution fusion | flops 4296540160 | bytes 15732736 | tf_op jit(solution)/shard_map/dot_general | solution.py:576
  235.9 7.0 %multiply_reduce_fusion.1 = (f32[1024]{0:T(1024)S(1)}, f32[512]{0:T(512)S(1)}, f32[1024]{0:T(1024)S(1)}, f32[512,1024]{1,0:T(8,128)S(1)}) fusion(f32[512,1024]{1,0:T(8,128)S(1)} %get-tuple-element.257, f32[512]{0:T(512)S(1)} %fusion.74, f32[512]{0:T(512)S(1)} %broadcast_multiply_fusion, f32[1024]{0:T(1024)S(1)} %reshape.550, ...), kind=kOutput, calls=%fused_computation.70 | convolution fusion | flops 4299159040 | bytes 16795648 | tf_op jit(solution)/shard_map/dot_general | solution.py:589
  243.0 2.0 fusion.91
  245.1 2.3 fusion.51
  249.6 19.5 %fusion.2 = f32[16,64,512]{2,1,0:T(8,128)S(1)} fusion(f32[16,512,512]{1,2,0:T(8,128)} %get-tuple-element.253, f32[512,512]{0,1:T(8,128)S(1)} %fusion.63, f32[512,16,64]{0,2,1:T(8,128)S(1)} %get-tuple-element.261, f32[512,16]{0,1:T(8,128)S(1)} %fusion.71), kind=kOutput, calls=%fused_computation.3 | convolution fusion | flops 3225944064 | bytes 22052864 | tf_op jit(solution)/shard_map/while/body/eval_jaxpr/while/body/eval_jaxpr/hij,ihe->jhe/dot_general | solution.py:441
  270.4 2.6 convolution_convert_fusion.2
  274.3 7.4 %convolution_convert_fusion.1 = bf16[1024,4096]{1,0:T(8,128)(2,1)} fusion(bf16[512,4096]{1,0:T(8,128)(2,1)S(1)} %copy-done.31, f32[512,1024]{1,0:T(8,128)S(1)} %copy-done.2, f32[1024]{0:T(1024)S(1)} %reshape.551, f32[1024]{0:T(1024)S(1)} %reshape.550, f32[512]{0:T(512)S(1)} %fusion.74, f32[512]{0:T(512)S(1)} %broadcast_multiply_fusion), kind=kOutput, calls=%fused_computation.41 | convolution fusion | flops 4301783040 | bytes 14692352 | tf_op jit(solution)/shard_map/dot_general | solution.py:588
  281.7 2.8 convolution_convert_fusion.3
  287.1 6.8 %convolution_convert_fusion = bf16[4096,1024]{1,0:T(8,128)(2,1)} fusion(bf16[512,4096]{1,0:T(8,128)(2,1)S(1)} %copy-done.30, bf16[1,512,1024]{2,1,0:T(8,128)(2,1)S(1)} %copy-done.11), kind=kOutput, calls=%fused_computation.40 | convolution fusion | flops 4299161600 | bytes 13631488 | tf_op jit(solution)/shard_map/dot_general | solution.py:584
  293.8 10.4 %fusion.79 = f32[16,512,512]{1,2,0:T(8,128)} fusion(bf16[512,16,64]{0,2,1:T(8,128)(2,1)S(1)} %bitcast.190, f32[512,16,64]{0,2,1:T(8,128)S(1)} %get-tuple-element.261, f32[512,16]{0,1:T(8,128)S(1)} %fusion.71), kind=kOutput, calls=%fused_computation.150 | convolution fusion | flops 3221749760 | bytes 19955712 | tf_op jit(solution)/shard_map/while/body/eval_jaxpr/while/body/eval_jaxpr/ihe,jhe->hij/dot_general | solution.py:425
  304.3 14.5 %fusion.43 = f32[512,16,64]{0,2,1:T(8,128)} fusion(f32[16,64,512]{2,1,0:T(8,128)S(1)} %fusion.67, bf16[512,16,64]{0,2,1:T(8,128)(2,1)S(1)} %bitcast.198, f32[16,512,512]{1,2,0:T(8,128)} %fusion.79, f32[16,512]{1,0:T(8,128)S(1)} %bitcast_divide_fusion.1, f32[512,512]{0,1:T(8,128)S(1)} %fusion.63, f32[512,16]{0,1:T(8,128)S(1)} %divide_multiply_fusion, ...), kind=kOutput, calls=%fused_computation.68 | convolution fusion | flops 3231186944 | bytes 23136256 | tf_op jit(solution)/shard_map/while/body/eval_jaxpr/while/body/eval_jaxpr/hij,jhe->ihe/dot_general | solution.py:432
  318.8 13.5 %fusion = f32[16,64,512]{2,1,0:T(8,128)S(1)} fusion(bf16[512,16,64]{0,2,1:T(8,128)(2,1)S(1)} %bitcast.195, f32[16,512,512]{1,2,0:T(8,128)} %fusion.79, f32[16,512]{1,0:T(8,128)S(1)} %bitcast_divide_fusion.1, f32[512,512]{0,1:T(8,128)S(1)} %fusion.63), kind=kOutput, calls=%fused_computation.1 | convolution fusion | flops 3229614080 | bytes 21004288 | tf_op jit(solution)/shard_map/while/body/eval_jaxpr/while/body/eval_jaxpr/hij,ihe->jhe/dot_general | solution.py:437
  332.3 2.4 multiply_add_fusion
  336.6 2.4 add_convert_fusion.2
  339.0 2.6 fusion.98
  343.5 3.0 add_convert_fusion.3
  353.7 2.1 convert_reduce_fusion.2
  356.8 4.1 convolution_convert_fusion.5
  360.9 2.8 convolution_convert_fusion.4
  363.7 125.1 %scatter.1 = (f32[8,128]{1,0:T(8,128)}, f32[32,4096]{1,0:T(8,128)}, f32[128,1024]{1,0:T(8,128)}, f32[32,1024]{1,0:T(8,128)}, f32[32,1024]{1,0:T(8,128)}, /*index=5*/f32[32,1024]{1,0:T(8,128)}, f32[32,1024]{1,0:T(8,128)}) custom-call(f32[2,2,2,4,8,128]{5,4,3,2,1,0:T(8,128)} %bitcast.215, bf16[2,2,2,4,32,4096]{5,4,3,2,1,0:T(8,128)(2,1)} %bitcast.201, ...), custom_call_target="tpu_custom_call" | custom-call | tf_op jit(solution)/shard_map/scatter/pallas_call | solution.py:327
  (124 shorter events, 44.5 us)
Async XLA Ops:
  0.6 9.9 %copy-start.24 = (s32[1,512]{1,0:T(1,128)S(1)}, s32[1,512]{1,0:T(1,128)}, u32[]{:S(2)}) copy-start(s32[1,512]{1,0:T(1,128)} %param.17) | copy-start | bytes 6148
  6.8 128.9 %copy-start = (bf16[1,512,1024]{2,1,0:T(8,128)(2,1)S(1)}, bf16[1,512,1024]{2,1,0:T(8,128)(2,1)}, u32[]{:S(2)}) copy-start(bf16[1,512,1024]{2,1,0:T(8,128)(2,1)} %param.16) | copy-start | bytes 3145732
  9.9 129.6 %copy-start.25 = (f32[512]{0:T(512)}, f32[512]{0:T(512)S(1)}, u32[]{:S(2)}) copy-start(f32[512]{0:T(512)S(1)} %fusion.36) | copy-start | bytes 6148
  167.6 10.8 %copy-start.4 = (bf16[512,1024]{0,1:T(8,128)(2,1)S(1)}, bf16[512,1024]{0,1:T(8,128)(2,1)}, u32[]{:S(2)}) copy-start(bf16[512,1024]{0,1:T(8,128)(2,1)} %copy.49) | copy-start | bytes 3145732
  178.4 2.5 copy-start.7
  180.9 1.4 copy-start.21
  180.9 55.0 %slice-start = ((s8[8388608]{0:T(1024)(128)(4,1)}), s8[4194304]{0:T(1024)(128)(4,1)S(1)}, s32[]{:S(2)}) async-start(s8[8388608]{0:T(1024)(128)(4,1)} %bitcast.226), calls=%async_computation | async-start | bytes 8388608
  182.3 60.7 %copy-start.1 = (f32[512,1024]{1,0:T(8,128)}, f32[512,1024]{1,0:T(8,128)S(1)}, u32[]{:S(2)}) copy-start(f32[512,1024]{1,0:T(8,128)S(1)} %get-tuple-element.257) | copy-start | bytes 6291460
  182.7 28.0 %copy-start.10 = (bf16[1,512,1024]{2,1,0:T(8,128)(2,1)S(1)}, bf16[1,512,1024]{2,1,0:T(8,128)(2,1)}, u32[]{:S(2)}) copy-start(bf16[1,512,1024]{2,1,0:T(8,128)(2,1)} %param.31) | copy-start | bytes 3145732
  182.7 53.2 %slice-start.1 = ((s8[8388608]{0:T(1024)(128)(4,1)}), s8[4194304]{0:T(1024)(128)(4,1)S(1)}, s32[]{:S(2)}) async-start(s8[8388608]{0:T(1024)(128)(4,1)} %bitcast.226), calls=%async_computation.1 | async-start | bytes 8388608
  210.6 16.4 %copy-start.29 = (bf16[512,4096]{1,0:T(8,128)(2,1)}, bf16[512,4096]{1,0:T(8,128)(2,1)S(1)}, u32[]{:S(2)}) copy-start(bf16[512,4096]{1,0:T(8,128)(2,1)S(1)} %get-tuple-element.232) | copy-start | bytes 12582916
  245.1 2.5 copy-start.8
  245.1 3.2 copy-start.15
  249.6 19.6 %copy-start.6 = (bf16[512,1024]{0,1:T(8,128)(2,1)S(1)}, bf16[512,1024]{0,1:T(8,128)(2,1)}, u32[]{:S(2)}) copy-start(bf16[512,1024]{0,1:T(8,128)(2,1)} %copy.50) | copy-start | bytes 3145732
  270.3 11.4 %copy-start.13 = (bf16[16,64,512]{2,1,0:T(8,128)(2,1)}, bf16[16,64,512]{2,1,0:T(8,128)(2,1)S(1)}, u32[]{:S(2)}) copy-start(bf16[16,64,512]{2,1,0:T(8,128)(2,1)S(1)} %add_convert_fusion.1) | copy-start | bytes 3145732
  270.4 2.6 copy-start.2
  270.4 3.9 copy-start.31
  284.6 1.8 copy-start.11
  284.6 2.5 copy-start.30
  304.2 14.6 %copy-start.5 = (bf16[512,1024]{0,1:T(8,128)(2,1)S(1)}, bf16[512,1024]{0,1:T(8,128)(2,1)}, u32[]{:S(2)}) copy-start(bf16[512,1024]{0,1:T(8,128)(2,1)} %copy.49) | copy-start | bytes 3145732
  336.6 2.4 copy-start.28
  339.0 2.6 copy-start.18
  339.0 2.6 copy-start.9
  343.5 4.0 copy-start.27
  347.5 1.3 copy-start.14
  347.5 1.9 copy-start.16
  347.5 2.5 copy-start.17
  350.1 1.8 copy-start.26
  351.8 1.6 copy-start.3
  351.9 1.9 copy-start.12
  356.8 4.1 copy-start.19
  488.9 10.9 %copy-start.23 = (f32[128,1024]{1,0:T(8,128)S(1)}, f32[128,1024]{1,0:T(8,128)}, u32[]{:S(2)}) copy-start(f32[128,1024]{1,0:T(8,128)} %get-tuple-element.291) | copy-start | bytes 1572868
  (2 other events, 2.2 us)

commit v2 on v1

--- a/solution.py
+++ b/solution.py
@@ -509,7 +509,7 @@
     return (grad_query.reshape(shape), grad_key.reshape(shape), grad_value.reshape(shape))
 
 
-def body(
+def general_body(
     tokens,
     crop_ids,
     kv_mask,
@@ -664,6 +664,1170 @@
         own_up_bias,
         own_down,
         own_down_bias,
+    )
+
+
+LENGTH = 512
+WIDTH = 1024
+HIDDEN = 4096
+UNIT = 32
+GATHERED = 24
+DOWN, UP = 8, 16
+LAG = 2
+AHEAD = 4
+WIDE32 = jnp.float32
+HALF16 = jnp.bfloat16
+VMEM_LIMIT = 63 << 20
+
+
+def when(condition):
+    if isinstance(condition, bool):
+        return (lambda work: work()) if condition else (lambda work: None)
+    return pl.when(condition)
+
+
+def each(count, work):
+    def step(index, carry):
+        work(index)
+        return carry
+
+    lax.fori_loop(0, count, step, 0)
+
+
+def dot(left, right):
+    return jnp.dot(left, right, preferred_element_type=jnp.float32)
+
+
+def dot_nt(left, right):
+    return lax.dot_general(
+        left, right, (((1,), (1,)), ((), ())), preferred_element_type=jnp.float32
+    )
+
+
+def dot_tn(left, right):
+    return lax.dot_general(
+        left, right, (((0,), (0,)), ((), ())), preferred_element_type=jnp.float32
+    )
+
+
+class Mover:
+    def __init__(self, place, send_sem, recv_sem):
+        self.place, self.send_sem, self.recv_sem = place, send_sem, recv_sem
+
+    def copy(self, lead, stage, step, axis, source, target):
+        at = lead + (stage, step - 1)
+        return pltpu.make_async_remote_copy(
+            source,
+            target,
+            self.send_sem.at[at],
+            self.recv_sem.at[at],
+            device_id=self.place.device(axis, step),
+            device_id_type=MESH,
+        )
+
+
+class Gather(Mover):
+    def region(self, chunk, done, spot):
+        lead = tuple(slice(None) if axis in done else spot[axis] for axis in "abcz")
+        return chunk.at[lead]
+
+    def send(self, chunk, lead, order, stage):
+        axis, done = order[stage], order[:stage]
+        source = self.region(chunk, done, self.place.at)
+        for step in self.place.partners(axis):
+            self.copy(lead, stage, step, axis, source, source).start()
+
+    def receive(self, chunk, lead, order, stage):
+        axis, done = order[stage], order[:stage]
+        for step in self.place.partners(axis):
+            spot = self.place.moved(axis, self.place.size[axis] - step)
+            target = self.region(chunk, done, spot)
+            self.copy(lead, stage, step, axis, target, target).wait_recv()
+
+    def drain(self, chunk, lead, order):
+        for stage in range(4):
+            axis, done = order[stage], order[:stage]
+            source = self.region(chunk, done, self.place.at)
+            for step in self.place.partners(axis):
+                self.copy(lead, stage, step, axis, source, source).wait_send()
+
+
+class Weights(Gather):
+    orders = ("zbac", "zabc")
+
+    def __init__(self, place, buffer, send_sem, recv_sem):
+        super().__init__(place, send_sem, recv_sem)
+        self.buffer, self.total = buffer, buffer.shape[0]
+
+    def by_order(self, index, work):
+        for parity, order in enumerate(self.orders):
+
+            @when(index % 2 == parity)
+            def _(order=order):
+                work(order)
+
+    def begin(self, index):
+        @when(index < self.total)
+        def _():
+            self.send(self.buffer.at[index], (index,), self.orders[0], 0)
+
+    def tick(self, now):
+        self.begin(now + AHEAD)
+        for stage in range(4):
+            index = now - stage * LAG
+            live = (index >= 0) & (index < self.total)
+
+            @when(live)
+            def _(index=index, stage=stage):
+                def work(order):
+                    chunk = self.buffer.at[index]
+                    self.receive(chunk, (index,), order, stage)
+                    if stage < 3:
+                        self.send(chunk, (index,), order, stage + 1)
+
+                self.by_order(index, work)
+
+    def finish(self):
+        each(
+            self.total,
+            lambda index: self.by_order(
+                index, lambda order: self.drain(self.buffer.at[index], (index,), order)
+            ),
+        )
+
+
+def moments(values):
+    mean = jnp.mean(values, axis=-1, keepdims=True)
+    centred = values - mean
+    spread = jnp.mean(centred * centred, axis=-1, keepdims=True)
+    scale = lax.rsqrt(spread + norm_eps)
+    return centred * scale, scale
+
+
+def gelu_pair(upper):
+    bell = jnp.exp(-0.5 * upper * upper) * 0.3989422804014327
+    below = 0.5 * (1.0 + lax.erf(upper * 0.7071067811865476))
+    return upper * below, below + upper * bell
+
+
+def matrix(buffer, index):
+    return buffer[index].reshape(WIDTH, WIDE)
+
+
+def column_of(row):
+    tall = jnp.transpose(jnp.broadcast_to(row.astype(jnp.float32), (8, row.shape[1])))
+    return tall[:, 0:1]
+
+
+def read_vectors(gathered, devices):
+    flat = gathered[...].reshape(devices * 8, 128).astype(jnp.bfloat16)
+
+    def line(number):
+        shape = (devices, devices * 8)
+        wanted = lax.broadcasted_iota(jnp.int32, shape, 0) * 8 + number
+        chosen = lax.broadcasted_iota(jnp.int32, shape, 1) == wanted
+        return dot(chosen.astype(jnp.bfloat16), flat).astype(jnp.bfloat16)
+
+    def spread(lines, start, wide):
+        total = wide * devices
+        lane = lax.broadcasted_iota(jnp.int32, (128, total), 1)
+        wanted = lax.broadcasted_iota(jnp.int32, (128, total), 0) == start + lane % wide
+        found = dot(lines, wanted.astype(jnp.bfloat16))
+        owner = lax.broadcasted_iota(jnp.int32, (devices, total), 1) // wide
+        mine = owner == lax.broadcasted_iota(jnp.int32, (devices, total), 0)
+        return jnp.sum(jnp.where(mine, found, 0.0), axis=0, keepdims=True)
+
+    first = line(0)
+    rows = [spread(first, index * UNIT, UNIT) for index in range(4)]
+    rows.append(spread(line(2), 0, UNIT))
+    return rows, spread(line(1), 0, 4 * UNIT)
+
+
+def write_vectors(rows, devices):
+    result = None
+    for index, row in enumerate(rows):
+        owner = lax.broadcasted_iota(jnp.int32, (devices, WIDTH), 1) // UNIT
+        mine = owner == lax.broadcasted_iota(jnp.int32, (devices, WIDTH), 0)
+        spread = jnp.where(mine, row, 0.0)
+        lane = lax.broadcasted_iota(jnp.int32, (WIDTH, 128), 0)
+        wanted = lax.broadcasted_iota(jnp.int32, (WIDTH, 128), 1) == index * UNIT + lane % UNIT
+        found = jnp.dot(
+            spread,
+            wanted.astype(jnp.float32),
+            preferred_element_type=jnp.float32,
+            precision=HIGH,
+        )
+        result = found if result is None else result + found
+    return result
+
+
+def head_lanes(which, shape):
+    lane = lax.broadcasted_iota(jnp.int32, shape, 1)
+    return lane < 64 if which == 0 else lane >= 64
+
+
+def allowed(crop_row, mask_row):
+    shape = (LENGTH, LENGTH)
+    row = lax.broadcasted_iota(jnp.int32, shape, 0)
+    column = lax.broadcasted_iota(jnp.int32, shape, 1)
+    same = column_of(crop_row) == crop_row.astype(jnp.float32)
+    seen = (mask_row > 0) | (row == column)
+    return jnp.where(same & (column <= row) & seen, 1.0, 0.0).astype(jnp.bfloat16)
+
+
+def allowed_back(crop_row, mask_row):
+    shape = (LENGTH, LENGTH)
+    row = lax.broadcasted_iota(jnp.int32, shape, 0)
+    column = lax.broadcasted_iota(jnp.int32, shape, 1)
+    same = column_of(crop_row) == crop_row.astype(jnp.float32)
+    seen = (column_of(mask_row) > 0) | (row == column)
+    return jnp.where(same & (row <= column) & seen, 1.0, 0.0).astype(jnp.bfloat16)
+
+
+def transpose_into(source, target):
+    def work(index):
+        at = pl.ds(pl.multiple_of(index * 128, 128), 128)
+        target[at, :] = jnp.transpose(source[:, at])
+
+    each(source.shape[1] // 128, work)
+
+
+def by_rows(work):
+    each(LENGTH // 64, lambda index: work(pl.ds(pl.multiple_of(index * 64, 64), 64)))
+
+
+def forward_heads(pair, qkv, mask, mixed, inverse, attended):
+    chunk = pair // 4
+    lanes = pl.ds(pl.multiple_of((pair % 4) * 128, 128), 128)
+    columns = pl.ds(pl.multiple_of(pair * 128, 128), 128)
+    for part in (0, 1):
+        keys = 256 * (part + 1)
+        rows = slice(part * 256, part * 256 + 256)
+        query = qkv[chunk, rows, lanes]
+        key = qkv[2 + chunk, 0:keys, lanes]
+        value = qkv[4 + chunk, 0:keys, lanes]
+        zero, one = jnp.zeros_like(key), jnp.ones_like(key)
+        total = None
+        for which in (0, 1):
+            mine = head_lanes(which, key.shape)
+            scores = dot_nt(query, jnp.where(mine, key, zero)).astype(jnp.bfloat16)
+            scores = scores * mask[rows, 0:keys]
+            right = jnp.concatenate(
+                [jnp.where(mine, value, zero), jnp.where(mine, one, zero)], axis=1
+            )
+            term = dot(scores, right)
+            total = term if total is None else total + term
+        inverted = 1.0 / total[:, 128:]
+        result = total[:, :128] * inverted
+        mixed[rows, columns] = result
+        inverse[rows, columns] = inverted
+        attended[rows, columns] = result.astype(jnp.bfloat16)
+
+
+def down_rows(dims, buffer, block, half):
+    outer, inner, depth = dims
+    at = (block // (2 * inner), (block // 2) % inner, block % 2)
+    return jnp.concatenate(
+        [
+            buffer[(DOWN + 2 * group + half,) + at + (z,)]
+            for z in range(depth)
+            for group in range(4)
+        ],
+        axis=0,
+    )
+
+
+def feed_block(dims, block, refs):
+    normed, normed_t, grad_out, weights, up_bias, result, grad_normed, to_up, to_down, grad_bias = refs
+    up = matrix(weights, UP + block)
+    upper = dot(normed[...], up) + up_bias[pl.ds(block, 1), :]
+    hidden, slope = gelu_pair(upper)
+    hidden = hidden.astype(jnp.bfloat16)
+    grad_hidden = None
+    for half in (0, 1):
+        columns = slice(half * WIDE, half * WIDE + WIDE)
+        down = down_rows(dims, weights, block, half)
+        result[:, columns] += dot(hidden, down)
+        term = dot_nt(grad_out[:, columns], down)
+        grad_hidden = term if grad_hidden is None else grad_hidden + term
+    grad_upper = (grad_hidden * slope).astype(jnp.bfloat16)
+    grad_bias[pl.ds(block, 1), :] = jnp.sum(
+        grad_upper.astype(jnp.float32), axis=0, keepdims=True
+    )
+    grad_normed[...] += dot_nt(grad_upper, up)
+    to_up[...] = dot(normed_t[...], grad_upper).astype(jnp.bfloat16).reshape(to_up.shape)
+    for half in (0, 1):
+        columns = slice(half * WIDE, half * WIDE + WIDE)
+        term = dot_tn(hidden, grad_out[:, columns]).astype(jnp.bfloat16)
+        for z in range(dims[2]):
+            for group in range(4):
+                start = (z * 4 + group) * UNIT
+                to_down[2 * group + half, z] = term[start : start + UNIT]
+
+
+def forward_kernel(dims, *refs):
+    (
+        tokens,
+        grad_out,
+        crops,
+        kept,
+        gain_one,
+        bias_one,
+        gain_two,
+        bias_two,
+        bias_down,
+        bias_up,
+    ) = refs[:10]
+    shards = refs[10:16]
+    (
+        output,
+        sums,
+        grad_up_bias,
+        rows,
+        qkv_out,
+        mixed_out,
+        inverse_out,
+        attended_t_out,
+        normed_t_out,
+        grad_middle_out,
+        attention_out,
+        terms,
+    ) = refs[16:28]
+    (
+        weights,
+        vectors,
+        up_bias,
+        mask,
+        qkv,
+        mixed,
+        inverse,
+        attended,
+        attended_t,
+        normed,
+        normed_t,
+        middle,
+        normed_two,
+        normed_two_t,
+        result,
+        grad_normed,
+        grad_middle,
+        to_up,
+        to_down,
+        send_sem,
+        recv_sem,
+        vector_send_sem,
+        vector_recv_sem,
+        load_sem,
+        store_sem,
+        up_sem,
+        down_sem,
+    ) = refs[28:]
+    outer, inner, depth = dims
+    devices = 2 * outer * inner * depth
+    place = Place(dims)
+    spot = (place.at["a"], place.at["b"], place.at["c"], place.at["z"])
+    place.greet()
+
+    loads = []
+    for index in range(GATHERED):
+        if index < DOWN:
+            source = shards[index // 2].at[:, pl.ds((index % 2) * WIDE, WIDE)]
+        elif index < UP:
+            group, half = (index - DOWN) // 2, (index - DOWN) % 2
+            source = shards[5].at[pl.ds(group * UNIT, UNIT), pl.ds(half * WIDE, WIDE)]
+        else:
+            source = shards[4].at[:, pl.ds((index - UP) * WIDE, WIDE)]
+        item = pltpu.make_async_copy(source, weights.at[(index,) + spot], load_sem.at[index])
+        item.start()
+        loads.append(item)
+
+    small = Gather(place, vector_send_sem, vector_recv_sem)
+    order = "zbac"
+    lines = [
+        jnp.concatenate([item[...] for item in (gain_one, bias_one, gain_two, bias_two)], axis=1),
+        bias_up[...],
+        jnp.concatenate([bias_down[...], jnp.zeros((1, 128 - UNIT), jnp.bfloat16)], axis=1),
+    ]
+    packed = jnp.concatenate(
+        [line.astype(jnp.float32) for line in lines] + [jnp.zeros((5, 128), jnp.float32)], axis=0
+    )
+    vectors[spot] = packed
+    small.send(vectors, (), order, 0)
+    for item in loads:
+        item.wait()
+    gather_all = Weights(place, weights, send_sem, recv_sem)
+    for index in range(AHEAD):
+        gather_all.begin(index)
+    mask[...] = allowed(crops[...], kept[...])
+    sums[...] = jnp.zeros(sums.shape, jnp.float32)
+    for stage in range(4):
+        small.receive(vectors, (), order, stage)
+        if stage < 3:
+            small.send(vectors, (), order, stage + 1)
+            gather_all.tick(stage)
+    width_rows, up_row = read_vectors(vectors, devices)
+    for index, row in enumerate(width_rows):
+        rows[index : index + 1, :] = row
+    rows[5:8, :] = jnp.zeros((3, WIDTH), jnp.float32)
+    for index in range(8):
+        up_bias[index : index + 1, :] = up_row[:, index * WIDE : (index + 1) * WIDE]
+
+    def first_norm(at):
+        unit, _ = moments(tokens[at, :].astype(jnp.float32))
+        normed[at, :] = (unit * rows[0:1, :] + rows[1:2, :]).astype(jnp.bfloat16)
+
+    by_rows(first_norm)
+    stores = []
+
+    def store(source, target):
+        item = pltpu.make_async_copy(source, target, store_sem.at[len(stores)])
+        item.start()
+        stores.append(item)
+
+    transpose_into(normed, normed_t)
+    store(normed_t, normed_t_out)
+    for now in range(3, 6):
+        gather_all.tick(now)
+
+    def project(index):
+        gather_all.tick(6 + index)
+        value = dot(normed[...], matrix(weights, index))
+        mapped = jnp.where(value > 0, value + 1.0, jnp.exp(jnp.minimum(value, 0.0)))
+        qkv[index] = jnp.where(index < 4, mapped, value).astype(jnp.bfloat16)
+
+    each(6, project)
+    store(qkv, qkv_out)
+
+    def heads(pair):
+        gather_all.tick(12 + pair)
+        forward_heads(pair, qkv, mask, mixed, inverse, attended)
+
+    each(8, heads)
+    store(mixed, mixed_out)
+    store(inverse, inverse_out)
+    store(weights.at[pl.ds(0, DOWN)], attention_out)
+    gather_all.tick(20)
+    for half in (0, 1):
+        columns = slice(half * WIDE, half * WIDE + WIDE)
+        middle[:, columns] = tokens[:, columns].astype(jnp.float32) + dot(
+            attended[...], matrix(weights, 6 + half)
+        )
+    transpose_into(attended, attended_t)
+    store(attended_t, attended_t_out)
+    gather_all.tick(21)
+
+    def second_norm(at):
+        value = middle[at, :]
+        unit, _ = moments(value)
+        normed_two[at, :] = (unit * rows[2:3, :] + rows[3:4, :]).astype(jnp.bfloat16)
+        result[at, :] = value + rows[4:5, :]
+        grad_normed[at, :] = jnp.zeros((64, WIDTH), jnp.float32)
+
+    by_rows(second_norm)
+    transpose_into(normed_two, normed_two_t)
+
+    def leave(block):
+        slot = block % 2
+        owner = (block // (2 * inner), (block // 2) % inner, block % 2)
+        return (
+            pltpu.make_async_copy(to_up.at[slot], terms.at[8 + block], up_sem.at[slot]),
+            pltpu.make_async_copy(
+                to_down.at[slot], terms.at[(pl.ds(0, 8),) + owner], down_sem.at[slot]
+            ),
+        )
+
+    def feed(block):
+        gather_all.tick(22 + block)
+
+        @pl.when(block >= 2)
+        def _():
+            for item in leave(block - 2):
+                item.wait()
+
+        feed_block(
+            dims,
+            block,
+            (
+                normed_two,
+                normed_two_t,
+                grad_out,
+                weights,
+                up_bias,
+                result,
+                grad_normed,
+                to_up.at[block % 2],
+                to_down.at[block % 2],
+                grad_up_bias,
+            ),
+        )
+        for item in leave(block):
+            item.start()
+
+    each(8, feed)
+
+    def close(at):
+        unit, scale = moments(middle[at, :])
+        grad = grad_out[at, :].astype(jnp.float32)
+        value = grad_normed[at, :]
+        output[at, :] = result[at, :].astype(jnp.bfloat16)
+        sums[0:1, :] += jnp.sum(value * unit, axis=0, keepdims=True)
+        sums[1:2, :] += jnp.sum(value, axis=0, keepdims=True)
+        sums[2:3, :] += jnp.sum(grad, axis=0, keepdims=True)
+        scaled = value * rows[2:3, :]
+        grad_middle[at, :] = grad + scale * (
+            scaled
+            - jnp.mean(scaled, axis=-1, keepdims=True)
+            - unit * jnp.mean(scaled * unit, axis=-1, keepdims=True)
+        )
+
+    by_rows(close)
+    store(grad_middle, grad_middle_out)
+    for block in (6, 7):
+        for item in leave(block):
+            item.wait()
+    small.drain(vectors, (), order)
+    gather_all.finish()
+    for item in stores:
+        item.wait()
+
+
+def forward(dims, tokens, cotangent, crops, kept, small, shards):
+    outer, inner, depth = dims
+    most = max(dims) - 1
+    lead = (outer, inner, 2, depth)
+    tile = (UNIT, WIDE)
+    whole = (LENGTH, WIDTH)
+    f32, bf16 = jnp.float32, jnp.bfloat16
+    shape = jax.ShapeDtypeStruct
+    vmem, anywhere = pl.BlockSpec(memory_space=pltpu.VMEM), pl.BlockSpec(memory_space=pl.ANY)
+    return pl.pallas_call(
+        functools.partial(forward_kernel, dims),
+        out_shape=[
+            shape(whole, bf16),
+            shape((8, WIDTH), f32),
+            shape((8, WIDE), f32),
+            shape((8, WIDTH), f32),
+            shape((6, LENGTH, WIDE), bf16),
+            shape(whole, f32),
+            shape(whole, f32),
+            shape((WIDTH, LENGTH), bf16),
+            shape((WIDTH, LENGTH), bf16),
+            shape(whole, f32),
+            shape((DOWN,) + lead + tile, bf16),
+            shape((16,) + lead + tile, bf16),
+        ],
+        in_specs=[vmem] * 10 + [anywhere] * 6,
+        out_specs=[vmem] * 4 + [anywhere] * 8,
+        scratch_shapes=[
+            pltpu.VMEM((GATHERED,) + lead + tile, bf16),
+            pltpu.VMEM(lead + (8, 128), f32),
+            pltpu.VMEM((8, WIDE), f32),
+            pltpu.VMEM((LENGTH, LENGTH), bf16),
+            pltpu.VMEM((6, LENGTH, WIDE), bf16),
+            pltpu.VMEM(whole, f32),
+            pltpu.VMEM(whole, f32),
+            pltpu.VMEM(whole, bf16),
+            pltpu.VMEM((WIDTH, LENGTH), bf16),
+            pltpu.VMEM(whole, bf16),
+            pltpu.VMEM((WIDTH, LENGTH), bf16),
+            pltpu.VMEM(whole, f32),
+            pltpu.VMEM(whole, bf16),
+            pltpu.VMEM((WIDTH, LENGTH), bf16),
+            pltpu.VMEM(whole, f32),
+            pltpu.VMEM(whole, f32),
+            pltpu.VMEM(whole, f32),
+            pltpu.VMEM((2,) + lead + tile, bf16),
+            pltpu.VMEM((2, 8, depth) + tile, bf16),
+            pltpu.SemaphoreType.DMA((GATHERED, 4, most)),
+            pltpu.SemaphoreType.DMA((GATHERED, 4, most)),
+            pltpu.SemaphoreType.DMA((4, most)),
+            pltpu.SemaphoreType.DMA((4, most)),
+            pltpu.SemaphoreType.DMA((GATHERED,)),
+            pltpu.SemaphoreType.DMA((8,)),
+            pltpu.SemaphoreType.DMA((2,)),
+            pltpu.SemaphoreType.DMA((2,)),
+        ],
+        compiler_params=pltpu.CompilerParams(
+            collective_id=0, has_side_effects=True, vmem_limit_bytes=VMEM_LIMIT
+        ),
+        name="forward",
+    )(tokens, cotangent, crops, kept, *small, *shards)
+
+
+class Sums(Mover):
+    def start(self, lead, stage, step, axis, source, target):
+        self.copy(lead, stage, step, axis, source, target).start()
+
+    def await_all(self, lead, stage, axis, room):
+        for step in self.place.partners(axis):
+            self.copy(lead, stage, step, axis, room.at[step - 1], room.at[step - 1]).wait_recv()
+
+    @staticmethod
+    def pick(order, first, second):
+        return (first, second) if order == "ab" else (second, first)
+
+    def after_core(self, lead, order, own, other, came):
+        place = self.place
+        axis, rest = order
+
+        def add(where):
+            for item in range(place.size[rest]):
+                at = self.pick(order, where, item)
+                other[at] = own[at] + other[at]
+
+        for step in place.partners(axis):
+            where = place.moved(axis, step)[axis]
+            add(where)
+            source = other.at[where] if order == "ab" else other.at[:, where]
+            self.start(lead, 1, step, axis, source, came.at[step - 1])
+        add(place.at[axis])
+
+    def after_first(self, lead, order, total, came, later):
+        place = self.place
+        axis, rest = order
+        self.await_all(lead, 1, axis, came)
+
+        def add(where):
+            at = self.pick(order, place.at[axis], where)
+            value = total[at].astype(jnp.float32)
+            for step in place.partners(axis):
+                value = value + came[step - 1, where].astype(jnp.float32)
+            total[at] = value.astype(total.dtype)
+
+        for step in place.partners(rest):
+            where = place.moved(rest, step)[rest]
+            add(where)
+            at = self.pick(order, place.at[axis], where)
+            self.start(lead, 2, step, rest, total.at[at], later.at[step - 1])
+        add(place.at[rest])
+
+    def after_second(self, lead, order, total, later, last):
+        place = self.place
+        rest = order[1]
+        a, b = place.at["a"], place.at["b"]
+        self.await_all(lead, 2, rest, later)
+
+        def add(where):
+            value = total[a, b, where].astype(jnp.float32)
+            for step in place.partners(rest):
+                value = value + later[step - 1, where].astype(jnp.float32)
+            return value
+
+        for step in place.partners("z"):
+            where = place.moved("z", step)["z"]
+            total[a, b, where] = add(where).astype(total.dtype)
+            self.start(lead, 3, step, "z", total.at[a, b, where], last.at[step - 1])
+        return add(place.at["z"])
+
+    def after_last(self, lead, value, last):
+        self.await_all(lead, 3, "z", last)
+        for step in self.place.partners("z"):
+            value = value + last[step - 1].astype(jnp.float32)
+        return value
+
+    def drain(self, lead, order, total, came, later, last):
+        place = self.place
+        axis, rest = order
+        self.copy(lead, 0, 1, "c", total, total).wait_send()
+        for step in place.partners(axis):
+            self.copy(lead, 1, step, axis, came.at[step - 1], came.at[step - 1]).wait_send()
+        for step in place.partners(rest):
+            self.copy(lead, 2, step, rest, later.at[step - 1], later.at[step - 1]).wait_send()
+        for step in place.partners("z"):
+            self.copy(lead, 3, step, "z", last.at[step - 1], last.at[step - 1]).wait_send()
+
+
+class Gradients(Sums):
+    def __init__(self, place, terms, rooms, results, ring, ring_sem, send_sem, recv_sem):
+        super().__init__(place, send_sem, recv_sem)
+        self.terms, self.rooms, self.results = terms, rooms, results
+        self.ring, self.ring_sem = ring, ring_sem
+        self.total = results.shape[0]
+        self.first = terms[0].shape[0]
+
+    def by_order(self, index, work):
+        half = index // 2
+        total, ones, others, twos, fours, last = self.rooms
+
+        @when(index % 2 == 0)
+        def _():
+            work("ab", total.at[index], ones.at[half], twos.at[half], last.at[index])
+
+        @when(index % 2 == 1)
+        def _():
+            work("ba", total.at[index], others.at[half], fours.at[half], last.at[index])
+
+    def begin(self, index):
+        side = self.place.at["c"]
+        slot = index % (AHEAD + 1)
+
+        def go(source):
+            self.start((index,), 0, 1, "c", source.at[:, :, 1 - side], self.rooms[0].at[index])
+            pltpu.make_async_copy(
+                source.at[:, :, side], self.ring.at[slot], self.ring_sem.at[slot]
+            ).start()
+
+        @when(index < self.first)
+        def _():
+            go(self.terms[0].at[index])
+
+        @when((index >= self.first) & (index < self.total))
+        def _():
+            go(self.terms[1].at[index - self.first])
+
+    def tick(self, now):
+        self.begin(now + AHEAD)
+
+        def live(index):
+            return (index >= 0) & (index < self.total)
+
+        @when(live(now))
+        def _():
+            slot = now % (AHEAD + 1)
+            room = self.ring.at[slot]
+            pltpu.make_async_copy(room, room, self.ring_sem.at[slot]).wait()
+            total = self.rooms[0].at[now]
+            self.copy((now,), 0, 1, "c", total, total).wait_recv()
+            self.by_order(
+                now,
+                lambda order, total, came, later, last: self.after_core(
+                    (now,), order, room, total, came
+                ),
+            )
+
+        second = now - LAG
+
+        @when(live(second))
+        def _():
+            self.by_order(
+                second,
+                lambda order, total, came, later, last: self.after_first(
+                    (second,), order, total, came, later
+                ),
+            )
+
+        third = now - 2 * LAG
+
+        @when(live(third))
+        def _():
+            def work(order, total, came, later, last):
+                self.results[third] = self.after_second((third,), order, total, later, last)
+
+            self.by_order(third, work)
+
+        fourth = now - 3 * LAG
+
+        @when(live(fourth))
+        def _():
+            self.results[fourth] = self.after_last(
+                (fourth,), self.results[fourth], self.rooms[5].at[fourth]
+            )
+
+    def finish(self):
+        def work(index):
+            self.by_order(
+                index,
+                lambda order, total, came, later, last: self.drain(
+                    (index,), order, total, came, later, last
+                ),
+            )
+
+        each(self.total, work)
+
+
+def backward_heads(pair, qkv, mask, mask_t, mixed, inverse, grad_mixed):
+    chunk = pair // 4
+    lanes = pl.ds(pl.multiple_of((pair % 4) * 128, 128), 128)
+    columns = pl.ds(pl.multiple_of(pair * 128, 128), 128)
+    query = qkv[chunk, :, lanes]
+    key = qkv[2 + chunk, :, lanes]
+    value = qkv[4 + chunk, :, lanes]
+    grad_numer = (grad_mixed[:, columns] * inverse[:, columns]).astype(jnp.bfloat16)
+    part = grad_numer.astype(jnp.float32) * mixed[:, columns]
+    high = part.astype(jnp.bfloat16)
+    low = pltpu.roll(part - high.astype(jnp.float32), 64, 1).astype(jnp.bfloat16)
+    zero, minus = jnp.zeros_like(query), jnp.full_like(query, -1.0)
+    heads = []
+    for which in (0, 1):
+        mine = head_lanes(which, query.shape)
+        heads.append(
+            (
+                jnp.concatenate([grad_numer, jnp.where(mine, high, low)], axis=1),
+                jnp.concatenate([jnp.where(mine, value, zero), minus], axis=1),
+                jnp.where(mine, query, zero),
+                jnp.where(mine, key, zero),
+                jnp.where(mine, grad_numer, zero),
+            )
+        )
+    for part in (0, 1):
+        keys = 256 * (part + 1)
+        rows = slice(part * 256, part * 256 + 256)
+        total = None
+        for left, right, _, own_key, _ in heads:
+            grad_scores = dot_nt(left[rows], right[:keys]).astype(jnp.bfloat16)
+            term = dot(grad_scores * mask[rows, 0:keys], own_key[:keys])
+            total = term if total is None else total + term
+        slope = jnp.minimum(query[rows].astype(jnp.float32), 1.0)
+        qkv[chunk, rows, lanes] = (total * slope).astype(jnp.bfloat16)
+    for part in (0, 1):
+        start = part * 256
+        rows = slice(start, start + 256)
+        grad_key = grad_value = None
+        for left, right, own_query, own_key, own_grad in heads:
+            seen = mask_t[rows, start:LENGTH]
+            scores = dot_nt(own_key[rows], query[start:]).astype(jnp.bfloat16) * seen
+            grad_scores = dot_nt(right[rows], left[start:]).astype(jnp.bfloat16) * seen
+            term = dot(scores, own_grad[start:])
+            grad_value = term if grad_value is None else grad_value + term
+            term = dot(grad_scores, own_query[start:])
+            grad_key = term if grad_key is None else grad_key + term
+        slope = jnp.minimum(key[rows].astype(jnp.float32), 1.0)
+        qkv[2 + chunk, rows, lanes] = (grad_key * slope).astype(jnp.bfloat16)
+        qkv[4 + chunk, rows, lanes] = grad_value.astype(jnp.bfloat16)
+
+
+def backward_kernel(dims, *refs):
+    tokens, crops, kept, sums_in, grad_up_bias, rows = refs[:6]
+    qkv_in, mixed_in, inverse_in, attended_t_in, normed_t_in, grad_middle_in = refs[6:12]
+    attention_in, terms = refs[12:14]
+    input_grad, owned, owned_small, attention_terms = refs[14:18]
+    (
+        weights,
+        mask,
+        mask_t,
+        grad_attended,
+        grad_mixed,
+        qkv,
+        turned,
+        mixed,
+        inverse,
+        grad_middle,
+        sums,
+        staged,
+        small,
+        ring,
+        total,
+        ones,
+        others,
+        twos,
+        fours,
+        last,
+        side_other,
+        side_came,
+        side_later,
+        side_last,
+        load_sem,
+        stage_sem,
+        ring_sem,
+        send_sem,
+        recv_sem,
+        side_send_sem,
+        side_recv_sem,
+    ) = refs[18:]
+    outer, inner, depth = dims
+    devices = 2 * outer * inner * depth
+    place = Place(dims)
+    spot = place.at
+    place.greet()
+    adder = Gradients(
+        place,
+        (terms, attention_terms),
+        (total, ones, others, twos, fours, last),
+        owned,
+        ring,
+        ring_sem,
+        send_sem,
+        recv_sem,
+    )
+    for index in range(AHEAD):
+        adder.begin(index)
+    loads = {}
+
+    def load(name, source, target):
+        item = pltpu.make_async_copy(source, target, load_sem.at[len(loads)])
+        item.start()
+        loads[name] = item
+
+    load("grad_middle", grad_middle_in, grad_middle)
+    load("out", attention_in.at[pl.ds(6, 2)], weights.at[pl.ds(6, 2)])
+    load("attended", attended_t_in, turned.at[0])
+    load("qkv", qkv_in, qkv)
+    load("mixed", mixed_in, mixed)
+    load("inverse", inverse_in, inverse)
+    load("normed", normed_t_in, turned.at[1])
+    load("rest", attention_in.at[pl.ds(0, 6)], weights.at[pl.ds(0, 6)])
+    mask[...] = allowed(crops[...], kept[...])
+    mask_t[...] = allowed_back(crops[...], kept[...])
+    sums[...] = sums_in[...]
+    loads["grad_middle"].wait()
+
+    def round_rows(at):
+        grad_attended[at, :] = grad_middle[at, :].astype(jnp.bfloat16)
+
+    by_rows(round_rows)
+    adder.tick(0)
+    loads["out"].wait()
+    grad_mixed[...] = dot_nt(grad_attended[:, 0:WIDE], matrix(weights, 6)) + dot_nt(
+        grad_attended[:, WIDE:WIDTH], matrix(weights, 7)
+    )
+    adder.tick(1)
+    loads["attended"].wait()
+    for half in (0, 1):
+        columns = slice(half * WIDE, half * WIDE + WIDE)
+        value = dot(turned[0], grad_attended[:, columns]).astype(jnp.bfloat16)
+        staged[half] = value.reshape(staged.shape[1:])
+        pltpu.make_async_copy(
+            staged.at[half], attention_terms.at[half], stage_sem.at[half]
+        ).start()
+    for name in ("qkv", "mixed", "inverse"):
+        loads[name].wait()
+
+    def heads(pair):
+        adder.tick(2 + pair)
+        backward_heads(pair, qkv, mask, mask_t, mixed, inverse, grad_mixed)
+
+    each(8, heads)
+    loads["normed"].wait()
+    loads["rest"].wait()
+    grad_normed = grad_mixed
+    grad_normed[...] = jnp.zeros(grad_normed.shape, jnp.float32)
+
+    def stage_copy(index):
+        slot = index % 2
+        return pltpu.make_async_copy(
+            staged.at[slot], attention_terms.at[2 + index], stage_sem.at[slot]
+        )
+
+    def project(index):
+        pltpu.make_async_copy(
+            staged.at[index % 2], staged.at[index % 2], stage_sem.at[index % 2]
+        ).wait()
+        adder.tick(10 + index)
+        value = dot(turned[1], qkv[index]).astype(jnp.bfloat16)
+        staged[index % 2] = value.reshape(staged.shape[1:])
+        stage_copy(index).start()
+        grad_normed[...] += dot_nt(qkv[index], matrix(weights, index))
+
+    each(4, project)
+    for index in (4, 5):
+        slot = index % 2
+        stage_copy(index - 2).wait()
+        value = dot(turned[1], qkv[index]).astype(jnp.bfloat16)
+        staged[slot] = value.reshape(staged.shape[1:])
+        stage_copy(index).start()
+        grad_normed[...] += dot_nt(qkv[index], matrix(weights, index))
+        adder.tick(10 + index)
+    for index in (4, 5):
+        stage_copy(index).wait()
+    adder.tick(16)
+
+    def close(at):
+        unit, scale = moments(tokens[at, :].astype(jnp.float32))
+        value = grad_normed[at, :]
+        sums[3:4, :] += jnp.sum(value * unit, axis=0, keepdims=True)
+        sums[4:5, :] += jnp.sum(value, axis=0, keepdims=True)
+        scaled = value * rows[0:1, :]
+        input_grad[at, :] = (
+            grad_middle[at, :]
+            + scale
+            * (
+                scaled
+                - jnp.mean(scaled, axis=-1, keepdims=True)
+                - unit * jnp.mean(scaled * unit, axis=-1, keepdims=True)
+            )
+        ).astype(jnp.bfloat16)
+
+    by_rows(close)
+    order = [sums[index : index + 1, :] for index in (3, 4, 0, 1)]
+    first = write_vectors(order, devices)
+    third = write_vectors([sums[2:3, :]], devices)
+    for device in range(devices):
+        at = (
+            device // (2 * inner * depth),
+            (device // (2 * depth)) % inner,
+            (device // depth) % 2,
+            device % depth,
+        )
+        block, lane = device // 4, (device % 4) * 128
+        small[at + (slice(0, 1),)] = first[device : device + 1, :]
+        small[at + (slice(1, 2),)] = grad_up_bias[block : block + 1, lane : lane + 128]
+        small[at + (slice(2, 3),)] = third[device : device + 1, :]
+        small[at + (slice(3, 8),)] = jnp.zeros((5, 128), jnp.float32)
+    side = Sums(place, side_send_sem, side_recv_sem)
+    side.start((), 0, 1, "c", small.at[:, :, 1 - spot["c"]], side_other)
+    adder.tick(17)
+    side.copy((), 0, 1, "c", side_other, side_other).wait_recv()
+    side.after_core((), "ab", small.at[:, :, spot["c"]], side_other, side_came)
+    adder.tick(18)
+    side.after_first((), "ab", side_other, side_came, side_later)
+    adder.tick(19)
+    owned_small[...] = side.after_second((), "ab", side_other, side_later, side_last)
+    adder.tick(20)
+    owned_small[...] = side.after_last((), owned_small[...], side_last)
+    each(GATHERED + 3 * LAG - 21, lambda index: adder.tick(21 + index))
+    side.drain((), "ab", side_other, side_came, side_later, side_last)
+    adder.finish()
+
+
+def backward(dims, tokens, crops, kept, sums, grad_up_bias, rows, kept_values, terms):
+    outer, inner, depth = dims
+    most = max(dims) - 1
+    lead = (outer, inner, 2, depth)
+    tile = (UNIT, WIDE)
+    whole = (LENGTH, WIDTH)
+    f32, bf16 = jnp.float32, jnp.bfloat16
+    shape = jax.ShapeDtypeStruct
+    vmem, anywhere = pl.BlockSpec(memory_space=pltpu.VMEM), pl.BlockSpec(memory_space=pl.ANY)
+    half = GATHERED // 2
+    chip = (outer, inner, depth)
+    small_tile = (8, 128)
+    return pl.pallas_call(
+        functools.partial(backward_kernel, dims),
+        out_shape=[
+            shape(whole, bf16),
+            shape((GATHERED,) + tile, f32),
+            shape(small_tile, f32),
+            shape((8,) + lead + tile, bf16),
+        ],
+        in_specs=[vmem] * 6 + [anywhere] * 8,
+        out_specs=[vmem] * 3 + [anywhere],
+        scratch_shapes=[
+            pltpu.VMEM((8,) + lead + tile, bf16),
+            pltpu.VMEM((LENGTH, LENGTH), bf16),
+            pltpu.VMEM((LENGTH, LENGTH), bf16),
+            pltpu.VMEM(whole, bf16),
+            pltpu.VMEM(whole, f32),
+            pltpu.VMEM((6, LENGTH, WIDE), bf16),
+            pltpu.VMEM((2, WIDTH, LENGTH), bf16),
+            pltpu.VMEM(whole, f32),
+            pltpu.VMEM(whole, f32),
+            pltpu.VMEM(whole, f32),
+            pltpu.VMEM((8, WIDTH), f32),
+            pltpu.VMEM((2,) + lead + tile, bf16),
+            pltpu.VMEM(lead + small_tile, f32),
+            pltpu.VMEM((AHEAD + 1,) + chip + tile, bf16),
+            pltpu.VMEM((GATHERED,) + chip + tile, bf16),
+            pltpu.VMEM((half, outer - 1, inner, depth) + tile, bf16),
+            pltpu.VMEM((half, inner - 1, outer, depth) + tile, bf16),
+            pltpu.VMEM((half, inner - 1, depth) + tile, bf16),
+            pltpu.VMEM((half, outer - 1, depth) + tile, bf16),
+            pltpu.VMEM((GATHERED, depth - 1) + tile, bf16),
+            pltpu.VMEM(chip + small_tile, f32),
+            pltpu.VMEM((outer - 1, inner, depth) + small_tile, f32),
+            pltpu.VMEM((inner - 1, depth) + small_tile, f32),
+            pltpu.VMEM((depth - 1,) + small_tile, f32),
+            pltpu.SemaphoreType.DMA((8,)),
+            pltpu.SemaphoreType.DMA((2,)),
+            pltpu.SemaphoreType.DMA((AHEAD + 1,)),
+            pltpu.SemaphoreType.DMA((GATHERED, 4, most)),
+            pltpu.SemaphoreType.DMA((GATHERED, 4, most)),
+            pltpu.SemaphoreType.DMA((4, most)),
+            pltpu.SemaphoreType.DMA((4, most)),
+        ],
+        compiler_params=pltpu.CompilerParams(
+            collective_id=1, has_side_effects=True, vmem_limit_bytes=VMEM_LIMIT
+        ),
+        name="backward",
+    )(tokens, crops, kept, sums, grad_up_bias, rows, *kept_values, terms)
+
+
+def body(
+    tokens,
+    crop_ids,
+    kv_mask,
+    norm1_gain,
+    norm1_bias,
+    w_query,
+    w_key,
+    w_value,
+    w_out,
+    norm2_gain,
+    norm2_bias,
+    w_up,
+    up_bias,
+    w_down,
+    down_bias,
+    cotangent,
+):
+    inner = lax.axis_size("dp") // (2 * OUTER)
+    dims = (OUTER, inner, lax.axis_size("fsdp"))
+    fits = (
+        tokens.shape == (1, LENGTH, WIDTH)
+        and w_up.shape == (UNIT, HIDDEN)
+        and w_down.shape == (HIDDEN // WIDTH * UNIT, WIDTH)
+        and dims[2] * 4 * UNIT == WIDE
+    )
+    if not fits:
+        return general_body(
+            tokens,
+            crop_ids,
+            kv_mask,
+            norm1_gain,
+            norm1_bias,
+            w_query,
+            w_key,
+            w_value,
+            w_out,
+            norm2_gain,
+            norm2_bias,
+            w_up,
+            up_bias,
+            w_down,
+            down_bias,
+            cotangent,
+        )
+    small = [
+        vector.reshape(1, -1)
+        for vector in (norm1_gain, norm1_bias, norm2_gain, norm2_bias, down_bias, up_bias)
+    ]
+    pixels = tokens.reshape(LENGTH, WIDTH)
+    (output, sums, grad_up, rows, qkv, mixed, inverse, attended_t, normed_t, grad_middle, attention, terms) = (
+        forward(
+            dims,
+            pixels,
+            cotangent.reshape(LENGTH, WIDTH),
+            crop_ids,
+            kv_mask,
+            small,
+            (w_query, w_key, w_value, w_out, w_up, w_down),
+        )
+    )
+    input_grad, owned, owned_small, _ = backward(
+        dims,
+        pixels,
+        crop_ids,
+        kv_mask,
+        sums,
+        grad_up,
+        rows,
+        (qkv, mixed, inverse, attended_t, normed_t, grad_middle, attention),
+        terms,
+    )
+
+    def side_by_side(start, count):
+        return owned[start : start + count].transpose(1, 0, 2).reshape(UNIT, count * WIDE)
+
+    own_down = owned[0:8].reshape(4, 2, UNIT, WIDE).transpose(0, 2, 1, 3).reshape(4 * UNIT, WIDTH)
+    own_up = side_by_side(8, 8)
+    own_out, own_query, own_key, own_value = (side_by_side(16 + 2 * index, 2) for index in range(4))
+    gain_one, bias_one, gain_two, bias_two = (
+        owned_small[0, index * UNIT : (index + 1) * UNIT] for index in range(4)
+    )
+    return (
+        output.reshape(tokens.shape),
+        input_grad.reshape(tokens.shape),
+        gain_one,
+        bias_one,
+        own_query,
+        own_key,
+        own_value,
+        own_out,
+        gain_two,
+        bias_two,
+        own_up,
+        owned_small[1],
+        own_down,
+        owned_small[2, :UNIT],
     )
 
 

time: 506 us -> 285 us (0.56)
  matrix products: 197 us -> 0 us
  local copies, waits for them, and re-layouts: 36.4 us -> 11.8 us
  Pallas kernels: 248 us -> 272 us
  other arithmetic: 18.1 us -> 0 us
    dot_general x29 -> x0, matrix products: 197 us -> none  [the longest x1 28 us: body(): jnp.dot(normed_two, full_up, preferred_element_type=jnp.float32)]
    pallas_call x2, Pallas kernels: 248 us -> 272 us  [the longest x1 145 us: forward(): pl.pallas_call(functools.partial(forward_kernel, dims), out_shape=[shape(...]
    unnamed x77 -> x8, local copies, waits for them, and re-layouts: 16.6 us -> 3.97 us
    convert_element_type x7 -> x0, other arithmetic: 8.76 us -> none  [the longest x1 3.02 us: body(): pull_query(grad_query_feat.reshape(count, width))[0].astype(jnp.bfloat16)]
    reduce_sum x6 -> x0, other arithmetic: 8.57 us -> none  [the longest x1 2.11 us: body(): grad_down_bias = jnp.sum(grad_out.astype(jnp.float32), axis=0)]
    convert_element_type x8 -> x0, local copies, waits for them, and re-layouts: 6.86 us -> none  [the longest x1 2.31 us: body(): query_wide.astype(jnp.bfloat16).reshape(slots, length, heads, head_width)]
where the time goes in v2:
time: 285 us
  Pallas kernels  272 us (95%)
  local copies, waits for them, and re-layouts  11.8 us (4%)
    pallas_call x1, Pallas kernels, forward(): pl.pallas_call(functools.partial(forward_kernel, dims), out_shape=[shape(...  145 us
    pallas_call x1, Pallas kernels, backward(): pl.pallas_call(functools.partial(backward_kernel, dims), out_shape=[shape...  127 us

profile of v2, /device:TPU:0, one launch (start us, length us, event | category | flops | bytes accessed | tf_op | source)
XLA Modules:
  0.0 284.8 jit_solution(4027671557218050848)
XLA Ops:
  0.7 145.3 %forward.1 = (bf16[512,1024]{1,0:T(8,128)(2,1)}, f32[8,1024]{1,0:T(8,128)}, f32[8,512]{1,0:T(8,128)}, f32[8,1024]{1,0:T(8,128)}, bf16[6,512,512]{2,1,0:T(8,128)(...) custom-call(bf16[512,1024]{1,0:T(8,128)(2,1)} %bitcast.48, ...), custom_call_target="tpu_custom_call" | custom-call | tf_op jit(solution)/shard_map/forward/pallas_call | solution.py:1203
  145.9 127.0 %backward.1 = (bf16[512,1024]{1,0:T(8,128)(2,1)}, f32[24,32,512]{2,1,0:T(8,128)}, f32[8,128]{1,0:T(8,128)}, bf16[8,2,2,2,4,32,512]{6,5,4,3,2,1,0:T(8,128)(2,1)}) custom-call(bf16[512,1024]{1,0:T(8,128)(2,1)} %bitcast.49, s32[1,512]{1,0:T(1,128)} %refs_1_.1, s32[1,512]{1,0:T(1,128)} %refs_2_.3, f32[8,1024]{1,0:T(8,128)} %get-tuple-element.30.refs_3_, ...), custom_call_target="tpu_custom_call" | custom-call | tf_op jit(solution)/shard_map/backward/pallas_call | solution.py:1684
  272.9 1.2 slice_bitcast_fusion.6
  274.1 1.5 slice_bitcast_fusion.5
  275.6 1.1 slice_bitcast_fusion.1
  276.7 1.3 fusion
  278.0 0.0 copy-start
  278.0 0.4 copy.36
  278.4 0.9 copy.42
  279.3 0.0 copy-start.1
  279.3 0.7 copy.40
  280.0 0.7 copy.39
  280.6 0.7 copy.38
  281.3 0.7 copy.37
  282.0 0.8 copy.41
  282.8 0.0 copy-done
  282.8 1.0 copy.45
  283.8 0.0 copy-done.1
  283.8 1.0 copy.46
Async XLA Ops:
  278.0 4.8 %copy-start = (bf16[512,1024]{1,0:T(8,128)(2,1)S(1)}, bf16[512,1024]{1,0:T(8,128)(2,1)}, u32[]{:S(2)}) copy-start(bf16[512,1024]{1,0:T(8,128)(2,1)} %get-tuple-element.29) | copy-start | bytes 3145732
  279.3 4.5 %copy-start.1 = (bf16[512,1024]{1,0:T(8,128)(2,1)S(1)}, bf16[512,1024]{1,0:T(8,128)(2,1)}, u32[]{:S(2)}) copy-start(bf16[512,1024]{1,0:T(8,128)(2,1)} %get-tuple-element.41) | copy-start | bytes 3145732

commit v3 on v2

--- a/solution.py
+++ b/solution.py
@@ -1,4 +1,5 @@
 import functools
+import itertools
 
 import jax
 import jax.numpy as jnp
@@ -710,6 +711,19 @@
     )
 
 
+def by_order(place, orders, index, work):
+    turn = (index + 3 * place.at["c"]) % len(orders)
+    for order in dict.fromkeys(orders):
+        turns = [number for number, item in enumerate(orders) if item == order]
+        match = turn == turns[0]
+        for number in turns[1:]:
+            match = match | (turn == number)
+
+        @pl.when(match)
+        def _(order=order):
+            work(order)
+
+
 class Mover:
     def __init__(self, place, send_sem, recv_sem):
         self.place, self.send_sem, self.recv_sem = place, send_sem, recv_sem
@@ -753,23 +767,21 @@
 
 
 class Weights(Gather):
-    orders = ("zbac", "zabc")
+    orders = ("zbac", "zabc", "bzac", "zbac", "zabc", "azbc")
 
     def __init__(self, place, buffer, send_sem, recv_sem):
         super().__init__(place, send_sem, recv_sem)
         self.buffer, self.total = buffer, buffer.shape[0]
 
     def by_order(self, index, work):
-        for parity, order in enumerate(self.orders):
-
-            @when(index % 2 == parity)
-            def _(order=order):
-                work(order)
+        by_order(self.place, self.orders, index, work)
 
     def begin(self, index):
         @when(index < self.total)
         def _():
-            self.send(self.buffer.at[index], (index,), self.orders[0], 0)
+            self.by_order(
+                index, lambda order: self.send(self.buffer.at[index], (index,), order, 0)
+            )
 
     def tick(self, now):
         self.begin(now + AHEAD)
@@ -967,8 +979,6 @@
 
 def forward_kernel(dims, *refs):
     (
-        tokens,
-        grad_out,
         crops,
         kept,
         gain_one,
@@ -977,11 +987,11 @@
         bias_two,
         bias_down,
         bias_up,
+        tokens_in,
+        grad_out_in,
     ) = refs[:10]
     shards = refs[10:16]
     (
-        output,
-        sums,
         grad_up_bias,
         rows,
         qkv_out,
@@ -989,11 +999,15 @@
         inverse_out,
         attended_t_out,
         normed_t_out,
-        grad_middle_out,
+        middle_out,
+        result_out,
+        grad_normed_out,
         attention_out,
         terms,
     ) = refs[16:28]
     (
+        tokens,
+        grad_out,
         weights,
         vectors,
         up_bias,
@@ -1010,7 +1024,6 @@
         normed_two_t,
         result,
         grad_normed,
-        grad_middle,
         to_up,
         to_down,
         send_sem,
@@ -1026,7 +1039,6 @@
     devices = 2 * outer * inner * depth
     place = Place(dims)
     spot = (place.at["a"], place.at["b"], place.at["c"], place.at["z"])
-    place.greet()
 
     loads = []
     for index in range(GATHERED):
@@ -1040,6 +1052,10 @@
         item = pltpu.make_async_copy(source, weights.at[(index,) + spot], load_sem.at[index])
         item.start()
         loads.append(item)
+    for index, (source, target) in enumerate(((tokens_in, tokens), (grad_out_in, grad_out))):
+        item = pltpu.make_async_copy(source, target, load_sem.at[GATHERED + index])
+        item.start()
+        loads.append(item)
 
     small = Gather(place, vector_send_sem, vector_recv_sem)
     order = "zbac"
@@ -1052,14 +1068,15 @@
         [line.astype(jnp.float32) for line in lines] + [jnp.zeros((5, 128), jnp.float32)], axis=0
     )
     vectors[spot] = packed
+    place.greet()
     small.send(vectors, (), order, 0)
-    for item in loads:
-        item.wait()
     gather_all = Weights(place, weights, send_sem, recv_sem)
     for index in range(AHEAD):
+        loads[index].wait()
         gather_all.begin(index)
+    for item in loads[AHEAD:]:
+        item.wait()
     mask[...] = allowed(crops[...], kept[...])
-    sums[...] = jnp.zeros(sums.shape, jnp.float32)
     for stage in range(4):
         small.receive(vectors, (), order, stage)
         if stage < 3:
@@ -1124,6 +1141,7 @@
         grad_normed[at, :] = jnp.zeros((64, WIDTH), jnp.float32)
 
     by_rows(second_norm)
+    store(middle, middle_out)
     transpose_into(normed_two, normed_two_t)
 
     def leave(block):
@@ -1165,23 +1183,8 @@
 
     each(8, feed)
 
-    def close(at):
-        unit, scale = moments(middle[at, :])
-        grad = grad_out[at, :].astype(jnp.float32)
-        value = grad_normed[at, :]
-        output[at, :] = result[at, :].astype(jnp.bfloat16)
-        sums[0:1, :] += jnp.sum(value * unit, axis=0, keepdims=True)
-        sums[1:2, :] += jnp.sum(value, axis=0, keepdims=True)
-        sums[2:3, :] += jnp.sum(grad, axis=0, keepdims=True)
-        scaled = value * rows[2:3, :]
-        grad_middle[at, :] = grad + scale * (
-            scaled
-            - jnp.mean(scaled, axis=-1, keepdims=True)
-            - unit * jnp.mean(scaled * unit, axis=-1, keepdims=True)
-        )
-
-    by_rows(close)
-    store(grad_middle, grad_middle_out)
+    store(result, result_out)
+    store(grad_normed, grad_normed_out)
     for block in (6, 7):
         for item in leave(block):
             item.wait()
@@ -1203,8 +1206,6 @@
     return pl.pallas_call(
         functools.partial(forward_kernel, dims),
         out_shape=[
-            shape(whole, bf16),
-            shape((8, WIDTH), f32),
             shape((8, WIDE), f32),
             shape((8, WIDTH), f32),
             shape((6, LENGTH, WIDE), bf16),
@@ -1213,12 +1214,16 @@
             shape((WIDTH, LENGTH), bf16),
             shape((WIDTH, LENGTH), bf16),
             shape(whole, f32),
+            shape(whole, f32),
+            shape(whole, f32),
             shape((DOWN,) + lead + tile, bf16),
             shape((16,) + lead + tile, bf16),
         ],
-        in_specs=[vmem] * 10 + [anywhere] * 6,
-        out_specs=[vmem] * 4 + [anywhere] * 8,
+        in_specs=[vmem] * 8 + [anywhere] * 8,
+        out_specs=[vmem] * 2 + [anywhere] * 10,
         scratch_shapes=[
+            pltpu.VMEM(whole, bf16),
+            pltpu.VMEM(whole, bf16),
             pltpu.VMEM((GATHERED,) + lead + tile, bf16),
             pltpu.VMEM(lead + (8, 128), f32),
             pltpu.VMEM((8, WIDE), f32),
@@ -1235,15 +1240,14 @@
             pltpu.VMEM((WIDTH, LENGTH), bf16),
             pltpu.VMEM(whole, f32),
             pltpu.VMEM(whole, f32),
-            pltpu.VMEM(whole, f32),
             pltpu.VMEM((2,) + lead + tile, bf16),
             pltpu.VMEM((2, 8, depth) + tile, bf16),
             pltpu.SemaphoreType.DMA((GATHERED, 4, most)),
             pltpu.SemaphoreType.DMA((GATHERED, 4, most)),
             pltpu.SemaphoreType.DMA((4, most)),
             pltpu.SemaphoreType.DMA((4, most)),
-            pltpu.SemaphoreType.DMA((GATHERED,)),
-            pltpu.SemaphoreType.DMA((8,)),
+            pltpu.SemaphoreType.DMA((GATHERED + 2,)),
+            pltpu.SemaphoreType.DMA((9,)),
             pltpu.SemaphoreType.DMA((2,)),
             pltpu.SemaphoreType.DMA((2,)),
         ],
@@ -1251,118 +1255,113 @@
             collective_id=0, has_side_effects=True, vmem_limit_bytes=VMEM_LIMIT
         ),
         name="forward",
-    )(tokens, cotangent, crops, kept, *small, *shards)
+    )(crops, kept, *small, tokens, cotangent, *shards)
 
 
 class Sums(Mover):
     def start(self, lead, stage, step, axis, source, target):
         self.copy(lead, stage, step, axis, source, target).start()
 
-    def await_all(self, lead, stage, axis, room):
+    def region(self, order, stage, where):
+        at = {axis: self.place.at[axis] for axis in order[:stage]}
+        at[order[stage]] = where
+        return tuple(at.get(axis, slice(None)) for axis in "abz")
+
+    def blocks(self, order, stage, where):
+        rest = [axis for axis in "abz" if axis in order[stage + 1 :]]
+        base = self.region(order, stage, where)
+        sizes = [self.place.size[axis] for axis in rest]
+        for inner in itertools.product(*(range(size) for size in sizes)):
+            place = dict(zip(rest, inner))
+            yield (
+                tuple(place.get(axis, item) for axis, item in zip("abz", base)),
+                inner,
+            )
+
+    def room(self, order, stage, rooms, step):
+        if stage == 0:
+            return rooms[0]
+        if stage == 1:
+            size = self.place.size[order[2]]
+            return rooms[1].at[pl.ds((step - 1) * size, size)]
+        return rooms[2].at[step - 1]
+
+    def send_stage(self, lead, order, stage, total, rooms, add):
+        axis = order[stage]
         for step in self.place.partners(axis):
-            self.copy(lead, stage, step, axis, room.at[step - 1], room.at[step - 1]).wait_recv()
-
-    @staticmethod
-    def pick(order, first, second):
-        return (first, second) if order == "ab" else (second, first)
-
-    def after_core(self, lead, order, own, other, came):
-        place = self.place
-        axis, rest = order
-
-        def add(where):
-            for item in range(place.size[rest]):
-                at = self.pick(order, where, item)
-                other[at] = own[at] + other[at]
-
-        for step in place.partners(axis):
-            where = place.moved(axis, step)[axis]
-            add(where)
-            source = other.at[where] if order == "ab" else other.at[:, where]
-            self.start(lead, 1, step, axis, source, came.at[step - 1])
-        add(place.at[axis])
-
-    def after_first(self, lead, order, total, came, later):
-        place = self.place
-        axis, rest = order
-        self.await_all(lead, 1, axis, came)
-
-        def add(where):
-            at = self.pick(order, place.at[axis], where)
-            value = total[at].astype(jnp.float32)
-            for step in place.partners(axis):
-                value = value + came[step - 1, where].astype(jnp.float32)
-            total[at] = value.astype(total.dtype)
-
-        for step in place.partners(rest):
-            where = place.moved(rest, step)[rest]
-            add(where)
-            at = self.pick(order, place.at[axis], where)
-            self.start(lead, 2, step, rest, total.at[at], later.at[step - 1])
-        add(place.at[rest])
-
-    def after_second(self, lead, order, total, later, last):
-        place = self.place
-        rest = order[1]
-        a, b = place.at["a"], place.at["b"]
-        self.await_all(lead, 2, rest, later)
-
-        def add(where):
-            value = total[a, b, where].astype(jnp.float32)
-            for step in place.partners(rest):
-                value = value + later[step - 1, where].astype(jnp.float32)
-            return value
-
-        for step in place.partners("z"):
-            where = place.moved("z", step)["z"]
-            total[a, b, where] = add(where).astype(total.dtype)
-            self.start(lead, 3, step, "z", total.at[a, b, where], last.at[step - 1])
-        return add(place.at["z"])
-
-    def after_last(self, lead, value, last):
-        self.await_all(lead, 3, "z", last)
-        for step in self.place.partners("z"):
-            value = value + last[step - 1].astype(jnp.float32)
+            where = self.place.moved(axis, step)[axis]
+            for at, _ in self.blocks(order, stage, where):
+                add(at)
+            source = total.at[self.region(order, stage, where)]
+            room = self.room(order, stage, rooms, step)
+            self.start(lead, stage + 1, step, axis, source, room)
+        for at, _ in self.blocks(order, stage, self.place.at[axis]):
+            add(at)
+
+    def await_stage(self, lead, order, stage, rooms):
+        axis = order[stage]
+        for step in self.place.partners(axis):
+            room = self.room(order, stage, rooms, step)
+            self.copy(lead, stage + 1, step, axis, room, room).wait_recv()
+
+    def after_core(self, lead, order, own, total, rooms):
+        def add(at):
+            total[at] = own[at] + total[at]
+
+        self.send_stage(lead, order, 0, total, rooms, add)
+
+    def came_in(self, order, stage, total, rooms, at):
+        rest = [axis for axis in "abz" if axis in order[stage + 1 :]]
+        inner = tuple(item for axis, item in zip("abz", at) if axis in rest)
+        value = total[at].astype(jnp.float32)
+        for step in self.place.partners(order[stage]):
+            room = self.room(order, stage, rooms, step)
+            value = value + (room[inner] if inner else room[...]).astype(jnp.float32)
         return value
 
-    def drain(self, lead, order, total, came, later, last):
-        place = self.place
-        axis, rest = order
+    def after_stage(self, lead, order, stage, total, rooms):
+        self.await_stage(lead, order, stage - 1, rooms)
+
+        def add(at):
+            total[at] = self.came_in(order, stage - 1, total, rooms, at).astype(total.dtype)
+
+        self.send_stage(lead, order, stage, total, rooms, add)
+
+    def after_last(self, lead, order, total, rooms):
+        self.await_stage(lead, order, 2, rooms)
+        at = tuple(self.place.at[axis] for axis in "abz")
+        return self.came_in(order, 2, total, rooms, at)
+
+    def drain(self, lead, order, total, rooms):
         self.copy(lead, 0, 1, "c", total, total).wait_send()
-        for step in place.partners(axis):
-            self.copy(lead, 1, step, axis, came.at[step - 1], came.at[step - 1]).wait_send()
-        for step in place.partners(rest):
-            self.copy(lead, 2, step, rest, later.at[step - 1], later.at[step - 1]).wait_send()
-        for step in place.partners("z"):
-            self.copy(lead, 3, step, "z", last.at[step - 1], last.at[step - 1]).wait_send()
+        for stage in range(3):
+            axis = order[stage]
+            for step in self.place.partners(axis):
+                room = self.room(order, stage, rooms, step)
+                self.copy(lead, stage + 1, step, axis, room, room).wait_send()
 
 
 class Gradients(Sums):
-    def __init__(self, place, terms, rooms, results, ring, ring_sem, send_sem, recv_sem):
+    orders = ("abz", "baz", "azb", "abz", "baz", "bza")
+
+    def __init__(self, place, terms, total, rooms, results, ring, ring_sem, send_sem, recv_sem):
         super().__init__(place, send_sem, recv_sem)
-        self.terms, self.rooms, self.results = terms, rooms, results
+        self.terms, self.sums, self.rooms, self.results = terms, total, rooms, results
         self.ring, self.ring_sem = ring, ring_sem
         self.total = results.shape[0]
         self.first = terms[0].shape[0]
 
     def by_order(self, index, work):
-        half = index // 2
-        total, ones, others, twos, fours, last = self.rooms
-
-        @when(index % 2 == 0)
-        def _():
-            work("ab", total.at[index], ones.at[half], twos.at[half], last.at[index])
-
-        @when(index % 2 == 1)
-        def _():
-            work("ba", total.at[index], others.at[half], fours.at[half], last.at[index])
+        rooms = [room.at[index] for room in self.rooms]
+        total = self.sums.at[index]
+        by_order(self.place, self.orders, index, lambda order: work(order, total, rooms))
 
     def begin(self, index):
         side = self.place.at["c"]
         slot = index % (AHEAD + 1)
 
         def go(source):
-            self.start((index,), 0, 1, "c", source.at[:, :, 1 - side], self.rooms[0].at[index])
+            self.start((index,), 0, 1, "c", source.at[:, :, 1 - side], self.sums.at[index])
             pltpu.make_async_copy(
                 source.at[:, :, side], self.ring.at[slot], self.ring_sem.at[slot]
             ).start()
@@ -1384,52 +1383,41 @@
         @when(live(now))
         def _():
             slot = now % (AHEAD + 1)
-            room = self.ring.at[slot]
-            pltpu.make_async_copy(room, room, self.ring_sem.at[slot]).wait()
-            total = self.rooms[0].at[now]
+            own = self.ring.at[slot]
+            pltpu.make_async_copy(own, own, self.ring_sem.at[slot]).wait()
+            total = self.sums.at[now]
             self.copy((now,), 0, 1, "c", total, total).wait_recv()
             self.by_order(
                 now,
-                lambda order, total, came, later, last: self.after_core(
-                    (now,), order, room, total, came
-                ),
+                lambda order, total, rooms: self.after_core((now,), order, own, total, rooms),
             )
 
-        second = now - LAG
-
-        @when(live(second))
+        for stage in (1, 2):
+            index = now - stage * LAG
+
+            @when(live(index))
+            def _(index=index, stage=stage):
+                self.by_order(
+                    index,
+                    lambda order, total, rooms: self.after_stage(
+                        (index,), order, stage, total, rooms
+                    ),
+                )
+
+        index = now - 3 * LAG
+
+        @when(live(index))
         def _():
-            self.by_order(
-                second,
-                lambda order, total, came, later, last: self.after_first(
-                    (second,), order, total, came, later
-                ),
-            )
-
-        third = now - 2 * LAG
-
-        @when(live(third))
-        def _():
-            def work(order, total, came, later, last):
-                self.results[third] = self.after_second((third,), order, total, later, last)
-
-            self.by_order(third, work)
-
-        fourth = now - 3 * LAG
-
-        @when(live(fourth))
-        def _():
-            self.results[fourth] = self.after_last(
-                (fourth,), self.results[fourth], self.rooms[5].at[fourth]
-            )
+            def work(order, total, rooms):
+                self.results[index] = self.after_last((index,), order, total, rooms)
+
+            self.by_order(index, work)
 
     def finish(self):
         def work(index):
             self.by_order(
                 index,
-                lambda order, total, came, later, last: self.drain(
-                    (index,), order, total, came, later, last
-                ),
+                lambda order, total, rooms: self.drain((index,), order, total, rooms),
             )
 
         each(self.total, work)
@@ -1487,11 +1475,12 @@
 
 
 def backward_kernel(dims, *refs):
-    tokens, crops, kept, sums_in, grad_up_bias, rows = refs[:6]
-    qkv_in, mixed_in, inverse_in, attended_t_in, normed_t_in, grad_middle_in = refs[6:12]
-    attention_in, terms = refs[12:14]
-    input_grad, owned, owned_small, attention_terms = refs[14:18]
+    crops, kept, grad_up_bias, rows = refs[:4]
+    tokens_in, grad_out_in, qkv_in, mixed_in, inverse_in, attended_t_in, normed_t_in = refs[4:11]
+    middle_in, result_in, grad_normed_in, attention_in, terms = refs[11:16]
+    output, input_grad, owned, owned_small, attention_terms = refs[16:21]
     (
+        tokens,
         weights,
         mask,
         mask_t,
@@ -1507,15 +1496,13 @@
         small,
         ring,
         total,
-        ones,
-        others,
-        twos,
-        fours,
-        last,
-        side_other,
-        side_came,
-        side_later,
-        side_last,
+        rooms_one,
+        rooms_two,
+        rooms_three,
+        side_total,
+        side_one,
+        side_two,
+        side_three,
         load_sem,
         stage_sem,
         ring_sem,
@@ -1523,54 +1510,77 @@
         recv_sem,
         side_send_sem,
         side_recv_sem,
-    ) = refs[18:]
+    ) = refs[21:]
     outer, inner, depth = dims
     devices = 2 * outer * inner * depth
     place = Place(dims)
     spot = place.at
-    place.greet()
+    loads = {}
+
+    def load(name, source, target):
+        item = pltpu.make_async_copy(source, target, load_sem.at[len(loads)])
+        item.start()
+        loads[name] = item
+
+    load("grad_normed", grad_normed_in, inverse)
+    load("middle", middle_in, mixed)
+    load("grad_out", grad_out_in, grad_attended)
+    load("result", result_in, grad_mixed)
     adder = Gradients(
         place,
         (terms, attention_terms),
-        (total, ones, others, twos, fours, last),
+        total,
+        (rooms_one, rooms_two, rooms_three),
         owned,
         ring,
         ring_sem,
         send_sem,
         recv_sem,
     )
+    place.greet()
     for index in range(AHEAD):
         adder.begin(index)
-    loads = {}
-
-    def load(name, source, target):
-        item = pltpu.make_async_copy(source, target, load_sem.at[len(loads)])
-        item.start()
-        loads[name] = item
-
-    load("grad_middle", grad_middle_in, grad_middle)
     load("out", attention_in.at[pl.ds(6, 2)], weights.at[pl.ds(6, 2)])
     load("attended", attended_t_in, turned.at[0])
     load("qkv", qkv_in, qkv)
+    load("normed", normed_t_in, turned.at[1])
+    load("rest", attention_in.at[pl.ds(0, 6)], weights.at[pl.ds(0, 6)])
+    load("tokens", tokens_in, tokens)
+    adder.tick(0)
+    mask[...] = allowed(crops[...], kept[...])
+    mask_t[...] = allowed_back(crops[...], kept[...])
+    sums[...] = jnp.zeros(sums.shape, jnp.float32)
+    for name in ("grad_normed", "middle", "grad_out", "result"):
+        loads[name].wait()
+
+    def close_branch(at):
+        unit, scale = moments(mixed[at, :])
+        grad = grad_attended[at, :].astype(jnp.float32)
+        value = inverse[at, :]
+        input_grad[at, :] = grad_mixed[at, :].astype(jnp.bfloat16)
+        sums[0:1, :] += jnp.sum(value * unit, axis=0, keepdims=True)
+        sums[1:2, :] += jnp.sum(value, axis=0, keepdims=True)
+        sums[2:3, :] += jnp.sum(grad, axis=0, keepdims=True)
+        scaled = value * rows[2:3, :]
+        summed = grad + scale * (
+            scaled
+            - jnp.mean(scaled, axis=-1, keepdims=True)
+            - unit * jnp.mean(scaled * unit, axis=-1, keepdims=True)
+        )
+        grad_middle[at, :] = summed
+        grad_attended[at, :] = summed.astype(jnp.bfloat16)
+
+    adder.tick(1)
+    by_rows(close_branch)
     load("mixed", mixed_in, mixed)
     load("inverse", inverse_in, inverse)
-    load("normed", normed_t_in, turned.at[1])
-    load("rest", attention_in.at[pl.ds(0, 6)], weights.at[pl.ds(0, 6)])
-    mask[...] = allowed(crops[...], kept[...])
-    mask_t[...] = allowed_back(crops[...], kept[...])
-    sums[...] = sums_in[...]
-    loads["grad_middle"].wait()
-
-    def round_rows(at):
-        grad_attended[at, :] = grad_middle[at, :].astype(jnp.bfloat16)
-
-    by_rows(round_rows)
-    adder.tick(0)
+    load("output", input_grad, output)
+    adder.tick(2)
     loads["out"].wait()
     grad_mixed[...] = dot_nt(grad_attended[:, 0:WIDE], matrix(weights, 6)) + dot_nt(
         grad_attended[:, WIDE:WIDTH], matrix(weights, 7)
     )
-    adder.tick(1)
+    adder.tick(3)
     loads["attended"].wait()
     for half in (0, 1):
         columns = slice(half * WIDE, half * WIDE + WIDE)
@@ -1582,8 +1592,10 @@
     for name in ("qkv", "mixed", "inverse"):
         loads[name].wait()
 
+    loads["output"].wait()
+
     def heads(pair):
-        adder.tick(2 + pair)
+        adder.tick(4 + pair)
         backward_heads(pair, qkv, mask, mask_t, mixed, inverse, grad_mixed)
 
     each(8, heads)
@@ -1598,28 +1610,30 @@
             staged.at[slot], attention_terms.at[2 + index], stage_sem.at[slot]
         )
 
+    for half in (0, 1):
+        pltpu.make_async_copy(
+            staged.at[half], attention_terms.at[half], stage_sem.at[half]
+        ).wait()
+
     def project(index):
-        pltpu.make_async_copy(
-            staged.at[index % 2], staged.at[index % 2], stage_sem.at[index % 2]
-        ).wait()
-        adder.tick(10 + index)
+        @pl.when(index >= 2)
+        def _():
+            stage_copy(index - 2).wait()
+
         value = dot(turned[1], qkv[index]).astype(jnp.bfloat16)
         staged[index % 2] = value.reshape(staged.shape[1:])
         stage_copy(index).start()
         grad_normed[...] += dot_nt(qkv[index], matrix(weights, index))
 
-    each(4, project)
-    for index in (4, 5):
-        slot = index % 2
-        stage_copy(index - 2).wait()
-        value = dot(turned[1], qkv[index]).astype(jnp.bfloat16)
-        staged[slot] = value.reshape(staged.shape[1:])
-        stage_copy(index).start()
-        grad_normed[...] += dot_nt(qkv[index], matrix(weights, index))
-        adder.tick(10 + index)
+        @pl.when(index < 4)
+        def _():
+            adder.tick(12 + index)
+
+    each(6, project)
     for index in (4, 5):
         stage_copy(index).wait()
     adder.tick(16)
+    loads["tokens"].wait()
 
     def close(at):
         unit, scale = moments(tokens[at, :].astype(jnp.float32))
@@ -1654,22 +1668,33 @@
         small[at + (slice(2, 3),)] = third[device : device + 1, :]
         small[at + (slice(3, 8),)] = jnp.zeros((5, 128), jnp.float32)
     side = Sums(place, side_send_sem, side_recv_sem)
-    side.start((), 0, 1, "c", small.at[:, :, 1 - spot["c"]], side_other)
-    adder.tick(17)
-    side.copy((), 0, 1, "c", side_other, side_other).wait_recv()
-    side.after_core((), "ab", small.at[:, :, spot["c"]], side_other, side_came)
-    adder.tick(18)
-    side.after_first((), "ab", side_other, side_came, side_later)
-    adder.tick(19)
-    owned_small[...] = side.after_second((), "ab", side_other, side_later, side_last)
-    adder.tick(20)
-    owned_small[...] = side.after_last((), owned_small[...], side_last)
-    each(GATHERED + 3 * LAG - 21, lambda index: adder.tick(21 + index))
-    side.drain((), "ab", side_other, side_came, side_later, side_last)
+    rooms = (side_one, side_two, side_three)
+    side.start((), 0, 1, "c", small.at[:, :, 1 - spot["c"]], side_total)
+
+    def last_ticks(step):
+        adder.tick(17 + step)
+
+        @pl.when(step == 0)
+        def _():
+            side.copy((), 0, 1, "c", side_total, side_total).wait_recv()
+            side.after_core((), "abz", small.at[:, :, spot["c"]], side_total, rooms)
+
+        for stage in (1, 2):
+
+            @pl.when(step == stage)
+            def _(stage=stage):
+                side.after_stage((), "abz", stage, side_total, rooms)
+
+        @pl.when(step == 3)
+        def _():
+            owned_small[...] = side.after_last((), "abz", side_total, rooms)
+
+    each(GATHERED + 3 * LAG - 17, last_ticks)
+    side.drain((), "abz", side_total, rooms)
     adder.finish()
 
 
-def backward(dims, tokens, crops, kept, sums, grad_up_bias, rows, kept_values, terms):
+def backward(dims, crops, kept, grad_up_bias, rows, arrays):
     outer, inner, depth = dims
     most = max(dims) - 1
     lead = (outer, inner, 2, depth)
@@ -1678,20 +1703,21 @@
     f32, bf16 = jnp.float32, jnp.bfloat16
     shape = jax.ShapeDtypeStruct
     vmem, anywhere = pl.BlockSpec(memory_space=pltpu.VMEM), pl.BlockSpec(memory_space=pl.ANY)
-    half = GATHERED // 2
     chip = (outer, inner, depth)
     small_tile = (8, 128)
     return pl.pallas_call(
         functools.partial(backward_kernel, dims),
         out_shape=[
             shape(whole, bf16),
+            shape(whole, bf16),
             shape((GATHERED,) + tile, f32),
             shape(small_tile, f32),
             shape((8,) + lead + tile, bf16),
         ],
-        in_specs=[vmem] * 6 + [anywhere] * 8,
-        out_specs=[vmem] * 3 + [anywhere],
+        in_specs=[vmem] * 4 + [anywhere] * 12,
+        out_specs=[anywhere] + [vmem] * 3 + [anywhere],
         scratch_shapes=[
+            pltpu.VMEM(whole, bf16),
             pltpu.VMEM((8,) + lead + tile, bf16),
             pltpu.VMEM((LENGTH, LENGTH), bf16),
             pltpu.VMEM((LENGTH, LENGTH), bf16),
@@ -1707,16 +1733,14 @@
             pltpu.VMEM(lead + small_tile, f32),
             pltpu.VMEM((AHEAD + 1,) + chip + tile, bf16),
             pltpu.VMEM((GATHERED,) + chip + tile, bf16),
-            pltpu.VMEM((half, outer - 1, inner, depth) + tile, bf16),
-            pltpu.VMEM((half, inner - 1, outer, depth) + tile, bf16),
-            pltpu.VMEM((half, inner - 1, depth) + tile, bf16),
-            pltpu.VMEM((half, outer - 1, depth) + tile, bf16),
-            pltpu.VMEM((GATHERED, depth - 1) + tile, bf16),
+            pltpu.VMEM((GATHERED, 2, 4) + tile, bf16),
+            pltpu.VMEM((GATHERED, 6) + tile, bf16),
+            pltpu.VMEM((GATHERED, 3) + tile, bf16),
             pltpu.VMEM(chip + small_tile, f32),
-            pltpu.VMEM((outer - 1, inner, depth) + small_tile, f32),
-            pltpu.VMEM((inner - 1, depth) + small_tile, f32),
-            pltpu.VMEM((depth - 1,) + small_tile, f32),
-            pltpu.SemaphoreType.DMA((8,)),
+            pltpu.VMEM((2, 4) + small_tile, f32),
+            pltpu.VMEM((6,) + small_tile, f32),
+            pltpu.VMEM((3,) + small_tile, f32),
+            pltpu.SemaphoreType.DMA((13,)),
             pltpu.SemaphoreType.DMA((2,)),
             pltpu.SemaphoreType.DMA((AHEAD + 1,)),
             pltpu.SemaphoreType.DMA((GATHERED, 4, most)),
@@ -1728,7 +1752,55 @@
             collective_id=1, has_side_effects=True, vmem_limit_bytes=VMEM_LIMIT
         ),
         name="backward",
-    )(tokens, crops, kept, sums, grad_up_bias, rows, *kept_values, terms)
+    )(crops, kept, grad_up_bias, rows, *arrays)
+
+
+def place_kernel(*refs):
+    result, input_grad, owned, small = refs[:4]
+    result_out, input_grad_out, query, key, value, out, up, down = refs[4:12]
+    vectors, bias_up = refs[12:17], refs[17]
+    sems = refs[18]
+    copies = [(result, result_out.at[0]), (input_grad, input_grad_out.at[0])]
+    for index in range(GATHERED):
+        if index < 8:
+            group, half = index // 2, index % 2
+            target = down.at[pl.ds(group * UNIT, UNIT), pl.ds(half * WIDE, WIDE)]
+        elif index < 16:
+            target = up.at[:, pl.ds((index - 8) * WIDE, WIDE)]
+        else:
+            matrix_out = (out, query, key, value)[(index - 16) // 2]
+            target = matrix_out.at[:, pl.ds((index % 2) * WIDE, WIDE)]
+        copies.append((owned.at[index], target))
+    items = [
+        pltpu.make_async_copy(source, target, sems.at[index])
+        for index, (source, target) in enumerate(copies)
+    ]
+    for item in items:
+        item.start()
+    for index in range(4):
+        vectors[index][...] = small[0, index * UNIT : (index + 1) * UNIT]
+    vectors[4][...] = small[2, 0:UNIT]
+    bias_up[...] = small[1, :]
+    for item in items:
+        item.wait()
+
+
+def place_results(result, input_grad, owned, small):
+    f32, bf16 = jnp.float32, jnp.bfloat16
+    shape = jax.ShapeDtypeStruct
+    vmem, anywhere = pl.BlockSpec(memory_space=pltpu.VMEM), pl.BlockSpec(memory_space=pl.ANY)
+    return pl.pallas_call(
+        place_kernel,
+        out_shape=[shape((1, LENGTH, WIDTH), bf16)] * 2
+        + [shape((UNIT, WIDTH), f32)] * 4
+        + [shape((UNIT, HIDDEN), f32), shape((4 * UNIT, WIDTH), f32)]
+        + [shape((UNIT,), f32)] * 5
+        + [shape((4 * UNIT,), f32)],
+        in_specs=[anywhere] * 3 + [vmem],
+        out_specs=[vmem] * 14,
+        scratch_shapes=[pltpu.SemaphoreType.DMA((GATHERED + 2,))],
+        name="results",
+    )(result, input_grad, owned, small)
 
 
 def body(
@@ -1755,7 +1827,7 @@
         tokens.shape == (1, LENGTH, WIDTH)
         and w_up.shape == (UNIT, HIDDEN)
         and w_down.shape == (HIDDEN // WIDTH * UNIT, WIDTH)
-        and dims[2] * 4 * UNIT == WIDE
+        and dims == (2, 2, 4)
     )
     if not fits:
         return general_body(
@@ -1780,54 +1852,43 @@
         vector.reshape(1, -1)
         for vector in (norm1_gain, norm1_bias, norm2_gain, norm2_bias, down_bias, up_bias)
     ]
-    pixels = tokens.reshape(LENGTH, WIDTH)
-    (output, sums, grad_up, rows, qkv, mixed, inverse, attended_t, normed_t, grad_middle, attention, terms) = (
-        forward(
-            dims,
-            pixels,
-            cotangent.reshape(LENGTH, WIDTH),
-            crop_ids,
-            kv_mask,
-            small,
-            (w_query, w_key, w_value, w_out, w_up, w_down),
-        )
-    )
-    input_grad, owned, owned_small, _ = backward(
-        dims,
-        pixels,
-        crop_ids,
-        kv_mask,
-        sums,
+    pixels, grads = tokens.reshape(LENGTH, WIDTH), cotangent.reshape(LENGTH, WIDTH)
+    shards = (w_query, w_key, w_value, w_out, w_up, w_down)
+    grad_up, rows, *arrays = forward(dims, pixels, grads, crop_ids, kv_mask, small, shards)
+    result, input_grad, owned, owned_small, _ = backward(
+        dims, crop_ids, kv_mask, grad_up, rows, (pixels, grads, *arrays)
+    )
+    (
+        output,
+        grad_tokens,
+        grad_query,
+        grad_key,
+        grad_value,
+        grad_out,
         grad_up,
-        rows,
-        (qkv, mixed, inverse, attended_t, normed_t, grad_middle, attention),
-        terms,
-    )
-
-    def side_by_side(start, count):
-        return owned[start : start + count].transpose(1, 0, 2).reshape(UNIT, count * WIDE)
-
-    own_down = owned[0:8].reshape(4, 2, UNIT, WIDE).transpose(0, 2, 1, 3).reshape(4 * UNIT, WIDTH)
-    own_up = side_by_side(8, 8)
-    own_out, own_query, own_key, own_value = (side_by_side(16 + 2 * index, 2) for index in range(4))
-    gain_one, bias_one, gain_two, bias_two = (
-        owned_small[0, index * UNIT : (index + 1) * UNIT] for index in range(4)
-    )
+        grad_down,
+        grad_gain_one,
+        grad_bias_one,
+        grad_gain_two,
+        grad_bias_two,
+        grad_bias_down,
+        grad_bias_up,
+    ) = place_results(result, input_grad, owned, owned_small)
     return (
-        output.reshape(tokens.shape),
-        input_grad.reshape(tokens.shape),
-        gain_one,
-        bias_one,
-        own_query,
-        own_key,
-        own_value,
-        own_out,
-        gain_two,
-        bias_two,
-        own_up,
-        owned_small[1],
-        own_down,
-        owned_small[2, :UNIT],
+        output,
+        grad_tokens,
+        grad_gain_one,
+        grad_bias_one,
+        grad_query,
+        grad_key,
+        grad_value,
+        grad_out,
+        grad_gain_two,
+        grad_bias_two,
+        grad_up,
+        grad_bias_up,
+        grad_down,
+        grad_bias_down,
     )
 
 

time: 285 us -> 273 us (0.958)
  local copies, waits for them, and re-layouts: 11.8 us -> 0 us
    pallas_call x1, Pallas kernels: 145 us -> 137 us  [forward(): pl.pallas_call(functools.partial(forward_kernel, dims), out_shape=[shape(...]
    pallas_call x0 -> x1, Pallas kernels: none -> 4.67 us  [place_results(): pl.pallas_call(place_kernel, out_shape=[shape((1, LENGTH, WIDTH), bf16)]...]
    unnamed x8 -> x0, local copies, waits for them, and re-layouts: 3.97 us -> none
    reshape x5 -> x0, local copies, waits for them, and re-layouts: 3.49 us -> none  [side_by_side(): owned[start:start + count].transpose(1, 0, 2).reshape(UNIT, count * WIDE)]
    pallas_call x1, Pallas kernels: 127 us -> 130 us  [backward(): pl.pallas_call(functools.partial(backward_kernel, dims), out_shape=[shape...]
where the time goes in v3:
time: 273 us
  Pallas kernels  272 us (100%)
    pallas_call x1, Pallas kernels, forward(): pl.pallas_call(functools.partial(forward_kernel, dims), out_shape=[shape(...  137 us
    pallas_call x1, Pallas kernels, backward(): pl.pallas_call(functools.partial(backward_kernel, dims), out_shape=[shape...  130 us

profile of v3, /device:TPU:0, one launch (start us, length us, event | category | flops | bytes accessed | tf_op | source)
XLA Modules:
  0.0 272.7 jit_solution(10075535290774761955)
XLA Ops:
  0.6 137.1 %forward.1 = (f32[8,512]{1,0:T(8,128)}, f32[8,1024]{1,0:T(8,128)}, bf16[6,512,512]{2,1,0:T(8,128)(2,1)}, f32[512,1024]{1,0:T(8,128)}, f32[512,1024]{1,0:T(8,128)...) custom-call(s32[1,512]{1,0:T(1,128)} %refs_0_.3, ...), custom_call_target="tpu_custom_call" | custom-call | tf_op jit(solution)/shard_map/forward/pallas_call | solution.py:1206
  137.8 130.1 %backward.1 = (bf16[512,1024]{1,0:T(8,128)(2,1)}, bf16[512,1024]{1,0:T(8,128)(2,1)}, f32[24,32,512]{2,1,0:T(8,128)}, f32[8,128]{1,0:T(8,128)}, bf16[8,2,2,2,4,32,512]{6,5,4,3,2,1,0:T(8,128)(2,1)}) custom-call(s32[1,512]{1,0:T(1,128)} %refs_0_.3, s32[1,512]{1,0:T(1,128)} %refs_1_.3, f32[8,512]{1,0:T(8,128)} %get-tuple-element.44.refs_2_, ...), custom_call_target="tpu_custom_call" | custom-call | tf_op jit(solution)/shard_map/backward/pallas_call | solution.py:1708
  267.9 4.7 %results.1 = (bf16[1,512,1024]{2,1,0:T(8,128)(2,1)}, bf16[1,512,1024]{2,1,0:T(8,128)(2,1)}, f32[32,1024]{1,0:T(8,128)}, f32[32,1024]{1,0:T(8,128)}, f32[32,1024]...) custom-call(bf16[512,1024]{1,0:T(8,128)(2,1)} %get-tuple-element.56., ...), custom_call_target="tpu_custom_call" | custom-call | tf_op jit(solution)/shard_map/results/pallas_call | solution.py:1792

commit v4 on v3

--- a/solution.py
+++ b/solution.py
@@ -672,12 +672,13 @@
 WIDTH = 1024
 HIDDEN = 4096
 UNIT = 32
-GATHERED = 24
-DOWN, UP = 8, 16
+CHUNKS = 24
+FEED = 8
+ROOMS = 12
 LAG = 2
 AHEAD = 4
-WIDE32 = jnp.float32
-HALF16 = jnp.bfloat16
+TERMS_AHEAD = 3
+TERMS_START = 23
 VMEM_LIMIT = 63 << 20
 
 
@@ -799,13 +800,14 @@
 
                 self.by_order(index, work)
 
-    def finish(self):
-        each(
-            self.total,
-            lambda index: self.by_order(
+    def finish(self, first, count):
+        def work(step):
+            index = first + step
+            self.by_order(
                 index, lambda order: self.drain(self.buffer.at[index], (index,), order)
-            ),
-        )
+            )
+
+        each(count, work)
 
 
 def moments(values):
@@ -849,10 +851,10 @@
         mine = owner == lax.broadcasted_iota(jnp.int32, (devices, total), 0)
         return jnp.sum(jnp.where(mine, found, 0.0), axis=0, keepdims=True)
 
-    first = line(0)
+    first, second = line(0), line(1)
     rows = [spread(first, index * UNIT, UNIT) for index in range(4)]
     rows.append(spread(line(2), 0, UNIT))
-    return rows, spread(line(1), 0, 4 * UNIT)
+    return rows, [spread(second, index * UNIT, UNIT) for index in range(4)]
 
 
 def write_vectors(rows, devices):
@@ -936,29 +938,27 @@
         attended[rows, columns] = result.astype(jnp.bfloat16)
 
 
-def down_rows(dims, buffer, block, half):
-    outer, inner, depth = dims
-    at = (block // (2 * inner), (block // 2) % inner, block % 2)
-    return jnp.concatenate(
-        [
-            buffer[(DOWN + 2 * group + half,) + at + (z,)]
-            for z in range(depth)
-            for group in range(4)
-        ],
-        axis=0,
-    )
-
-
-def feed_block(dims, block, refs):
-    normed, normed_t, grad_out, weights, up_bias, result, grad_normed, to_up, to_down, grad_bias = refs
-    up = matrix(weights, UP + block)
+def hidden_order(flip):
+    shape = (4 * 128, 4 * 128)
+    rows, columns = (lax.broadcasted_iota(jnp.int32, shape, axis) for axis in (0, 1))
+    if flip:
+        rows, columns = columns, rows
+    wanted = (rows // UNIT) % 4 * 128 + rows // 128 * UNIT + rows % UNIT
+    return columns == wanted
+
+
+def feed_block(block, refs):
+    normed, normed_t, grad_out, weights, up_bias, result, grad_normed, staged, grad_bias = refs
+    group, half = block // 2, block % 2
+    first = FEED + 4 * group
+    up = matrix(weights, first + 2 + half)
     upper = dot(normed[...], up) + up_bias[pl.ds(block, 1), :]
     hidden, slope = gelu_pair(upper)
     hidden = hidden.astype(jnp.bfloat16)
     grad_hidden = None
-    for half in (0, 1):
-        columns = slice(half * WIDE, half * WIDE + WIDE)
-        down = down_rows(dims, weights, block, half)
+    for side in (0, 1):
+        columns = slice(side * WIDE, side * WIDE + WIDE)
+        down = weights[first + side, half].reshape(WIDE, WIDE)
         result[:, columns] += dot(hidden, down)
         term = dot_nt(grad_out[:, columns], down)
         grad_hidden = term if grad_hidden is None else grad_hidden + term
@@ -967,295 +967,12 @@
         grad_upper.astype(jnp.float32), axis=0, keepdims=True
     )
     grad_normed[...] += dot_nt(grad_upper, up)
-    to_up[...] = dot(normed_t[...], grad_upper).astype(jnp.bfloat16).reshape(to_up.shape)
-    for half in (0, 1):
-        columns = slice(half * WIDE, half * WIDE + WIDE)
-        term = dot_tn(hidden, grad_out[:, columns]).astype(jnp.bfloat16)
-        for z in range(dims[2]):
-            for group in range(4):
-                start = (z * 4 + group) * UNIT
-                to_down[2 * group + half, z] = term[start : start + UNIT]
-
-
-def forward_kernel(dims, *refs):
-    (
-        crops,
-        kept,
-        gain_one,
-        bias_one,
-        gain_two,
-        bias_two,
-        bias_down,
-        bias_up,
-        tokens_in,
-        grad_out_in,
-    ) = refs[:10]
-    shards = refs[10:16]
-    (
-        grad_up_bias,
-        rows,
-        qkv_out,
-        mixed_out,
-        inverse_out,
-        attended_t_out,
-        normed_t_out,
-        middle_out,
-        result_out,
-        grad_normed_out,
-        attention_out,
-        terms,
-    ) = refs[16:28]
-    (
-        tokens,
-        grad_out,
-        weights,
-        vectors,
-        up_bias,
-        mask,
-        qkv,
-        mixed,
-        inverse,
-        attended,
-        attended_t,
-        normed,
-        normed_t,
-        middle,
-        normed_two,
-        normed_two_t,
-        result,
-        grad_normed,
-        to_up,
-        to_down,
-        send_sem,
-        recv_sem,
-        vector_send_sem,
-        vector_recv_sem,
-        load_sem,
-        store_sem,
-        up_sem,
-        down_sem,
-    ) = refs[28:]
-    outer, inner, depth = dims
-    devices = 2 * outer * inner * depth
-    place = Place(dims)
-    spot = (place.at["a"], place.at["b"], place.at["c"], place.at["z"])
-
-    loads = []
-    for index in range(GATHERED):
-        if index < DOWN:
-            source = shards[index // 2].at[:, pl.ds((index % 2) * WIDE, WIDE)]
-        elif index < UP:
-            group, half = (index - DOWN) // 2, (index - DOWN) % 2
-            source = shards[5].at[pl.ds(group * UNIT, UNIT), pl.ds(half * WIDE, WIDE)]
-        else:
-            source = shards[4].at[:, pl.ds((index - UP) * WIDE, WIDE)]
-        item = pltpu.make_async_copy(source, weights.at[(index,) + spot], load_sem.at[index])
-        item.start()
-        loads.append(item)
-    for index, (source, target) in enumerate(((tokens_in, tokens), (grad_out_in, grad_out))):
-        item = pltpu.make_async_copy(source, target, load_sem.at[GATHERED + index])
-        item.start()
-        loads.append(item)
-
-    small = Gather(place, vector_send_sem, vector_recv_sem)
-    order = "zbac"
-    lines = [
-        jnp.concatenate([item[...] for item in (gain_one, bias_one, gain_two, bias_two)], axis=1),
-        bias_up[...],
-        jnp.concatenate([bias_down[...], jnp.zeros((1, 128 - UNIT), jnp.bfloat16)], axis=1),
-    ]
-    packed = jnp.concatenate(
-        [line.astype(jnp.float32) for line in lines] + [jnp.zeros((5, 128), jnp.float32)], axis=0
-    )
-    vectors[spot] = packed
-    place.greet()
-    small.send(vectors, (), order, 0)
-    gather_all = Weights(place, weights, send_sem, recv_sem)
-    for index in range(AHEAD):
-        loads[index].wait()
-        gather_all.begin(index)
-    for item in loads[AHEAD:]:
-        item.wait()
-    mask[...] = allowed(crops[...], kept[...])
-    for stage in range(4):
-        small.receive(vectors, (), order, stage)
-        if stage < 3:
-            small.send(vectors, (), order, stage + 1)
-            gather_all.tick(stage)
-    width_rows, up_row = read_vectors(vectors, devices)
-    for index, row in enumerate(width_rows):
-        rows[index : index + 1, :] = row
-    rows[5:8, :] = jnp.zeros((3, WIDTH), jnp.float32)
-    for index in range(8):
-        up_bias[index : index + 1, :] = up_row[:, index * WIDE : (index + 1) * WIDE]
-
-    def first_norm(at):
-        unit, _ = moments(tokens[at, :].astype(jnp.float32))
-        normed[at, :] = (unit * rows[0:1, :] + rows[1:2, :]).astype(jnp.bfloat16)
-
-    by_rows(first_norm)
-    stores = []
-
-    def store(source, target):
-        item = pltpu.make_async_copy(source, target, store_sem.at[len(stores)])
-        item.start()
-        stores.append(item)
-
-    transpose_into(normed, normed_t)
-    store(normed_t, normed_t_out)
-    for now in range(3, 6):
-        gather_all.tick(now)
-
-    def project(index):
-        gather_all.tick(6 + index)
-        value = dot(normed[...], matrix(weights, index))
-        mapped = jnp.where(value > 0, value + 1.0, jnp.exp(jnp.minimum(value, 0.0)))
-        qkv[index] = jnp.where(index < 4, mapped, value).astype(jnp.bfloat16)
-
-    each(6, project)
-    store(qkv, qkv_out)
-
-    def heads(pair):
-        gather_all.tick(12 + pair)
-        forward_heads(pair, qkv, mask, mixed, inverse, attended)
-
-    each(8, heads)
-    store(mixed, mixed_out)
-    store(inverse, inverse_out)
-    store(weights.at[pl.ds(0, DOWN)], attention_out)
-    gather_all.tick(20)
-    for half in (0, 1):
-        columns = slice(half * WIDE, half * WIDE + WIDE)
-        middle[:, columns] = tokens[:, columns].astype(jnp.float32) + dot(
-            attended[...], matrix(weights, 6 + half)
-        )
-    transpose_into(attended, attended_t)
-    store(attended_t, attended_t_out)
-    gather_all.tick(21)
-
-    def second_norm(at):
-        value = middle[at, :]
-        unit, _ = moments(value)
-        normed_two[at, :] = (unit * rows[2:3, :] + rows[3:4, :]).astype(jnp.bfloat16)
-        result[at, :] = value + rows[4:5, :]
-        grad_normed[at, :] = jnp.zeros((64, WIDTH), jnp.float32)
-
-    by_rows(second_norm)
-    store(middle, middle_out)
-    transpose_into(normed_two, normed_two_t)
-
-    def leave(block):
-        slot = block % 2
-        owner = (block // (2 * inner), (block // 2) % inner, block % 2)
-        return (
-            pltpu.make_async_copy(to_up.at[slot], terms.at[8 + block], up_sem.at[slot]),
-            pltpu.make_async_copy(
-                to_down.at[slot], terms.at[(pl.ds(0, 8),) + owner], down_sem.at[slot]
-            ),
-        )
-
-    def feed(block):
-        gather_all.tick(22 + block)
-
-        @pl.when(block >= 2)
-        def _():
-            for item in leave(block - 2):
-                item.wait()
-
-        feed_block(
-            dims,
-            block,
-            (
-                normed_two,
-                normed_two_t,
-                grad_out,
-                weights,
-                up_bias,
-                result,
-                grad_normed,
-                to_up.at[block % 2],
-                to_down.at[block % 2],
-                grad_up_bias,
-            ),
-        )
-        for item in leave(block):
-            item.start()
-
-    each(8, feed)
-
-    store(result, result_out)
-    store(grad_normed, grad_normed_out)
-    for block in (6, 7):
-        for item in leave(block):
-            item.wait()
-    small.drain(vectors, (), order)
-    gather_all.finish()
-    for item in stores:
-        item.wait()
-
-
-def forward(dims, tokens, cotangent, crops, kept, small, shards):
-    outer, inner, depth = dims
-    most = max(dims) - 1
-    lead = (outer, inner, 2, depth)
-    tile = (UNIT, WIDE)
-    whole = (LENGTH, WIDTH)
-    f32, bf16 = jnp.float32, jnp.bfloat16
-    shape = jax.ShapeDtypeStruct
-    vmem, anywhere = pl.BlockSpec(memory_space=pltpu.VMEM), pl.BlockSpec(memory_space=pl.ANY)
-    return pl.pallas_call(
-        functools.partial(forward_kernel, dims),
-        out_shape=[
-            shape((8, WIDE), f32),
-            shape((8, WIDTH), f32),
-            shape((6, LENGTH, WIDE), bf16),
-            shape(whole, f32),
-            shape(whole, f32),
-            shape((WIDTH, LENGTH), bf16),
-            shape((WIDTH, LENGTH), bf16),
-            shape(whole, f32),
-            shape(whole, f32),
-            shape(whole, f32),
-            shape((DOWN,) + lead + tile, bf16),
-            shape((16,) + lead + tile, bf16),
-        ],
-        in_specs=[vmem] * 8 + [anywhere] * 8,
-        out_specs=[vmem] * 2 + [anywhere] * 10,
-        scratch_shapes=[
-            pltpu.VMEM(whole, bf16),
-            pltpu.VMEM(whole, bf16),
-            pltpu.VMEM((GATHERED,) + lead + tile, bf16),
-            pltpu.VMEM(lead + (8, 128), f32),
-            pltpu.VMEM((8, WIDE), f32),
-            pltpu.VMEM((LENGTH, LENGTH), bf16),
-            pltpu.VMEM((6, LENGTH, WIDE), bf16),
-            pltpu.VMEM(whole, f32),
-            pltpu.VMEM(whole, f32),
-            pltpu.VMEM(whole, bf16),
-            pltpu.VMEM((WIDTH, LENGTH), bf16),
-            pltpu.VMEM(whole, bf16),
-            pltpu.VMEM((WIDTH, LENGTH), bf16),
-            pltpu.VMEM(whole, f32),
-            pltpu.VMEM(whole, bf16),
-            pltpu.VMEM((WIDTH, LENGTH), bf16),
-            pltpu.VMEM(whole, f32),
-            pltpu.VMEM(whole, f32),
-            pltpu.VMEM((2,) + lead + tile, bf16),
-            pltpu.VMEM((2, 8, depth) + tile, bf16),
-            pltpu.SemaphoreType.DMA((GATHERED, 4, most)),
-            pltpu.SemaphoreType.DMA((GATHERED, 4, most)),
-            pltpu.SemaphoreType.DMA((4, most)),
-            pltpu.SemaphoreType.DMA((4, most)),
-            pltpu.SemaphoreType.DMA((GATHERED + 2,)),
-            pltpu.SemaphoreType.DMA((9,)),
-            pltpu.SemaphoreType.DMA((2,)),
-            pltpu.SemaphoreType.DMA((2,)),
-        ],
-        compiler_params=pltpu.CompilerParams(
-            collective_id=0, has_side_effects=True, vmem_limit_bytes=VMEM_LIMIT
-        ),
-        name="forward",
-    )(crops, kept, *small, tokens, cotangent, *shards)
+    value = dot(normed_t[...], grad_upper).astype(jnp.bfloat16)
+    staged[0] = value.reshape(staged.shape[1:])
+    for side in (0, 1):
+        columns = slice(side * WIDE, side * WIDE + WIDE)
+        value = dot_tn(hidden, grad_out[:, columns]).astype(jnp.bfloat16)
+        staged[1, side] = value.reshape(staged.shape[2:])
 
 
 class Sums(Mover):
@@ -1313,10 +1030,12 @@
     def came_in(self, order, stage, total, rooms, at):
         rest = [axis for axis in "abz" if axis in order[stage + 1 :]]
         inner = tuple(item for axis, item in zip("abz", at) if axis in rest)
-        value = total[at].astype(jnp.float32)
-        for step in self.place.partners(order[stage]):
+        steps = self.place.partners(order[stage])
+        wide = total.dtype if len(steps) == 1 and stage < 2 else jnp.float32
+        value = total[at].astype(wide)
+        for step in steps:
             room = self.room(order, stage, rooms, step)
-            value = value + (room[inner] if inner else room[...]).astype(jnp.float32)
+            value = value + (room[inner] if inner else room[...]).astype(wide)
         return value
 
     def after_stage(self, lead, order, stage, total, rooms):
@@ -1344,48 +1063,43 @@
 class Gradients(Sums):
     orders = ("abz", "baz", "azb", "abz", "baz", "bza")
 
-    def __init__(self, place, terms, total, rooms, results, ring, ring_sem, send_sem, recv_sem):
+    def __init__(self, place, terms, sums, rooms, results, ring, ring_sem, send_sem, recv_sem):
         super().__init__(place, send_sem, recv_sem)
-        self.terms, self.sums, self.rooms, self.results = terms, total, rooms, results
+        self.terms, self.sums, self.rooms, self.results = terms, sums, rooms, results
         self.ring, self.ring_sem = ring, ring_sem
         self.total = results.shape[0]
-        self.first = terms[0].shape[0]
+
+    def sum_at(self, index):
+        return self.sums.at[index // 2, :, :, index % 2]
 
     def by_order(self, index, work):
-        rooms = [room.at[index] for room in self.rooms]
-        total = self.sums.at[index]
+        rooms = [room.at[index % ROOMS] for room in self.rooms]
+        total = self.sum_at(index)
         by_order(self.place, self.orders, index, lambda order: work(order, total, rooms))
 
     def begin(self, index):
-        side = self.place.at["c"]
-        slot = index % (AHEAD + 1)
-
-        def go(source):
-            self.start((index,), 0, 1, "c", source.at[:, :, 1 - side], self.sums.at[index])
+        @when(index < self.total)
+        def _():
+            side = self.place.at["c"]
+            slot = index % (TERMS_AHEAD + 1)
+            source = self.terms.at[index]
+            self.start((index,), 0, 1, "c", source.at[:, :, 1 - side], self.sum_at(index))
             pltpu.make_async_copy(
                 source.at[:, :, side], self.ring.at[slot], self.ring_sem.at[slot]
             ).start()
 
-        @when(index < self.first)
-        def _():
-            go(self.terms[0].at[index])
-
-        @when((index >= self.first) & (index < self.total))
-        def _():
-            go(self.terms[1].at[index - self.first])
-
     def tick(self, now):
-        self.begin(now + AHEAD)
+        self.begin(now + TERMS_AHEAD)
 
         def live(index):
             return (index >= 0) & (index < self.total)
 
         @when(live(now))
         def _():
-            slot = now % (AHEAD + 1)
+            slot = now % (TERMS_AHEAD + 1)
             own = self.ring.at[slot]
             pltpu.make_async_copy(own, own, self.ring_sem.at[slot]).wait()
-            total = self.sums.at[now]
+            total = self.sum_at(now)
             self.copy((now,), 0, 1, "c", total, total).wait_recv()
             self.by_order(
                 now,
@@ -1474,28 +1188,35 @@
         qkv[4 + chunk, rows, lanes] = grad_value.astype(jnp.bfloat16)
 
 
-def backward_kernel(dims, *refs):
-    crops, kept, grad_up_bias, rows = refs[:4]
-    tokens_in, grad_out_in, qkv_in, mixed_in, inverse_in, attended_t_in, normed_t_in = refs[4:11]
-    middle_in, result_in, grad_normed_in, attention_in, terms = refs[11:16]
-    output, input_grad, owned, owned_small, attention_terms = refs[16:21]
+def layer_kernel(dims, *refs):
+    crops, kept, gain_one, bias_one, gain_two, bias_two, bias_down, bias_up = refs[:8]
+    tokens_in, grad_out_in = refs[8:10]
+    shards = refs[10:16]
+    output, input_grad, mixed_kept, inverse_kept, normed_t_kept, attention_kept, terms = refs[16:23]
+    owned, owned_up, owned_small = refs[23:26]
     (
-        tokens,
+        pixels,
+        grad_out,
         weights,
+        up_shard,
+        vectors,
+        rows,
+        up_bias,
         mask,
         mask_t,
-        grad_attended,
-        grad_mixed,
         qkv,
-        turned,
-        mixed,
-        inverse,
-        grad_middle,
+        normed,
+        turned_one,
+        turned_two,
+        middle,
+        wide_one,
+        wide_two,
+        wide_three,
+        staged,
+        grad_up_bias,
         sums,
-        staged,
         small,
         ring,
-        total,
         rooms_one,
         rooms_two,
         rooms_three,
@@ -1503,61 +1224,246 @@
         side_one,
         side_two,
         side_three,
+        send_sem,
+        recv_sem,
+        vector_send_sem,
+        vector_recv_sem,
         load_sem,
+        store_sem,
         stage_sem,
         ring_sem,
-        send_sem,
-        recv_sem,
+        terms_send_sem,
+        terms_recv_sem,
         side_send_sem,
         side_recv_sem,
-    ) = refs[21:]
+        sibling_sem,
+    ) = refs[26:]
     outer, inner, depth = dims
     devices = 2 * outer * inner * depth
     place = Place(dims)
-    spot = place.at
-    loads = {}
-
-    def load(name, source, target):
-        item = pltpu.make_async_copy(source, target, load_sem.at[len(loads)])
+    spot = (place.at["a"], place.at["b"], place.at["c"], place.at["z"])
+    copies = {}
+
+    def move(name, source, target):
+        item = pltpu.make_async_copy(source, target, load_sem.at[len(copies)])
         item.start()
-        loads[name] = item
-
-    load("grad_normed", grad_normed_in, inverse)
-    load("middle", middle_in, mixed)
-    load("grad_out", grad_out_in, grad_attended)
-    load("result", result_in, grad_mixed)
+        copies[name] = item
+
+    for index in range(FEED):
+        source = shards[index // 2].at[:, pl.ds((index % 2) * WIDE, WIDE)]
+        move(index, source, weights.at[(index,) + spot])
+    move("tokens", tokens_in, pixels)
+    move("up", shards[4], up_shard)
+    for group in range(4):
+        for half in (0, 1):
+            source = shards[5].at[pl.ds(group * UNIT, UNIT), pl.ds(half * WIDE, WIDE)]
+            index = FEED + 4 * group + half
+            move(index, source, weights.at[(index,) + spot])
+    move("grad_out", grad_out_in, grad_out)
+
+    vector_gather = Gather(place, vector_send_sem, vector_recv_sem)
+    vector_order = "zbac"
+    lines = [
+        jnp.concatenate([item[...] for item in (gain_one, bias_one, gain_two, bias_two)], axis=1),
+        bias_up[...],
+        jnp.concatenate([bias_down[...], jnp.zeros((1, 128 - UNIT), jnp.bfloat16)], axis=1),
+    ]
+    vectors[spot] = jnp.concatenate(
+        [line.astype(jnp.float32) for line in lines] + [jnp.zeros((5, 128), jnp.float32)], axis=0
+    )
+    place.greet()
+    vector_gather.send(vectors, (), vector_order, 0)
+    gather_all = Weights(place, weights, send_sem, recv_sem)
+    for index in range(AHEAD):
+        copies[index].wait()
+        gather_all.begin(index)
+    copies["up"].wait()
+    stacked = jnp.concatenate(
+        [up_shard[:, index * WIDE : (index + 1) * WIDE] for index in range(8)], axis=0
+    )
+    stacked = dot(stacked, hidden_order(False).astype(jnp.bfloat16)).astype(jnp.bfloat16)
+    for part in range(8):
+        for group in range(4):
+            at = (FEED + 4 * group + 2 + part // 4,) + spot
+            lanes = slice((part % 4) * 128, (part % 4) * 128 + 128)
+            weights[at + (slice(None), lanes)] = stacked[
+                part * UNIT : (part + 1) * UNIT, group * 128 : (group + 1) * 128
+            ]
+    for name, item in copies.items():
+        if name not in (0, 1, 2, 3, "up"):
+            item.wait()
+    for stage in range(4):
+        vector_gather.receive(vectors, (), vector_order, stage)
+        if stage < 3:
+            vector_gather.send(vectors, (), vector_order, stage + 1)
+            gather_all.tick(stage)
+    width_rows, up_rows = read_vectors(vectors, devices)
+    for index, row in enumerate(width_rows):
+        rows[index : index + 1, :] = row
+    for group, row in enumerate(up_rows):
+        for half in (0, 1):
+            up_bias[2 * group + half : 2 * group + half + 1, :] = row[
+                :, half * WIDE : half * WIDE + WIDE
+            ]
+    mask[...] = allowed(crops[...], kept[...])
+    mask_t[...] = allowed_back(crops[...], kept[...])
+    sums[...] = jnp.zeros(sums.shape, jnp.float32)
+
+    def first_norm(at):
+        value = pixels[at, :].astype(jnp.float32)
+        unit, _ = moments(value)
+        normed[at, :] = (unit * rows[0:1, :] + rows[1:2, :]).astype(jnp.bfloat16)
+        middle[at, :] = value
+
+    by_rows(first_norm)
+    stores = {}
+
+    def store(name, source, target):
+        item = pltpu.make_async_copy(source, target, store_sem.at[len(stores)])
+        item.start()
+        stores[name] = item
+
+    transpose_into(normed, turned_one)
+    store("normed", turned_one, normed_t_kept)
+    each(3, lambda index: gather_all.tick(3 + index))
+
+    def project(index):
+        gather_all.tick(6 + index)
+        value = dot(normed[...], matrix(weights, index))
+        mapped = jnp.where(value > 0, value + 1.0, jnp.exp(jnp.minimum(value, 0.0)))
+        qkv[index] = jnp.where(index < 4, mapped, value).astype(jnp.bfloat16)
+
+    each(6, project)
+    attended, mixed, inverse = pixels, wide_one, wide_two
+
+    def heads(pair):
+        @pl.when(pair % 2 == 0)
+        def _():
+            gather_all.tick(12 + pair // 2)
+
+        forward_heads(pair, qkv, mask, mixed, inverse, attended)
+
+    each(8, heads)
+    store("mixed", mixed, mixed_kept)
+    store("inverse", inverse, inverse_kept)
+    store("attention", weights.at[pl.ds(0, FEED)], attention_kept)
+    for half in (0, 1):
+        columns = slice(half * WIDE, half * WIDE + WIDE)
+        middle[:, columns] += dot(attended[...], matrix(weights, 6 + half))
+    stores["normed"].wait()
+    transpose_into(attended, turned_one)
+    result, grad_normed, normed_two = wide_one, wide_two, normed
+    stores["mixed"].wait()
+    stores["inverse"].wait()
+
+    def second_norm(at):
+        value = middle[at, :]
+        unit, _ = moments(value)
+        normed_two[at, :] = (unit * rows[2:3, :] + rows[3:4, :]).astype(jnp.bfloat16)
+        result[at, :] = value + rows[4:5, :]
+        grad_normed[at, :] = jnp.zeros((64, WIDTH), jnp.float32)
+
+    by_rows(second_norm)
+    transpose_into(normed_two, turned_two)
+
     adder = Gradients(
         place,
-        (terms, attention_terms),
-        total,
+        terms,
+        weights,
         (rooms_one, rooms_two, rooms_three),
         owned,
         ring,
         ring_sem,
-        send_sem,
-        recv_sem,
-    )
-    place.greet()
-    for index in range(AHEAD):
-        adder.begin(index)
-    load("out", attention_in.at[pl.ds(6, 2)], weights.at[pl.ds(6, 2)])
-    load("attended", attended_t_in, turned.at[0])
-    load("qkv", qkv_in, qkv)
-    load("normed", normed_t_in, turned.at[1])
-    load("rest", attention_in.at[pl.ds(0, 6)], weights.at[pl.ds(0, 6)])
-    load("tokens", tokens_in, tokens)
-    adder.tick(0)
-    mask[...] = allowed(crops[...], kept[...])
-    mask_t[...] = allowed_back(crops[...], kept[...])
-    sums[...] = jnp.zeros(sums.shape, jnp.float32)
-    for name in ("grad_normed", "middle", "grad_out", "result"):
-        loads[name].wait()
+        terms_send_sem,
+        terms_recv_sem,
+    )
+
+    def leave(block):
+        first, half = 4 * (block // 2), block % 2
+        return (
+            pltpu.make_async_copy(staged.at[0], terms.at[first + 2 + half], stage_sem.at[0]),
+            pltpu.make_async_copy(
+                staged.at[1], terms.at[pl.ds(first, 2), half], stage_sem.at[1]
+            ),
+        )
+
+    def last_tick(block):
+        return 16 + 4 * (block // 2) + block % 2
+
+    def feed(block):
+        begin = last_tick(block - 1) + 1
+
+        def both(step, carry):
+            @pl.when(step >= 16)
+            def _():
+                gather_all.tick(step)
+
+            @pl.when((step == begin) & (block > 0))
+            def _():
+                for item in leave(block - 1):
+                    item.wait()
+
+            @pl.when(step == TERMS_START)
+            def _():
+                pl.semaphore_wait(sibling_sem, 1)
+                for index in range(TERMS_AHEAD):
+                    adder.begin(index)
+
+            @pl.when(step >= TERMS_START)
+            def _():
+                adder.tick(step - TERMS_START)
+
+            return carry
+
+        lax.fori_loop(begin, last_tick(block) + 1, both, 0)
+        feed_block(
+            block,
+            (
+                normed_two,
+                turned_two,
+                grad_out,
+                weights,
+                up_bias,
+                result,
+                grad_normed,
+                staged,
+                grad_up_bias,
+            ),
+        )
+        for item in leave(block):
+            item.start()
+
+        @pl.when(block == 1)
+        def _():
+            gather_all.finish(0, ROOMS)
+            stores["attention"].wait()
+            pl.semaphore_signal(
+                sibling_sem, 1, device_id=place.device("c", 1), device_id_type=MESH
+            )
+
+    each(8, feed)
+    done = last_tick(7) + 1 - TERMS_START
+    adder.tick(done)
+    for item in leave(7):
+        item.wait()
+    gather_all.finish(ROOMS, CHUNKS - ROOMS)
+    loads = {}
+
+    def load(name, source, target):
+        item = pltpu.make_async_copy(source, target, store_sem.at[4 + len(loads)])
+        item.start()
+        loads[name] = item
+
+    load("out", attention_kept.at[pl.ds(6, 2)], weights.at[pl.ds(ROOMS + 6, 2)])
+    load("normed", normed_t_kept, turned_two)
+    load("rest", attention_kept.at[pl.ds(0, 6)], weights.at[pl.ds(ROOMS, 6)])
+    grad_attended, shown, grad_middle = pixels, normed, middle
 
     def close_branch(at):
-        unit, scale = moments(mixed[at, :])
-        grad = grad_attended[at, :].astype(jnp.float32)
-        value = inverse[at, :]
-        input_grad[at, :] = grad_mixed[at, :].astype(jnp.bfloat16)
+        unit, scale = moments(middle[at, :])
+        grad = grad_out[at, :].astype(jnp.float32)
+        value = grad_normed[at, :]
+        shown[at, :] = result[at, :].astype(jnp.bfloat16)
         sums[0:1, :] += jnp.sum(value * unit, axis=0, keepdims=True)
         sums[1:2, :] += jnp.sum(value, axis=0, keepdims=True)
         sums[2:3, :] += jnp.sum(grad, axis=0, keepdims=True)
@@ -1570,78 +1476,70 @@
         grad_middle[at, :] = summed
         grad_attended[at, :] = summed.astype(jnp.bfloat16)
 
-    adder.tick(1)
     by_rows(close_branch)
-    load("mixed", mixed_in, mixed)
-    load("inverse", inverse_in, inverse)
-    load("output", input_grad, output)
-    adder.tick(2)
+    load("mixed", mixed_kept, mixed)
+    load("inverse", inverse_kept, inverse)
+    load("output", shown, output)
+    adder.tick(done + 1)
     loads["out"].wait()
-    grad_mixed[...] = dot_nt(grad_attended[:, 0:WIDE], matrix(weights, 6)) + dot_nt(
-        grad_attended[:, WIDE:WIDTH], matrix(weights, 7)
-    )
-    adder.tick(3)
-    loads["attended"].wait()
+    grad_mixed = wide_three
+    grad_mixed[...] = dot_nt(grad_attended[:, 0:WIDE], matrix(weights, ROOMS + 6)) + dot_nt(
+        grad_attended[:, WIDE:WIDTH], matrix(weights, ROOMS + 7)
+    )
+    adder.tick(done + 2)
+
+    def stage_out(slot, index):
+        return pltpu.make_async_copy(staged.at[slot], terms.at[index], stage_sem.at[slot])
+
     for half in (0, 1):
         columns = slice(half * WIDE, half * WIDE + WIDE)
-        value = dot(turned[0], grad_attended[:, columns]).astype(jnp.bfloat16)
+        value = dot(turned_one[...], grad_attended[:, columns]).astype(jnp.bfloat16)
         staged[half] = value.reshape(staged.shape[1:])
-        pltpu.make_async_copy(
-            staged.at[half], attention_terms.at[half], stage_sem.at[half]
-        ).start()
-    for name in ("qkv", "mixed", "inverse"):
+        stage_out(half, 16 + half).start()
+    load("tokens", tokens_in, pixels)
+    adder.tick(done + 3)
+    for name in ("mixed", "inverse", "normed", "rest"):
         loads[name].wait()
-
+    for half in (0, 1):
+        stage_out(half, 16 + half).wait()
+    spread = 14 - (done + 4)
+
+    def back_heads(pair):
+        @pl.when((pair + 1) * spread // 8 > pair * spread // 8)
+        def _():
+            adder.tick(done + 4 + pair * spread // 8)
+
+        backward_heads(pair, qkv, mask, mask_t, mixed, inverse, grad_mixed)
+
+    each(8, back_heads)
+    grad_first = grad_mixed
+    grad_first[...] = jnp.zeros(grad_first.shape, jnp.float32)
+
+    def back_project(index):
+        value = dot(turned_two[...], qkv[index]).astype(jnp.bfloat16)
+        staged[index % 2] = value.reshape(staged.shape[1:])
+        stage_out(index % 2, 18 + index).start()
+        grad_first[...] += dot_nt(qkv[index], matrix(weights, ROOMS + index))
+
+        @pl.when(index > 0)
+        def _():
+            stage_out((index - 1) % 2, 17 + index).wait()
+
+        adder.tick(14 + index)
+
+    each(6, back_project)
+    stage_out(1, 23).wait()
+    adder.tick(20)
+    loads["tokens"].wait()
     loads["output"].wait()
 
-    def heads(pair):
-        adder.tick(4 + pair)
-        backward_heads(pair, qkv, mask, mask_t, mixed, inverse, grad_mixed)
-
-    each(8, heads)
-    loads["normed"].wait()
-    loads["rest"].wait()
-    grad_normed = grad_mixed
-    grad_normed[...] = jnp.zeros(grad_normed.shape, jnp.float32)
-
-    def stage_copy(index):
-        slot = index % 2
-        return pltpu.make_async_copy(
-            staged.at[slot], attention_terms.at[2 + index], stage_sem.at[slot]
-        )
-
-    for half in (0, 1):
-        pltpu.make_async_copy(
-            staged.at[half], attention_terms.at[half], stage_sem.at[half]
-        ).wait()
-
-    def project(index):
-        @pl.when(index >= 2)
-        def _():
-            stage_copy(index - 2).wait()
-
-        value = dot(turned[1], qkv[index]).astype(jnp.bfloat16)
-        staged[index % 2] = value.reshape(staged.shape[1:])
-        stage_copy(index).start()
-        grad_normed[...] += dot_nt(qkv[index], matrix(weights, index))
-
-        @pl.when(index < 4)
-        def _():
-            adder.tick(12 + index)
-
-    each(6, project)
-    for index in (4, 5):
-        stage_copy(index).wait()
-    adder.tick(16)
-    loads["tokens"].wait()
-
     def close(at):
-        unit, scale = moments(tokens[at, :].astype(jnp.float32))
-        value = grad_normed[at, :]
+        unit, scale = moments(pixels[at, :].astype(jnp.float32))
+        value = grad_first[at, :]
         sums[3:4, :] += jnp.sum(value * unit, axis=0, keepdims=True)
         sums[4:5, :] += jnp.sum(value, axis=0, keepdims=True)
         scaled = value * rows[0:1, :]
-        input_grad[at, :] = (
+        shown[at, :] = (
             grad_middle[at, :]
             + scale
             * (
@@ -1652,9 +1550,19 @@
         ).astype(jnp.bfloat16)
 
     by_rows(close)
-    order = [sums[index : index + 1, :] for index in (3, 4, 0, 1)]
-    first = write_vectors(order, devices)
-    third = write_vectors([sums[2:3, :]], devices)
+    load("input_grad", shown, input_grad)
+    adder.tick(21)
+    groups = [
+        jnp.concatenate(
+            [grad_up_bias[2 * group + half : 2 * group + half + 1, :] for half in (0, 1)], axis=1
+        )
+        for group in range(4)
+    ]
+    lines = [
+        write_vectors([sums[index : index + 1, :] for index in (3, 4, 0, 1)], devices),
+        write_vectors(groups, devices),
+        write_vectors([sums[2:3, :]], devices),
+    ]
     for device in range(devices):
         at = (
             device // (2 * inner * depth),
@@ -1662,22 +1570,21 @@
             (device // depth) % 2,
             device % depth,
         )
-        block, lane = device // 4, (device % 4) * 128
-        small[at + (slice(0, 1),)] = first[device : device + 1, :]
-        small[at + (slice(1, 2),)] = grad_up_bias[block : block + 1, lane : lane + 128]
-        small[at + (slice(2, 3),)] = third[device : device + 1, :]
+        for row, line in enumerate(lines):
+            small[at + (slice(row, row + 1),)] = line[device : device + 1, :]
         small[at + (slice(3, 8),)] = jnp.zeros((5, 128), jnp.float32)
     side = Sums(place, side_send_sem, side_recv_sem)
     rooms = (side_one, side_two, side_three)
-    side.start((), 0, 1, "c", small.at[:, :, 1 - spot["c"]], side_total)
+    core = place.at["c"]
+    side.start((), 0, 1, "c", small.at[:, :, 1 - core], side_total)
 
     def last_ticks(step):
-        adder.tick(17 + step)
+        adder.tick(22 + step)
 
         @pl.when(step == 0)
         def _():
             side.copy((), 0, 1, "c", side_total, side_total).wait_recv()
-            side.after_core((), "abz", small.at[:, :, spot["c"]], side_total, rooms)
+            side.after_core((), "abz", small.at[:, :, core], side_total, rooms)
 
         for stage in (1, 2):
 
@@ -1689,84 +1596,115 @@
         def _():
             owned_small[...] = side.after_last((), "abz", side_total, rooms)
 
-    each(GATHERED + 3 * LAG - 17, last_ticks)
+        @pl.when(step == 4)
+        def _():
+            back = hidden_order(True).astype(jnp.float32)
+            for part in range(8):
+                lanes = slice((part % 4) * 128, (part % 4) * 128 + 128)
+                value = jnp.concatenate(
+                    [owned[4 * group + 2 + part // 4, :, lanes] for group in range(4)], axis=1
+                )
+                owned_up[:, part * WIDE : (part + 1) * WIDE] = jnp.dot(
+                    value, back, preferred_element_type=jnp.float32, precision=HIGH
+                )
+
+    each(CHUNKS + 3 * LAG - 22, last_ticks)
+    vector_gather.drain(vectors, (), vector_order)
     side.drain((), "abz", side_total, rooms)
     adder.finish()
-
-
-def backward(dims, crops, kept, grad_up_bias, rows, arrays):
+    loads["input_grad"].wait()
+
+
+def layer(dims, tokens, cotangent, crops, kept, small, shards):
     outer, inner, depth = dims
     most = max(dims) - 1
     lead = (outer, inner, 2, depth)
-    tile = (UNIT, WIDE)
-    whole = (LENGTH, WIDTH)
+    chip = (outer, inner, depth)
+    tile, small_tile = (UNIT, WIDE), (8, 128)
+    whole, turned = (LENGTH, WIDTH), (WIDTH, LENGTH)
     f32, bf16 = jnp.float32, jnp.bfloat16
     shape = jax.ShapeDtypeStruct
+    room, dma = pltpu.VMEM, pltpu.SemaphoreType.DMA
     vmem, anywhere = pl.BlockSpec(memory_space=pltpu.VMEM), pl.BlockSpec(memory_space=pl.ANY)
-    chip = (outer, inner, depth)
-    small_tile = (8, 128)
     return pl.pallas_call(
-        functools.partial(backward_kernel, dims),
+        functools.partial(layer_kernel, dims),
         out_shape=[
             shape(whole, bf16),
             shape(whole, bf16),
-            shape((GATHERED,) + tile, f32),
+            shape(whole, f32),
+            shape(whole, f32),
+            shape(turned, bf16),
+            shape((FEED,) + lead + tile, bf16),
+            shape((CHUNKS,) + lead + tile, bf16),
+            shape((CHUNKS,) + tile, f32),
+            shape((UNIT, HIDDEN), f32),
             shape(small_tile, f32),
-            shape((8,) + lead + tile, bf16),
         ],
-        in_specs=[vmem] * 4 + [anywhere] * 12,
-        out_specs=[anywhere] + [vmem] * 3 + [anywhere],
+        in_specs=[vmem] * 8 + [anywhere] * 8,
+        out_specs=[anywhere] * 7 + [vmem] * 3,
         scratch_shapes=[
-            pltpu.VMEM(whole, bf16),
-            pltpu.VMEM((8,) + lead + tile, bf16),
-            pltpu.VMEM((LENGTH, LENGTH), bf16),
-            pltpu.VMEM((LENGTH, LENGTH), bf16),
-            pltpu.VMEM(whole, bf16),
-            pltpu.VMEM(whole, f32),
-            pltpu.VMEM((6, LENGTH, WIDE), bf16),
-            pltpu.VMEM((2, WIDTH, LENGTH), bf16),
-            pltpu.VMEM(whole, f32),
-            pltpu.VMEM(whole, f32),
-            pltpu.VMEM(whole, f32),
-            pltpu.VMEM((8, WIDTH), f32),
-            pltpu.VMEM((2,) + lead + tile, bf16),
-            pltpu.VMEM(lead + small_tile, f32),
-            pltpu.VMEM((AHEAD + 1,) + chip + tile, bf16),
-            pltpu.VMEM((GATHERED,) + chip + tile, bf16),
-            pltpu.VMEM((GATHERED, 2, 4) + tile, bf16),
-            pltpu.VMEM((GATHERED, 6) + tile, bf16),
-            pltpu.VMEM((GATHERED, 3) + tile, bf16),
-            pltpu.VMEM(chip + small_tile, f32),
-            pltpu.VMEM((2, 4) + small_tile, f32),
-            pltpu.VMEM((6,) + small_tile, f32),
-            pltpu.VMEM((3,) + small_tile, f32),
-            pltpu.SemaphoreType.DMA((13,)),
-            pltpu.SemaphoreType.DMA((2,)),
-            pltpu.SemaphoreType.DMA((AHEAD + 1,)),
-            pltpu.SemaphoreType.DMA((GATHERED, 4, most)),
-            pltpu.SemaphoreType.DMA((GATHERED, 4, most)),
-            pltpu.SemaphoreType.DMA((4, most)),
-            pltpu.SemaphoreType.DMA((4, most)),
+            room(whole, bf16),
+            room(whole, bf16),
+            room((CHUNKS,) + lead + tile, bf16),
+            room((UNIT, HIDDEN), bf16),
+            room(lead + small_tile, f32),
+            room((8, WIDTH), f32),
+            room((8, WIDE), f32),
+            room((LENGTH, LENGTH), bf16),
+            room((LENGTH, LENGTH), bf16),
+            room((6, LENGTH, WIDE), bf16),
+            room(whole, bf16),
+            room(turned, bf16),
+            room(turned, bf16),
+            room(whole, f32),
+            room(whole, f32),
+            room(whole, f32),
+            room(whole, f32),
+            room((2,) + lead + tile, bf16),
+            room((8, WIDE), f32),
+            room((8, WIDTH), f32),
+            room(lead + small_tile, f32),
+            room((TERMS_AHEAD + 1,) + chip + tile, bf16),
+            room((ROOMS, 2, 4) + tile, bf16),
+            room((ROOMS, 6) + tile, bf16),
+            room((ROOMS, 3) + tile, bf16),
+            room(chip + small_tile, f32),
+            room((2, 4) + small_tile, f32),
+            room((6,) + small_tile, f32),
+            room((3,) + small_tile, f32),
+            dma((CHUNKS, 4, most)),
+            dma((CHUNKS, 4, most)),
+            dma((4, most)),
+            dma((4, most)),
+            dma((19,)),
+            dma((12,)),
+            dma((2,)),
+            dma((TERMS_AHEAD + 1,)),
+            dma((CHUNKS, 4, most)),
+            dma((CHUNKS, 4, most)),
+            dma((4, most)),
+            dma((4, most)),
+            pltpu.SemaphoreType.REGULAR,
         ],
         compiler_params=pltpu.CompilerParams(
-            collective_id=1, has_side_effects=True, vmem_limit_bytes=VMEM_LIMIT
+            collective_id=0, has_side_effects=True, vmem_limit_bytes=VMEM_LIMIT
         ),
-        name="backward",
-    )(crops, kept, grad_up_bias, rows, *arrays)
+        name="layer",
+    )(crops, kept, *small, tokens, cotangent, *shards)
 
 
 def place_kernel(*refs):
-    result, input_grad, owned, small = refs[:4]
-    result_out, input_grad_out, query, key, value, out, up, down = refs[4:12]
-    vectors, bias_up = refs[12:17], refs[17]
-    sems = refs[18]
-    copies = [(result, result_out.at[0]), (input_grad, input_grad_out.at[0])]
-    for index in range(GATHERED):
-        if index < 8:
-            group, half = index // 2, index % 2
+    result, input_grad, owned, owned_up, small = refs[:5]
+    result_out, input_grad_out, query, key, value, out, up, down = refs[5:13]
+    vectors, bias_up = refs[13:18], refs[18]
+    sems = refs[19]
+    copies = [(result, result_out.at[0]), (input_grad, input_grad_out.at[0]), (owned_up, up)]
+    for index in range(CHUNKS):
+        if index < 16:
+            group, half = index // 4, index % 4
+            if half >= 2:
+                continue
             target = down.at[pl.ds(group * UNIT, UNIT), pl.ds(half * WIDE, WIDE)]
-        elif index < 16:
-            target = up.at[:, pl.ds((index - 8) * WIDE, WIDE)]
         else:
             matrix_out = (out, query, key, value)[(index - 16) // 2]
             target = matrix_out.at[:, pl.ds((index % 2) * WIDE, WIDE)]
@@ -1785,7 +1723,7 @@
         item.wait()
 
 
-def place_results(result, input_grad, owned, small):
+def place_results(result, input_grad, owned, owned_up, small):
     f32, bf16 = jnp.float32, jnp.bfloat16
     shape = jax.ShapeDtypeStruct
     vmem, anywhere = pl.BlockSpec(memory_space=pltpu.VMEM), pl.BlockSpec(memory_space=pl.ANY)
@@ -1796,11 +1734,11 @@
         + [shape((UNIT, HIDDEN), f32), shape((4 * UNIT, WIDTH), f32)]
         + [shape((UNIT,), f32)] * 5
         + [shape((4 * UNIT,), f32)],
-        in_specs=[anywhere] * 3 + [vmem],
+        in_specs=[anywhere] * 4 + [vmem],
         out_specs=[vmem] * 14,
-        scratch_shapes=[pltpu.SemaphoreType.DMA((GATHERED + 2,))],
+        scratch_shapes=[pltpu.SemaphoreType.DMA((19,))],
         name="results",
-    )(result, input_grad, owned, small)
+    )(result, input_grad, owned, owned_up, small)
 
 
 def body(
@@ -1854,9 +1792,8 @@
     ]
     pixels, grads = tokens.reshape(LENGTH, WIDTH), cotangent.reshape(LENGTH, WIDTH)
     shards = (w_query, w_key, w_value, w_out, w_up, w_down)
-    grad_up, rows, *arrays = forward(dims, pixels, grads, crop_ids, kv_mask, small, shards)
-    result, input_grad, owned, owned_small, _ = backward(
-        dims, crop_ids, kv_mask, grad_up, rows, (pixels, grads, *arrays)
+    result, input_grad, *_, owned, owned_up, owned_small = layer(
+        dims, pixels, grads, crop_ids, kv_mask, small, shards
     )
     (
         output,
@@ -1873,7 +1810,7 @@
         grad_bias_two,
         grad_bias_down,
         grad_bias_up,
-    ) = place_results(result, input_grad, owned, owned_small)
+    ) = place_results(result, input_grad, owned, owned_up, owned_small)
     return (
         output,
         grad_tokens,

time: 273 us -> 253 us (0.927)
  Pallas kernels: 272 us -> 252 us
    pallas_call x2 -> x1, Pallas kernels: 267 us -> 247 us  [layer(): pl.pallas_call(functools.partial(layer_kernel, dims), out_shape=[shape(wh...]
where the time goes in v4:
time: 253 us
  Pallas kernels  252 us (100%)
    pallas_call x1, Pallas kernels, layer(): pl.pallas_call(functools.partial(layer_kernel, dims), out_shape=[shape(wh...  247 us

profile of v4, /device:TPU:0, one launch (start us, length us, event | category | flops | bytes accessed | tf_op | source)
XLA Modules:
  0.0 252.5 jit_solution(12246603250544347141)
XLA Ops:
  0.7 247.0 %layer.1 = (bf16[512,1024]{1,0:T(8,128)(2,1)}, bf16[512,1024]{1,0:T(8,128)(2,1)}, f32[512,1024]{1,0:T(8,128)}, f32[512,1024]{1,0:T(8,128)}, bf16[1024,512]{1,0:T...) custom-call(s32[1,512]{1,0:T(1,128)} %refs_0_.1, ...), custom_call_target="tpu_custom_call" | custom-call | tf_op jit(solution)/shard_map/layer/pallas_call | solution.py:1629
  247.7 4.6 %results.1 = (bf16[1,512,1024]{2,1,0:T(8,128)(2,1)}, bf16[1,512,1024]{2,1,0:T(8,128)(2,1)}, f32[32,1024]{1,0:T(8,128)}, f32[32,1024]{1,0:T(8,128)}, f32[32,1024]...) custom-call(bf16[512,1024]{1,0:T(8,128)(2,1)} %get-tuple-element.33., ...), custom_call_target="tpu_custom_call" | custom-call | tf_op jit(solution)/shard_map/results/pallas_call | solution.py:1730

commit v5 on v4

--- a/solution.py
+++ b/solution.py
@@ -675,10 +675,14 @@
 CHUNKS = 24
 FEED = 8
 ROOMS = 12
-LAG = 2
+LAG = 3
+LATE = 3 * LAG
 AHEAD = 4
+PASS_AHEAD = 2
 TERMS_AHEAD = 3
-TERMS_START = 23
+TERMS_START = 26
+PASS_AFTER = 2
+TERMS_PASS_AFTER = 2
 VMEM_LIMIT = 63 << 20
 
 
@@ -746,29 +750,79 @@
         lead = tuple(slice(None) if axis in done else spot[axis] for axis in "abcz")
         return chunk.at[lead]
 
+    def unless_passed(self, axis, step, work):
+        z = self.place.at["z"]
+        if axis == "z" and step == 3:
+            pl.when(z != 0)(work)
+        elif axis == "z" and step == 1:
+            pl.when(z != 3)(work)
+        else:
+            work()
+
     def send(self, chunk, lead, order, stage):
         axis, done = order[stage], order[:stage]
         source = self.region(chunk, done, self.place.at)
         for step in self.place.partners(axis):
-            self.copy(lead, stage, step, axis, source, source).start()
+            self.unless_passed(
+                axis, step, self.copy(lead, stage, step, axis, source, source).start
+            )
+
+    def passing(self, chunk, lead, order):
+        stage = order.index("z")
+        spot = dict(self.place.at)
+        z = spot["z"]
+        spot["z"] = 3 * (2 - z)
+        source = self.region(chunk, order[:stage], spot)
+        came = self.copy(lead, stage, 2, "z", source, source)
+        onward = pltpu.make_async_remote_copy(
+            source,
+            source,
+            self.send_sem.at[lead + (stage, 3)],
+            self.recv_sem.at[lead + (stage, 2 * (z - 1))],
+            device_id={"fsdp": 3 * (z - 1)},
+            device_id_type=MESH,
+        )
+        return came, onward
+
+    def pass_on(self, chunk, lead, order):
+        z = self.place.at["z"]
+
+        @pl.when((z == 1) | (z == 2))
+        def _():
+            came, onward = self.passing(chunk, lead, order)
+            came.wait_recv()
+            onward.start()
 
     def receive(self, chunk, lead, order, stage):
         axis, done = order[stage], order[:stage]
+        z = self.place.at["z"]
         for step in self.place.partners(axis):
             spot = self.place.moved(axis, self.place.size[axis] - step)
             target = self.region(chunk, done, spot)
-            self.copy(lead, stage, step, axis, target, target).wait_recv()
+            item = self.copy(lead, stage, step, axis, target, target)
+            if axis == "z" and step == 2:
+                pl.when((z == 0) | (z == 3))(item.wait_recv)
+            else:
+                item.wait_recv()
 
     def drain(self, chunk, lead, order):
+        z = self.place.at["z"]
         for stage in range(4):
             axis, done = order[stage], order[:stage]
             source = self.region(chunk, done, self.place.at)
             for step in self.place.partners(axis):
-                self.copy(lead, stage, step, axis, source, source).wait_send()
+                self.unless_passed(
+                    axis, step, self.copy(lead, stage, step, axis, source, source).wait_send
+                )
+            if axis == "z":
+
+                @pl.when((z == 1) | (z == 2))
+                def _():
+                    self.passing(chunk, lead, order)[1].wait_send()
 
 
 class Weights(Gather):
-    orders = ("zbac", "zabc", "bzac", "zbac", "zabc", "azbc")
+    orders = ("bzac", "azbc", "zbac", "azbc", "bzac", "zabc")
 
     def __init__(self, place, buffer, send_sem, recv_sem):
         super().__init__(place, send_sem, recv_sem)
@@ -784,8 +838,19 @@
                 index, lambda order: self.send(self.buffer.at[index], (index,), order, 0)
             )
 
+    def pass_on_at(self, index, stage):
+        @when((index >= 0) & (index < self.total))
+        def _():
+            def work(order):
+                if order.index("z") == stage:
+                    self.pass_on(self.buffer.at[index], (index,), order)
+
+            self.by_order(index, work)
+
     def tick(self, now):
         self.begin(now + AHEAD)
+        self.pass_on_at(now + PASS_AHEAD, 0)
+        self.pass_on_at(now - PASS_AFTER, 1)
         for stage in range(4):
             index = now - stage * LAG
             live = (index >= 0) & (index < self.total)
@@ -1005,21 +1070,59 @@
 
     def send_stage(self, lead, order, stage, total, rooms, add):
         axis = order[stage]
+        z = self.place.at["z"]
         for step in self.place.partners(axis):
             where = self.place.moved(axis, step)[axis]
             for at, _ in self.blocks(order, stage, where):
                 add(at)
             source = total.at[self.region(order, stage, where)]
             room = self.room(order, stage, rooms, step)
-            self.start(lead, stage + 1, step, axis, source, room)
+            item = self.copy(lead, stage + 1, step, axis, source, room)
+            if axis != "z":
+                item.start()
+            elif step == 2:
+                pl.when((z == 0) | (z == 3))(item.start)
+            else:
+                far = 3 if step == 1 else 0
+                pl.when(z != far)(item.start)
+
+                @pl.when(z == far)
+                def _(step=step, source=source, far=far):
+                    pltpu.make_async_remote_copy(
+                        source,
+                        self.room(order, stage, rooms, 4),
+                        self.send_sem.at[lead + (stage + 1, step - 1)],
+                        self.recv_sem.at[lead + (stage + 1, 3)],
+                        device_id={"fsdp": 2 if far == 3 else 1},
+                        device_id_type=MESH,
+                    ).start()
+
         for at, _ in self.blocks(order, stage, self.place.at[axis]):
             add(at)
+
+    def pass_on(self, lead, order, total, rooms):
+        z = self.place.at["z"]
+        stage = order.index("z")
+
+        @pl.when((z == 1) | (z == 2))
+        def _():
+            came = self.room(order, stage, rooms, 4)
+            self.copy(lead, stage + 1, 4, "z", came, came).wait_recv()
+            where = 3 * (2 - z)
+            for at, inner in self.blocks(order, stage, where):
+                total[at] = total[at] + (came[inner] if inner else came[...])
+            source = total.at[self.region(order, stage, where)]
+            self.start(lead, stage + 1, 2, "z", source, self.room(order, stage, rooms, 2))
 
     def await_stage(self, lead, order, stage, rooms):
         axis = order[stage]
         for step in self.place.partners(axis):
             room = self.room(order, stage, rooms, step)
-            self.copy(lead, stage + 1, step, axis, room, room).wait_recv()
+            item = self.copy(lead, stage + 1, step, axis, room, room)
+            if axis == "z" and step != 2:
+                pl.when(self.place.at["z"] != (0 if step == 1 else 3))(item.wait_recv)
+            else:
+                item.wait_recv()
 
     def after_core(self, lead, order, own, total, rooms):
         def add(at):
@@ -1035,7 +1138,11 @@
         value = total[at].astype(wide)
         for step in steps:
             room = self.room(order, stage, rooms, step)
-            value = value + (room[inner] if inner else room[...]).astype(wide)
+            term = (room[inner] if inner else room[...]).astype(wide)
+            if order[stage] == "z" and step != 2:
+                near = self.place.at["z"] != (0 if step == 1 else 3)
+                term = jnp.where(near, term, jnp.zeros_like(term))
+            value = value + term
         return value
 
     def after_stage(self, lead, order, stage, total, rooms):
@@ -1061,7 +1168,7 @@
 
 
 class Gradients(Sums):
-    orders = ("abz", "baz", "azb", "abz", "baz", "bza")
+    orders = ("azb", "bza", "abz", "bza", "azb", "baz")
 
     def __init__(self, place, terms, sums, rooms, results, ring, ring_sem, send_sem, recv_sem):
         super().__init__(place, send_sem, recv_sem)
@@ -1117,6 +1224,17 @@
                         (index,), order, stage, total, rooms
                     ),
                 )
+
+        for stage in (1, 2):
+            index = now - stage * LAG - TERMS_PASS_AFTER
+
+            @when(live(index))
+            def _(index=index, stage=stage):
+                def work(order, total, rooms):
+                    if order.index("z") == stage:
+                        self.pass_on((index,), order, total, rooms)
+
+                self.by_order(index, work)
 
         index = now - 3 * LAG
 
@@ -1277,6 +1395,8 @@
     for index in range(AHEAD):
         copies[index].wait()
         gather_all.begin(index)
+    for index in range(PASS_AHEAD):
+        gather_all.pass_on_at(index, 0)
     copies["up"].wait()
     stacked = jnp.concatenate(
         [up_shard[:, index * WIDE : (index + 1) * WIDE] for index in range(8)], axis=0
@@ -1292,6 +1412,7 @@
     for name, item in copies.items():
         if name not in (0, 1, 2, 3, "up"):
             item.wait()
+    vector_gather.pass_on(vectors, (), vector_order)
     for stage in range(4):
         vector_gather.receive(vectors, (), vector_order, stage)
         if stage < 3:
@@ -1325,10 +1446,10 @@
 
     transpose_into(normed, turned_one)
     store("normed", turned_one, normed_t_kept)
-    each(3, lambda index: gather_all.tick(3 + index))
+    each(LATE - 3, lambda index: gather_all.tick(3 + index))
 
     def project(index):
-        gather_all.tick(6 + index)
+        gather_all.tick(LATE + index)
         value = dot(normed[...], matrix(weights, index))
         mapped = jnp.where(value > 0, value + 1.0, jnp.exp(jnp.minimum(value, 0.0)))
         qkv[index] = jnp.where(index < 4, mapped, value).astype(jnp.bfloat16)
@@ -1339,7 +1460,7 @@
     def heads(pair):
         @pl.when(pair % 2 == 0)
         def _():
-            gather_all.tick(12 + pair // 2)
+            gather_all.tick(LATE + 6 + pair // 2)
 
         forward_heads(pair, qkv, mask, mixed, inverse, attended)
 
@@ -1388,13 +1509,13 @@
         )
 
     def last_tick(block):
-        return 16 + 4 * (block // 2) + block % 2
+        return LATE + 10 + 4 * (block // 2) + block % 2
 
     def feed(block):
         begin = last_tick(block - 1) + 1
 
         def both(step, carry):
-            @pl.when(step >= 16)
+            @pl.when(step >= LATE + 10)
             def _():
                 gather_all.tick(step)
 
@@ -1594,9 +1715,13 @@
 
         @pl.when(step == 3)
         def _():
+            side.pass_on((), "abz", side_total, rooms)
+
+        @pl.when(step == 4)
+        def _():
             owned_small[...] = side.after_last((), "abz", side_total, rooms)
 
-        @pl.when(step == 4)
+        @pl.when(step == 5)
         def _():
             back = hidden_order(True).astype(jnp.float32)
             for part in range(8):
@@ -1617,7 +1742,7 @@
 
 def layer(dims, tokens, cotangent, crops, kept, small, shards):
     outer, inner, depth = dims
-    most = max(dims) - 1
+    most = max(dims)
     lead = (outer, inner, 2, depth)
     chip = (outer, inner, depth)
     tile, small_tile = (UNIT, WIDE), (8, 128)
@@ -1666,12 +1791,12 @@
             room(lead + small_tile, f32),
             room((TERMS_AHEAD + 1,) + chip + tile, bf16),
             room((ROOMS, 2, 4) + tile, bf16),
-            room((ROOMS, 6) + tile, bf16),
-            room((ROOMS, 3) + tile, bf16),
+            room((ROOMS, 8) + tile, bf16),
+            room((ROOMS, 4) + tile, bf16),
             room(chip + small_tile, f32),
             room((2, 4) + small_tile, f32),
-            room((6,) + small_tile, f32),
-            room((3,) + small_tile, f32),
+            room((8,) + small_tile, f32),
+            room((4,) + small_tile, f32),
             dma((CHUNKS, 4, most)),
             dma((CHUNKS, 4, most)),
             dma((4, most)),

time: 253 us -> 243 us (0.960)
  Pallas kernels: 252 us -> 242 us
    pallas_call x1, Pallas kernels: 247 us -> 238 us  [layer(): pl.pallas_call(functools.partial(layer_kernel, dims), out_shape=[shape(wh...]
where the time goes in v5:
time: 243 us
  Pallas kernels  242 us (100%)
    pallas_call x1, Pallas kernels, layer(): pl.pallas_call(functools.partial(layer_kernel, dims), out_shape=[shape(wh...  238 us

profile of v5, /device:TPU:0, one launch (start us, length us, event | category | flops | bytes accessed | tf_op | source)
XLA Modules:
  0.0 243.0 jit_solution(10885829204970444807)
XLA Ops:
  0.7 237.5 %layer.1 = (bf16[512,1024]{1,0:T(8,128)(2,1)}, bf16[512,1024]{1,0:T(8,128)(2,1)}, f32[512,1024]{1,0:T(8,128)}, f32[512,1024]{1,0:T(8,128)}, bf16[1024,512]{1,0:T...) custom-call(s32[1,512]{1,0:T(1,128)} %refs_0_.1, ...), custom_call_target="tpu_custom_call" | custom-call | tf_op jit(solution)/shard_map/layer/pallas_call | solution.py:1754
  238.2 4.6 %results.1 = (bf16[1,512,1024]{2,1,0:T(8,128)(2,1)}, bf16[1,512,1024]{2,1,0:T(8,128)(2,1)}, f32[32,1024]{1,0:T(8,128)}, f32[32,1024]{1,0:T(8,128)}, f32[32,1024]...) custom-call(bf16[512,1024]{1,0:T(8,128)(2,1)} %get-tuple-element.33., ...), custom_call_target="tpu_custom_call" | custom-call | tf_op jit(solution)/shard_map/results/pallas_call | solution.py:1855

commit v6 on v5

--- a/solution.py
+++ b/solution.py
@@ -675,12 +675,13 @@
 CHUNKS = 24
 FEED = 8
 ROOMS = 12
+DRAINED = 12
 LAG = 3
 LATE = 3 * LAG
 AHEAD = 4
 PASS_AHEAD = 2
 TERMS_AHEAD = 3
-TERMS_START = 26
+TERMS_START = 27
 PASS_AFTER = 2
 TERMS_PASS_AFTER = 2
 VMEM_LIMIT = 63 << 20
@@ -849,6 +850,12 @@
 
     def tick(self, now):
         self.begin(now + AHEAD)
+        past = now - DRAINED
+
+        @when((past >= 0) & (past < self.total))
+        def _():
+            self.finish_one(past)
+
         self.pass_on_at(now + PASS_AHEAD, 0)
         self.pass_on_at(now - PASS_AFTER, 1)
         for stage in range(4):
@@ -865,14 +872,11 @@
 
                 self.by_order(index, work)
 
-    def finish(self, first, count):
-        def work(step):
-            index = first + step
-            self.by_order(
-                index, lambda order: self.drain(self.buffer.at[index], (index,), order)
-            )
-
-        each(count, work)
+    def finish_one(self, index):
+        self.by_order(index, lambda order: self.drain(self.buffer.at[index], (index,), order))
+
+    def finish(self, first, end):
+        each(end - first, lambda step: self.finish_one(first + step))
 
 
 def moments(values):
@@ -1201,6 +1205,10 @@
         def live(index):
             return (index >= 0) & (index < self.total)
 
+        @when(live(now - DRAINED))
+        def _():
+            self.finish_one(now - DRAINED)
+
         @when(live(now))
         def _():
             slot = now % (TERMS_AHEAD + 1)
@@ -1245,14 +1253,13 @@
 
             self.by_order(index, work)
 
-    def finish(self):
-        def work(index):
-            self.by_order(
-                index,
-                lambda order, total, rooms: self.drain((index,), order, total, rooms),
-            )
-
-        each(self.total, work)
+    def finish_one(self, index):
+        self.by_order(
+            index, lambda order, total, rooms: self.drain((index,), order, total, rooms)
+        )
+
+    def finish(self, first):
+        each(self.total - first, lambda step: self.finish_one(first + step))
 
 
 def backward_heads(pair, qkv, mask, mask_t, mixed, inverse, grad_mixed):
@@ -1311,8 +1318,10 @@
     tokens_in, grad_out_in = refs[8:10]
     shards = refs[10:16]
     output, input_grad, mixed_kept, inverse_kept, normed_t_kept, attention_kept, terms = refs[16:23]
-    owned, owned_up, owned_small = refs[23:26]
+    owned_out, owned_up_out, owned_small = refs[23:26]
     (
+        owned,
+        owned_up,
         pixels,
         grad_out,
         weights,
@@ -1397,6 +1406,13 @@
         gather_all.begin(index)
     for index in range(PASS_AHEAD):
         gather_all.pass_on_at(index, 0)
+    for name, item in copies.items():
+        if name not in range(AHEAD) and name not in ("up", "tokens", "grad_out"):
+            item.wait()
+    vector_gather.pass_on(vectors, (), vector_order)
+    vector_gather.receive(vectors, (), vector_order, 0)
+    vector_gather.send(vectors, (), vector_order, 1)
+    gather_all.tick(0)
     copies["up"].wait()
     stacked = jnp.concatenate(
         [up_shard[:, index * WIDE : (index + 1) * WIDE] for index in range(8)], axis=0
@@ -1409,15 +1425,17 @@
             weights[at + (slice(None), lanes)] = stacked[
                 part * UNIT : (part + 1) * UNIT, group * 128 : (group + 1) * 128
             ]
-    for name, item in copies.items():
-        if name not in (0, 1, 2, 3, "up"):
-            item.wait()
-    vector_gather.pass_on(vectors, (), vector_order)
-    for stage in range(4):
-        vector_gather.receive(vectors, (), vector_order, stage)
-        if stage < 3:
-            vector_gather.send(vectors, (), vector_order, stage + 1)
-            gather_all.tick(stage)
+    vector_gather.receive(vectors, (), vector_order, 1)
+    vector_gather.send(vectors, (), vector_order, 2)
+    gather_all.tick(1)
+    mask[...] = allowed(crops[...], kept[...])
+    vector_gather.receive(vectors, (), vector_order, 2)
+    vector_gather.send(vectors, (), vector_order, 3)
+    gather_all.tick(2)
+    copies["tokens"].wait()
+    copies["grad_out"].wait()
+    sums[...] = jnp.zeros(sums.shape, jnp.float32)
+    vector_gather.receive(vectors, (), vector_order, 3)
     width_rows, up_rows = read_vectors(vectors, devices)
     for index, row in enumerate(width_rows):
         rows[index : index + 1, :] = row
@@ -1426,9 +1444,7 @@
             up_bias[2 * group + half : 2 * group + half + 1, :] = row[
                 :, half * WIDE : half * WIDE + WIDE
             ]
-    mask[...] = allowed(crops[...], kept[...])
-    mask_t[...] = allowed_back(crops[...], kept[...])
-    sums[...] = jnp.zeros(sums.shape, jnp.float32)
+    gather_all.tick(3)
 
     def first_norm(at):
         value = pixels[at, :].astype(jnp.float32)
@@ -1437,6 +1453,7 @@
         middle[at, :] = value
 
     by_rows(first_norm)
+    gather_all.tick(4)
     stores = {}
 
     def store(name, source, target):
@@ -1446,7 +1463,7 @@
 
     transpose_into(normed, turned_one)
     store("normed", turned_one, normed_t_kept)
-    each(LATE - 3, lambda index: gather_all.tick(3 + index))
+    each(LATE - 5, lambda index: gather_all.tick(5 + index))
 
     def project(index):
         gather_all.tick(LATE + index)
@@ -1468,6 +1485,7 @@
     store("mixed", mixed, mixed_kept)
     store("inverse", inverse, inverse_kept)
     store("attention", weights.at[pl.ds(0, FEED)], attention_kept)
+    mask_t[...] = allowed_back(crops[...], kept[...])
     for half in (0, 1):
         columns = slice(half * WIDE, half * WIDE + WIDE)
         middle[:, columns] += dot(attended[...], matrix(weights, 6 + half))
@@ -1554,9 +1572,8 @@
         for item in leave(block):
             item.start()
 
-        @pl.when(block == 1)
+        @pl.when(block == 2)
         def _():
-            gather_all.finish(0, ROOMS)
             stores["attention"].wait()
             pl.semaphore_signal(
                 sibling_sem, 1, device_id=place.device("c", 1), device_id_type=MESH
@@ -1567,7 +1584,7 @@
     adder.tick(done)
     for item in leave(7):
         item.wait()
-    gather_all.finish(ROOMS, CHUNKS - ROOMS)
+    gather_all.finish(LATE + 24 - DRAINED, CHUNKS)
     loads = {}
 
     def load(name, source, target):
@@ -1733,11 +1750,16 @@
                     value, back, preferred_element_type=jnp.float32, precision=HIGH
                 )
 
-    each(CHUNKS + 3 * LAG - 22, last_ticks)
+    each(CHUNKS + LATE - 23, last_ticks)
+    load("up", owned_up, owned_up_out)
+    load("feed", owned.at[pl.ds(0, 16)], owned_out.at[pl.ds(0, 16)])
+    adder.tick(CHUNKS + LATE - 1)
+    load("attention", owned.at[pl.ds(16, 8)], owned_out.at[pl.ds(16, 8)])
     vector_gather.drain(vectors, (), vector_order)
     side.drain((), "abz", side_total, rooms)
-    adder.finish()
-    loads["input_grad"].wait()
+    adder.finish(CHUNKS + LATE - DRAINED)
+    for name in ("input_grad", "up", "feed", "attention"):
+        loads[name].wait()
 
 
 def layer(dims, tokens, cotangent, crops, kept, small, shards):
@@ -1766,8 +1788,10 @@
             shape(small_tile, f32),
         ],
         in_specs=[vmem] * 8 + [anywhere] * 8,
-        out_specs=[anywhere] * 7 + [vmem] * 3,
+        out_specs=[anywhere] * 9 + [vmem],
         scratch_shapes=[
+            room((CHUNKS,) + tile, f32),
+            room((UNIT, HIDDEN), f32),
             room(whole, bf16),
             room(whole, bf16),
             room((CHUNKS,) + lead + tile, bf16),
@@ -1802,7 +1826,7 @@
             dma((4, most)),
             dma((4, most)),
             dma((19,)),
-            dma((12,)),
+            dma((15,)),
             dma((2,)),
             dma((TERMS_AHEAD + 1,)),
             dma((CHUNKS, 4, most)),
@@ -1820,31 +1844,48 @@
 
 def place_kernel(*refs):
     result, input_grad, owned, owned_up, small = refs[:5]
-    result_out, input_grad_out, query, key, value, out, up, down = refs[5:13]
-    vectors, bias_up = refs[13:18], refs[18]
-    sems = refs[19]
-    copies = [(result, result_out.at[0]), (input_grad, input_grad_out.at[0]), (owned_up, up)]
-    for index in range(CHUNKS):
-        if index < 16:
-            group, half = index // 4, index % 4
-            if half >= 2:
-                continue
-            target = down.at[pl.ds(group * UNIT, UNIT), pl.ds(half * WIDE, WIDE)]
-        else:
-            matrix_out = (out, query, key, value)[(index - 16) // 2]
-            target = matrix_out.at[:, pl.ds((index % 2) * WIDE, WIDE)]
-        copies.append((owned.at[index], target))
-    items = [
-        pltpu.make_async_copy(source, target, sems.at[index])
-        for index, (source, target) in enumerate(copies)
-    ]
-    for item in items:
-        item.start()
+    outs, vectors, bias_up = refs[5:13], refs[13:18], refs[18]
+    buffers, in_sem, out_sem = refs[19:27], refs[27], refs[28]
+    _, _, query, key, value, out, _, down = buffers
+    parts = [[(result, buffers[0].at[0])], [(input_grad, buffers[1].at[0])]]
+    for number in (1, 2, 3, 0):
+        target = (out, query, key, value)[number]
+        parts.append(
+            [
+                (owned.at[16 + 2 * number + half], target.at[:, pl.ds(half * WIDE, WIDE)])
+                for half in (0, 1)
+            ]
+        )
+    parts.append([(owned_up, buffers[6])])
+    parts.append(
+        [
+            (
+                owned.at[4 * group + half],
+                down.at[pl.ds(group * UNIT, UNIT), pl.ds(half * WIDE, WIDE)],
+            )
+            for group in range(4)
+            for half in (0, 1)
+        ]
+    )
+    loads, count = [], 0
+    for items in parts:
+        group = []
+        for source, target in items:
+            group.append(pltpu.make_async_copy(source, target, in_sem.at[count]))
+            group[-1].start()
+            count += 1
+        loads.append(group)
     for index in range(4):
         vectors[index][...] = small[0, index * UNIT : (index + 1) * UNIT]
     vectors[4][...] = small[2, 0:UNIT]
     bias_up[...] = small[1, :]
-    for item in items:
+    stores = []
+    for index, group in enumerate(loads):
+        for item in group:
+            item.wait()
+        stores.append(pltpu.make_async_copy(buffers[index], outs[index], out_sem.at[index]))
+        stores[-1].start()
+    for item in stores:
         item.wait()
 
 
@@ -1852,16 +1893,18 @@
     f32, bf16 = jnp.float32, jnp.bfloat16
     shape = jax.ShapeDtypeStruct
     vmem, anywhere = pl.BlockSpec(memory_space=pltpu.VMEM), pl.BlockSpec(memory_space=pl.ANY)
+    large = (
+        [shape((1, LENGTH, WIDTH), bf16)] * 2
+        + [shape((UNIT, WIDTH), f32)] * 4
+        + [shape((UNIT, HIDDEN), f32), shape((4 * UNIT, WIDTH), f32)]
+    )
     return pl.pallas_call(
         place_kernel,
-        out_shape=[shape((1, LENGTH, WIDTH), bf16)] * 2
-        + [shape((UNIT, WIDTH), f32)] * 4
-        + [shape((UNIT, HIDDEN), f32), shape((4 * UNIT, WIDTH), f32)]
-        + [shape((UNIT,), f32)] * 5
-        + [shape((4 * UNIT,), f32)],
+        out_shape=large + [shape((UNIT,), f32)] * 5 + [shape((4 * UNIT,), f32)],
         in_specs=[anywhere] * 4 + [vmem],
-        out_specs=[vmem] * 14,
-        scratch_shapes=[pltpu.SemaphoreType.DMA((19,))],
+        out_specs=[anywhere] * 8 + [vmem] * 6,
+        scratch_shapes=[pltpu.VMEM(item.shape, item.dtype) for item in large]
+        + [pltpu.SemaphoreType.DMA((19,)), pltpu.SemaphoreType.DMA((8,))],
         name="results",
     )(result, input_grad, owned, owned_up, small)
 

time: 243 us -> 239 us (0.984)
  Pallas kernels: 242 us -> 238 us
    pallas_call x1, Pallas kernels: 238 us -> 233 us  [layer(): pl.pallas_call(functools.partial(layer_kernel, dims), out_shape=[shape(wh...]
where the time goes in v6:
time: 239 us
  Pallas kernels  238 us (100%)
    pallas_call x1, Pallas kernels, layer(): pl.pallas_call(functools.partial(layer_kernel, dims), out_shape=[shape(wh...  233 us

profile of v6, /device:TPU:0, one launch (start us, length us, event | category | flops | bytes accessed | tf_op | source)
XLA Modules:
  0.0 238.7 jit_solution(5533059473296935873)
XLA Ops:
  0.7 233.4 %layer.1 = (bf16[512,1024]{1,0:T(8,128)(2,1)}, bf16[512,1024]{1,0:T(8,128)(2,1)}, f32[512,1024]{1,0:T(8,128)}, f32[512,1024]{1,0:T(8,128)}, bf16[1024,512]{1,0:T...) custom-call(s32[1,512]{1,0:T(1,128)} %refs_0_.1, ...), custom_call_target="tpu_custom_call" | custom-call | tf_op jit(solution)/shard_map/layer/pallas_call | solution.py:1776
  234.0 4.5 %results.1 = (bf16[1,512,1024]{2,1,0:T(8,128)(2,1)}, bf16[1,512,1024]{2,1,0:T(8,128)(2,1)}, f32[32,1024]{1,0:T(8,128)}, f32[32,1024]{1,0:T(8,128)}, f32[32,1024]...) custom-call(bf16[512,1024]{1,0:T(8,128)(2,1)} %get-tuple-element.33., ...), custom_call_target="tpu_custom_call" | custom-call | tf_op jit(solution)/shard_map/results/pallas_call | solution.py:1901

commit v7 on v6

--- a/solution.py
+++ b/solution.py
@@ -823,7 +823,7 @@
 
 
 class Weights(Gather):
-    orders = ("bzac", "azbc", "zbac", "azbc", "bzac", "zabc")
+    orders = ("zbac", "azbc", "bzac", "zabc", "bzac", "azbc")
 
     def __init__(self, place, buffer, send_sem, recv_sem):
         super().__init__(place, send_sem, recv_sem)
@@ -1172,7 +1172,7 @@
 
 
 class Gradients(Sums):
-    orders = ("azb", "bza", "abz", "bza", "azb", "baz")
+    orders = ("baz", "azb", "bza", "abz", "bza", "azb")
 
     def __init__(self, place, terms, sums, rooms, results, ring, ring_sem, send_sem, recv_sem):
         super().__init__(place, send_sem, recv_sem)

time: 239 us -> 234 us (0.979)
  Pallas kernels: 238 us -> 232 us
    pallas_call x1, Pallas kernels: 233 us -> 228 us  [layer(): pl.pallas_call(functools.partial(layer_kernel, dims), out_shape=[shape(wh...]
where the time goes in v7:
time: 234 us; the launch traced here: 233 us
  Pallas kernels  232 us (99%)
    pallas_call x1, Pallas kernels, layer(): pl.pallas_call(functools.partial(layer_kernel, dims), out_shape=[shape(wh...  228 us

profile of v7, /device:TPU:0, one launch (start us, length us, event | category | flops | bytes accessed | tf_op | source)
XLA Modules:
  0.0 233.3 jit_solution(3263761632028953269)
XLA Ops:
  0.7 228.0 %layer.1 = (bf16[512,1024]{1,0:T(8,128)(2,1)}, bf16[512,1024]{1,0:T(8,128)(2,1)}, f32[512,1024]{1,0:T(8,128)}, f32[512,1024]{1,0:T(8,128)}, bf16[1024,512]{1,0:T...) custom-call(s32[1,512]{1,0:T(1,128)} %refs_0_.1, ...), custom_call_target="tpu_custom_call" | custom-call | tf_op jit(solution)/shard_map/layer/pallas_call | solution.py:1776
  228.6 4.5 %results.1 = (bf16[1,512,1024]{2,1,0:T(8,128)(2,1)}, bf16[1,512,1024]{2,1,0:T(8,128)(2,1)}, f32[32,1024]{1,0:T(8,128)}, f32[32,1024]{1,0:T(8,128)}, f32[32,1024]...) custom-call(bf16[512,1024]{1,0:T(8,128)(2,1)} %get-tuple-element.33., ...), custom_call_target="tpu_custom_call" | custom-call | tf_op jit(solution)/shard_map/results/pallas_call | solution.py:1901
